TPU v7x, 128 devices: a whole 4x4x4 slice. The times are simulated.
128 devices in a mesh: col: 16 (over z_lo, y, core), row: 8 (over z_hi, x).
Axes of the slice: x: 4, y: 4, z: 4 (z_hi: 2, z_lo: 2; z = z_hi * 2 + z_lo), core: 2. Of those that a mesh axis runs over, the one named last changes fastest.
Arguments:
- trace_start: float32 [32, 131072], P(None, ('col', 'row')), may hold values from -6 to 6
- surface_load: float32 [32, 131072], P(None, ('col', 'row')), may hold values from -6 to 6
- panel_tiles: bfloat16 [5504, 512, 512], P(('col', 'row')), may hold values from -0.015625 to 0.015625
- tile_list: int32 [5504], P(('col', 'row')), may hold values from -1 to 65535, as said below
- surf_map: int32 [32], replicated, may hold values from 0 to 31, as said below
- coef_index: int32 [4, 4, 32768], P(None, None, 'row'), may hold values from 0 to 15
- coef_table: float32 [16], replicated, may hold values from 0.2 to 2
- vol_source: float32 [4, 4, 32768], P(None, None, 'row'), may hold values from -6 to 6
Outputs:
- traces: float32 [32, 131072], P(None, ('col', 'row'))
- response: float32 [32, 131072], P(None, ('col', 'row'))
Inputs may be any that keep to these rules, and one draw needn't show every extreme that they name: `tile_list`: each device has 43 slots, ordered by col index, then row index, then slot. A value i * 256 + j names the tile of rows i * 512 to (i + 1) * 512 - 1 and columns j * 512 to (j + 1) * 512 - 1 of the boundary matrix, with j <= i and j < 16; each such tile is named exactly once. A device of col index c and row index r names only tiles whose rows lie in shards of row index r (i * 512 // 1024 leaves remainder r modulo 8), and none if c >= 12; its named tiles fill its first slots and the rest hold -1. Some device names 43 tiles. surf_map[r * 4 + q] leaves remainder r modulo 8; each volume tile lies under exactly one surface tile.
All inputs are finite; a program needn't handle non-finite values.
Results may differ from a plain program's by a relative error of at most 0.0041.
Values may be sent and summed in bfloat16 or wider, within the bound.
No kernel may reach another device: no remote copies, remote signals or barrier semaphores. Data moves between devices by JAX's collectives and lax.ppermute only.
A program may use at most 128 MiB of HBM per device.

v0:
```python
import jax
import jax.numpy as jnp
from jax import lax
from jax.sharding import PartitionSpec as P

ITERS = 2
SWEEPS = 4


COUPLING_STEP = 0.3
JACOBI_WEIGHT = 0.8
CELL_MASS = 0.05


def padded(x, sides, width):
    for axis, dim in sides:
        peers, length = (lax.axis_size(axis), x.shape[dim])
        up = [(i, (i + 1) % peers) for i in range(peers - 1)]
        down = [(j, i) for i, j in up]
        last = lax.slice_in_dim(x, length - width, length, axis=dim)
        first = lax.slice_in_dim(x, 0, width, axis=dim)
        before = lax.ppermute(last, axis, up)
        after = lax.ppermute(first, axis, down)
        x = jnp.concatenate([before, x, after], axis=dim)
    return x


def from_everyone(x, axis):
    peers = lax.axis_size(axis)
    return lax.all_to_all(jnp.broadcast_to(x[None], (peers, *x.shape)), axis, 0, 0, tiled=True)


def in_order(parts, dim):
    lengths = list(parts.shape[1:])
    lengths[dim] *= parts.shape[0]
    return jnp.moveaxis(parts, 0, dim).reshape(lengths)


def gather_directly(x, axis, dim):
    parts = from_everyone(x, axis)
    return in_order(parts, dim)


def in_blocks(x, dim, peers):
    before, after = (x.shape[:dim], x.shape[dim + 1 :])
    return jnp.moveaxis(x.reshape(*before, peers, -1, *after), dim, 0)


def summed_on_arrival(x, axis, dim):
    peers = lax.axis_size(axis)
    parts = lax.all_to_all(in_blocks(x, dim, peers), axis, 0, 0, tiled=True)
    return jnp.sum(parts, axis=0)


def lookup_coefs(indices, coef_values):
    levels = jnp.arange(coef_values.shape[0], dtype=jnp.int32)
    return jnp.sum(jnp.where(indices[..., None] == levels, coef_values, 0.0), axis=-1)


def relax_line(padded_values, coefs_pad, source, top_trace):
    centre_coef = coefs_pad[:, 1:-1]
    left_weight = 0.5 * (centre_coef + coefs_pad[:, :-2])
    right_weight = 0.5 * (centre_coef + coefs_pad[:, 2:])
    layer_weight = 0.5 * (centre_coef[:-1] + centre_coef[1:])
    upper_weight = jnp.concatenate([centre_coef[:1], layer_weight], 0)
    lower_weight = jnp.concatenate([layer_weight, jnp.zeros_like(centre_coef[:1])], 0)
    centre = padded_values[:, :, 1:-1]
    upper_values = jnp.concatenate([top_trace[:, None, :], centre[:, :-1]], 1)
    lower_values = jnp.concatenate([centre[:, 1:], jnp.zeros_like(centre[:, :1])], 1)
    gathered = (
        left_weight * padded_values[:, :, :-2]
        + right_weight * padded_values[:, :, 2:]
        + upper_weight * upper_values
        + lower_weight * lower_values
        + source
    )
    diagonal = left_weight + right_weight + upper_weight + lower_weight + CELL_MASS
    return (1.0 - JACOBI_WEIGHT) * centre + JACOBI_WEIGHT * gathered / diagonal


def add_block(partial_value, block_sum, block_start):
    current = lax.dynamic_slice_in_dim(partial_value, block_start, block_sum.shape[1], 1)
    return lax.dynamic_update_slice_in_dim(partial_value, current + block_sum, block_start, 1)


def apply_slots(panel_part, ident_part, band_traces, window_traces, row_count):
    rhs_count = band_traces.shape[0]
    tile_width = panel_part.shape[1]
    shard_width = window_traces.shape[1] // row_count
    per_shard = shard_width // tile_width
    tiles_side = band_traces.shape[1] * row_count // tile_width
    band_tiles = band_traces.shape[1] // tile_width
    window_tiles = window_traces.shape[1] // tile_width
    is_valid = ident_part >= 0
    safe_ident = jnp.where(is_valid, ident_part, 0)
    row_tile = safe_ident // tiles_side
    col_tile = safe_ident % tiles_side
    shard_number = row_tile // per_shard
    band_tile = shard_number // row_count * per_shard + row_tile % per_shard
    band_blocks = band_traces.reshape(rhs_count, band_tiles, tile_width)
    window_blocks = window_traces.reshape(rhs_count, window_tiles, tile_width)
    row_parts = jnp.take(band_blocks, band_tile, axis=1)
    col_parts = jnp.take(window_blocks, col_tile, axis=1)
    into_rows = jnp.einsum(
        "rsk,sjk->srj", col_parts, panel_part, preferred_element_type=jnp.float32
    )
    into_cols = jnp.einsum(
        "rsk,skj->srj", row_parts, panel_part, preferred_element_type=jnp.float32
    )
    valid_weight = is_valid.astype(jnp.float32)[:, None]
    band_onehot = (band_tile[:, None] == jnp.arange(band_tiles, dtype=jnp.int32)[None, :]).astype(
        jnp.float32
    ) * valid_weight
    window_onehot = (
        col_tile[:, None] == jnp.arange(window_tiles, dtype=jnp.int32)[None, :]
    ).astype(jnp.float32) * valid_weight
    band_add = jnp.einsum("srj,sb->rbj", into_rows, band_onehot, precision=lax.Precision.HIGHEST)
    window_add = jnp.einsum(
        "srj,sb->rbj", into_cols, window_onehot, precision=lax.Precision.HIGHEST
    )
    return (band_add.reshape(rhs_count, -1), window_add.reshape(rhs_count, -1))


def sweep_volume(volume_state, coefs_pad, line_source, top_trace):
    for sweep_index in range(SWEEPS):
        padded_state = padded(volume_state, (("row", 2),), 1)
        volume_state = relax_line(padded_state, coefs_pad, line_source, top_trace)
    return volume_state


def local(
    trace_start, surface_load, panel_tiles, tile_list, surf_map, coef_index, coef_table, vol_source
):
    column_count = lax.axis_size("col")
    row_count = lax.axis_size("row")
    volume_count = column_count // 4
    dense_count = column_count - volume_count
    col_index = lax.axis_index("col")
    row_index = lax.axis_index("row")
    volume_line = jnp.maximum(col_index - dense_count, 0)
    is_volume = col_index >= dense_count
    line_coefs = lookup_coefs(
        lax.dynamic_index_in_dim(coef_index, volume_line, 0, keepdims=False), coef_table
    )
    line_source = lax.dynamic_index_in_dim(vol_source, volume_line, 0, keepdims=False)
    coefs_pad = padded(line_coefs, (("row", 1),), 1)
    volume_tile = volume_line * row_count + row_index
    tile_numbers = jnp.arange(surf_map.shape[0], dtype=jnp.int32)
    surface_tile = jnp.sum(jnp.where(surf_map == volume_tile, tile_numbers, 0))
    node_count = line_coefs.shape[1]
    flux_start = surface_tile % volume_count * node_count
    rhs_count = trace_start.shape[0]
    shard_width = trace_start.shape[1]
    band_width = shard_width * column_count
    window_width = shard_width * row_count
    volume_state = jnp.zeros((rhs_count, line_coefs.shape[0], node_count), jnp.float32)
    work_lists = (panel_tiles, tile_list)
    traces = trace_start
    response = trace_start
    for iteration in range(ITERS):
        band_traces = gather_directly(traces.astype(jnp.bfloat16), "col", 1)
        window_traces = gather_directly(band_traces[:, :shard_width], "row", 1)
        partials = (
            jnp.zeros((rhs_count, band_width), jnp.float32),
            jnp.zeros((rhs_count, window_width), jnp.float32),
        )
        panel_part, ident_part = work_lists
        partials = apply_slots(panel_part, ident_part, band_traces, window_traces, row_count)
        band_partial, window_partial = partials
        top_trace = lax.dynamic_slice_in_dim(band_traces, flux_start, node_count, 1).astype(
            jnp.float32
        )
        volume_state = sweep_volume(volume_state, coefs_pad, line_source, top_trace)
        top_flux = jnp.where(is_volume, line_coefs[0] * (top_trace - volume_state[:, 0]), 0.0)
        band_partial = add_block(band_partial, top_flux, flux_start)
        window_share = summed_on_arrival(window_partial, "row", 1)
        band_partial = add_block(band_partial, window_share, 0)
        response = summed_on_arrival(band_partial, "col", 1)
        traces = traces + COUPLING_STEP * (surface_load - traces - response)
    return (traces, response)


def solution(mesh):
    return jax.shard_map(
        local,
        mesh=mesh,
        in_specs=(
            P(None, ("col", "row")),
            P(None, ("col", "row")),
            P(("col", "row"), None, None),
            P(("col", "row")),
            P(),
            P(None, None, "row"),
            P(),
            P(None, None, "row"),
        ),
        out_specs=(P(None, ("col", "row")), P(None, ("col", "row"))),
        check_vma=False,
    )
```

profile of v0, /device:TPU:1, one launch (start us, length us, event | category | flops | bytes accessed | tf_op | source)
XLA Modules:
  0.0 389.9 jit_solution(57831444358480930)
XLA Ops:
  2.1 4.6 %collective-permute-start.1 = (f32[32,4,1]{2,0,1:T(8,128)S(1)}, f32[32,4,1]{2,0,1:T(8,128)S(1)}, u32[]{:S(2)}, u32[]{:S(2)}) collective-permute-start(f32[32,4,1]{2,0,1:T(8,128)S(1)} %broadcast.107), channel_id=1, source_target_pairs={{0,1},{1,2},{2,3},{3,4},{4,5},{5,6},{6,7},{8,9},{9,10},{10,11},{11... | collective-permute-start | bytes 1544 | tf_op jit(solution)/shard_map/ppermute | solution.py:22
  14.5 7.4 %all-to-all-start = ((bf16[16,32,1024]{2,1,0:T(8,128)(2,1)}), bf16[16,32,1024]{2,1,0:T(8,128)(2,1)S(1)}, u32[]{:S(2)}, u32[]{:S(2)}) async-start(bf16[16,32,1024]{2,1,0:T(8,128)(2,1)} %broadcast_in_dim.49), calls=%async_computation | async-start | bytes 2097152 | tf_op jit(solution)/shard_map/all_to_all | solution.py:30
  25.7 12.0 %all-to-all-done = bf16[16,32,1024]{2,1,0:T(8,128)(2,1)S(1)} async-done(((bf16[16,32,1024]{2,1,0:T(8,128)(2,1)}), bf16[16,32,1024]{2,1,0:T(8,128)(2,1)S(1)}, u32[]{:S(2)}, u32[]{:S(2)}) %all-to-all-start) | async-done | bytes 1048608 | tf_op jit(solution)/shard_map/all_to_all | solution.py:30
  49.6 10.1 %all-to-all-start.1 = ((bf16[8,32,1024]{2,1,0:T(8,128)(2,1)}), bf16[8,32,1024]{2,1,0:T(8,128)(2,1)}, u32[]{:S(2)}, u32[]{:S(2)}) async-start(bf16[8,32,1024]{2,1,0:T(8,128)(2,1)} %broadcast_in_dim.50), calls=%async_computation.1 | async-start | bytes 1048576 | tf_op jit(solution)/shard_map/all_to_all | solution.py:30
  67.4 9.9 %fusion.84 = f32[43,32,512]{2,1,0:T(8,128)S(1)} fusion(bf16[43,512,512]{2,1,0:T(8,128)(2,1)} %param.14, bf16[43,32,512]{2,1,0:T(8,128)(2,1)} %gather_fusion.1, pred[43]{0:T(512)(128)(4,1)S(1)} %get-tuple-element.4), kind=kOutput, calls=%fused_computation.111 | convolution fusion | flops 722124800 | bytes 26771500 | tf_op jit(solution)/shard_map/rsk,skj->srj/dot_general | solution.py:107
  77.3 4.1 %fusion.96 = f32[32,16,512]{2,1,0:T(8,128)} fusion(f32[43,32,512]{2,1,0:T(8,128)S(1)} %fusion.84, f32[43]{0:T(128)S(1)} %get-tuple-element.44, s32[43]{0:T(128)S(1)} %get-tuple-element.12), kind=kOutput, calls=%fused_computation.123 | convolution fusion | flops 135267680 | bytes 3866968 | tf_op jit(solution)/shard_map/srj,sb->rbj/dot_general | solution.py:118
  90.2 4.0 %collective-permute-start.6 = (f32[32,4,1]{2,0,1:T(8,128)S(1)}, f32[32,4,1]{2,0,1:T(8,128)S(1)}, u32[]{:S(2)}, u32[]{:S(2)}) collective-permute-start(f32[32,4,1]{2,0,1:T(8,128)S(1)} %get-tuple-element.35), channel_id=1, source_target_pairs={{0,1},{1,2},{2,3},{3,4},{4,5},{5,6},{6,7},{8,9},{9,10},{10,11},{11... | collective-permute-start | bytes 1544 | tf_op jit(solution)/shard_map/ppermute | solution.py:22
  94.2 11.2 %collective-permute-start.7 = (f32[32,4,1]{2,0,1:T(8,128)S(1)}, f32[32,4,1]{2,0,1:T(8,128)S(1)}, u32[]{:S(2)}, u32[]{:S(2)}) collective-permute-start(f32[32,4,1]{2,0,1:T(8,128)S(1)} %get-tuple-element.36), channel_id=1, source_target_pairs={{1,0},{2,1},{3,2},{4,3},{5,4},{6,5},{7,6},{9,8},{10,9},{11,10},{12... | collective-permute-start | bytes 1544 | tf_op jit(solution)/shard_map/ppermute | solution.py:23
  119.4 15.6 %all-to-all-start.2 = ((f32[8,32,1024]{2,1,0:T(8,128)}), f32[8,32,1024]{2,1,0:T(8,128)}, u32[]{:S(2)}, u32[]{:S(2)}) async-start(f32[8,32,1024]{2,1,0:T(8,128)} %bitcast.82), calls=%async_computation.2 | async-start | bytes 2097152 | tf_op jit(solution)/shard_map/all_to_all | solution.py:51
  140.5 12.7 %fusion.86 = f32[43,32,512]{2,1,0:T(8,128)} fusion(bf16[43,512,512]{2,1,0:T(8,128)(2,1)} %param.14, bf16[43,32,512]{2,1,0:T(8,128)(2,1)} %gather_fusion, pred[43]{0:T(512)(128)(4,1)S(1)} %get-tuple-element.11), kind=kOutput, calls=%fused_computation.113 | convolution fusion | flops 722124800 | bytes 26771500 | tf_op jit(solution)/shard_map/rsk,sjk->srj/dot_general | solution.py:104
  153.2 5.4 %fusion.6 = f32[32,32,512]{2,0,1:T(8,128)S(1)} fusion(f32[43,32,512]{2,1,0:T(8,128)} %fusion.86, f32[43]{0:T(128)S(1)} %get-tuple-element.44, s32[43]{0:T(128)S(1)} %get-tuple-element.5), kind=kOutput, calls=%fused_computation.17 | convolution fusion | flops 270535360 | bytes 4915544 | tf_op jit(solution)/shard_map/srj,sb->rbj/dot_general | solution.py:117
  171.4 8.3 %all-to-all-start.3 = ((f32[16,32,1024]{2,1,0:T(8,128)}), f32[16,32,1024]{2,1,0:T(8,128)}, u32[]{:S(2)}, u32[]{:S(2)}) async-start(f32[16,32,1024]{2,1,0:T(8,128)} %copy.60), calls=%async_computation.3 | async-start | bytes 4194304 | tf_op jit(solution)/shard_map/all_to_all | solution.py:51
  181.6 4.3 %collective-permute-start.10 = (f32[32,4,1]{2,0,1:T(8,128)}, f32[32,4,1]{2,0,1:T(8,128)}, u32[]{:S(2)}, u32[]{:S(2)}) collective-permute-start(f32[32,4,1]{2,0,1:T(8,128)} %get-tuple-element.27), channel_id=1, source_target_pairs={{0,1},{1,2},{2,3},{3,4},{4,5},{5,6},{6,7},{8,9},{9,10},{10,11},{11... | collective-permute-start | bytes 1544 | tf_op jit(solution)/shard_map/ppermute | solution.py:22
  187.2 20.0 %all-to-all-done.3 = f32[16,32,1024]{2,1,0:T(8,128)} async-done(((f32[16,32,1024]{2,1,0:T(8,128)}), f32[16,32,1024]{2,1,0:T(8,128)}, u32[]{:S(2)}, u32[]{:S(2)}) %all-to-all-start.3) | async-done | bytes 2097184 | tf_op jit(solution)/shard_map/all_to_all | solution.py:51
  210.1 5.9 %all-to-all-start.4 = ((bf16[16,32,1024]{2,1,0:T(8,128)(2,1)}), bf16[16,32,1024]{2,1,0:T(8,128)(2,1)}, u32[]{:S(2)}, u32[]{:S(2)}) async-start(bf16[16,32,1024]{2,1,0:T(8,128)(2,1)} %broadcast_in_dim.56), calls=%async_computation.4 | async-start | bytes 2097152 | tf_op jit(solution)/shard_map/all_to_all | solution.py:30
  218.1 13.7 %all-to-all-done.4 = bf16[16,32,1024]{2,1,0:T(8,128)(2,1)} async-done(((bf16[16,32,1024]{2,1,0:T(8,128)(2,1)}), bf16[16,32,1024]{2,1,0:T(8,128)(2,1)}, u32[]{:S(2)}, u32[]{:S(2)}) %all-to-all-start.4) | async-done | bytes 1048608 | tf_op jit(solution)/shard_map/all_to_all | solution.py:30
  247.6 6.9 %all-to-all-start.5 = ((bf16[8,32,1024]{2,1,0:T(8,128)(2,1)}), bf16[8,32,1024]{2,1,0:T(8,128)(2,1)}, u32[]{:S(2)}, u32[]{:S(2)}) async-start(bf16[8,32,1024]{2,1,0:T(8,128)(2,1)} %broadcast_in_dim.57), calls=%async_computation.5 | async-start | bytes 1048576 | tf_op jit(solution)/shard_map/all_to_all | solution.py:30
  254.6 9.5 %fusion.80 = f32[43,32,512]{2,1,0:T(8,128)S(1)} fusion(bf16[43,512,512]{2,1,0:T(8,128)(2,1)} %param.14, bf16[43,32,512]{2,1,0:T(8,128)(2,1)S(1)} %gather_fusion.3, pred[43]{0:T(512)(128)(4,1)S(1)} %copy-done.23), kind=kOutput, calls=%fused_computation.107 | convolution fusion | flops 722124800 | bytes 26771500 | tf_op jit(solution)/shard_map/rsk,skj->srj/dot_general | solution.py:107
  268.8 4.1 %fusion.99 = f32[32,16,512]{2,1,0:T(8,128)} fusion(f32[43,32,512]{2,1,0:T(8,128)S(1)} %fusion.80, f32[43]{0:T(128)S(1)} %copy-done.27, s32[43]{0:T(128)S(1)} %copy-done.34), kind=kOutput, calls=%fused_computation.124 | convolution fusion | flops 135267680 | bytes 3866968 | tf_op jit(solution)/shard_map/srj,sb->rbj/dot_general | solution.py:118
  301.4 5.6 %collective-permute-done.17 = f32[32,4,1]{2,0,1:T(8,128)S(1)} collective-permute-done((f32[32,4,1]{2,0,1:T(8,128)S(1)}, f32[32,4,1]{2,0,1:T(8,128)S(1)}, u32[]{:S(2)}, u32[]{:S(2)}) %collective-permute-start.17) | collective-permute-done | bytes 544 | tf_op jit(solution)/shard_map/ppermute | solution.py:23
  309.5 10.6 %all-to-all-start.6 = ((f32[8,32,1024]{2,1,0:T(8,128)}), f32[8,32,1024]{2,1,0:T(8,128)}, u32[]{:S(2)}, u32[]{:S(2)}) async-start(f32[8,32,1024]{2,1,0:T(8,128)} %bitcast.81), calls=%async_computation.6 | async-start | bytes 2097152 | tf_op jit(solution)/shard_map/all_to_all | solution.py:51
  323.8 12.7 %fusion.82 = f32[43,32,512]{2,1,0:T(8,128)} fusion(bf16[43,512,512]{2,1,0:T(8,128)(2,1)} %param.14, bf16[43,32,512]{2,1,0:T(8,128)(2,1)} %gather_fusion.2, pred[43]{0:T(512)(128)(4,1)S(1)} %copy-done.25), kind=kOutput, calls=%fused_computation.109 | convolution fusion | flops 722124800 | bytes 26771500 | tf_op jit(solution)/shard_map/rsk,sjk->srj/dot_general | solution.py:104
  336.5 5.4 %fusion.2 = f32[32,32,512]{2,0,1:T(8,128)S(1)} fusion(f32[43,32,512]{2,1,0:T(8,128)} %fusion.82, f32[43]{0:T(128)S(1)} %copy-done.28, s32[43]{0:T(128)S(1)} %copy-done.30), kind=kOutput, calls=%fused_computation.13 | convolution fusion | flops 270535360 | bytes 4915544 | tf_op jit(solution)/shard_map/srj,sb->rbj/dot_general | solution.py:117
  353.9 34.1 %all_to_all.40 = f32[16,32,1024]{2,1,0:T(8,128)S(1)} all-to-all(f32[16,32,1024]{2,1,0:T(8,128)S(1)} %copy.69), channel_id=1, replica_groups=mesh['col'=16,'row'=8] {'col'}, dimensions={0} | all-to-all | bytes 4194304 | tf_op jit(solution)/shard_map/all_to_all | solution.py:51
  (199 shorter events, 148.3 us)
Async XLA Ops:
  0.7 38.0 %collective-permute-start.3 = (f32[32,4,1]{2,0,1:T(8,128)S(1)}, f32[32,4,1]{2,0,1:T(8,128)S(1)}, u32[]{:S(2)}, u32[]{:S(2)}) collective-permute-start(f32[32,4,1]{2,0,1:T(8,128)S(1)} %broadcast.107), channel_id=1, source_target_pairs={{1,0},{2,1},{3,2},{4,3},{5,4},{6,5},{7,6},{9,8},{10,9},{11,10},{12... | collective-permute-start | bytes 1544 | tf_op jit(solution)/shard_map/ppermute | solution.py:23
  2.1 36.6 %collective-permute-start.1 = (f32[32,4,1]{2,0,1:T(8,128)S(1)}, f32[32,4,1]{2,0,1:T(8,128)S(1)}, u32[]{:S(2)}, u32[]{:S(2)}) collective-permute-start(f32[32,4,1]{2,0,1:T(8,128)S(1)} %broadcast.107), channel_id=1, source_target_pairs={{0,1},{1,2},{2,3},{3,4},{4,5},{5,6},{6,7},{8,9},{9,10},{10,11},{11... | collective-permute-start | bytes 1544 | tf_op jit(solution)/shard_map/ppermute | solution.py:22
  7.8 17.8 %collective-permute-start = (f32[4,1]{1,0:T(4,128)S(1)}, f32[4,1]{1,0:T(4,128)S(1)}, u32[]{:S(2)}, u32[]{:S(2)}) collective-permute-start(f32[4,1]{1,0:T(4,128)S(1)} %get-tuple-element.42), channel_id=1, source_target_pairs={{0,1},{1,2},{2,3},{3,4},{4,5},{5,6},{6,7},{8,9},{9,10},{10,11},{11... | collective-permute-start | bytes 56 | tf_op jit(solution)/shard_map/ppermute | solution.py:22
  11.1 14.4 %collective-permute-start.2 = (f32[4,1]{1,0:T(4,128)S(1)}, f32[4,1]{1,0:T(4,128)S(1)}, u32[]{:S(2)}, u32[]{:S(2)}) collective-permute-start(f32[4,1]{1,0:T(4,128)S(1)} %get-tuple-element.43), channel_id=1, source_target_pairs={{1,0},{2,1},{3,2},{4,3},{5,4},{6,5},{7,6},{9,8},{10,9},{11,10},{12... | collective-permute-start | bytes 56 | tf_op jit(solution)/shard_map/ppermute | solution.py:23
  14.5 23.2 %all-to-all-start = ((bf16[16,32,1024]{2,1,0:T(8,128)(2,1)}), bf16[16,32,1024]{2,1,0:T(8,128)(2,1)S(1)}, u32[]{:S(2)}, u32[]{:S(2)}) async-start(bf16[16,32,1024]{2,1,0:T(8,128)(2,1)} %broadcast_in_dim.49), calls=%async_computation | async-start | bytes 2097152 | tf_op jit(solution)/shard_map/all_to_all | solution.py:30
  49.6 69.8 %all-to-all-start.1 = ((bf16[8,32,1024]{2,1,0:T(8,128)(2,1)}), bf16[8,32,1024]{2,1,0:T(8,128)(2,1)}, u32[]{:S(2)}, u32[]{:S(2)}) async-start(bf16[8,32,1024]{2,1,0:T(8,128)(2,1)} %broadcast_in_dim.50), calls=%async_computation.1 | async-start | bytes 1048576 | tf_op jit(solution)/shard_map/all_to_all | solution.py:30
  59.7 27.2 %collective-permute-start.4 = (f32[32,4,1]{2,0,1:T(8,128)S(1)}, f32[32,4,1]{2,0,1:T(8,128)S(1)}, u32[]{:S(2)}, u32[]{:S(2)}) collective-permute-start(f32[32,4,1]{2,0,1:T(8,128)S(1)} %get-tuple-element.39), channel_id=1, source_target_pairs={{0,1},{1,2},{2,3},{3,4},{4,5},{5,6},{6,7},{8,9},{9,10},{10,11},{11... | collective-permute-start | bytes 1544 | tf_op jit(solution)/shard_map/ppermute | solution.py:22
  63.0 23.8 %collective-permute-start.5 = (f32[32,4,1]{2,0,1:T(8,128)S(1)}, f32[32,4,1]{2,0,1:T(8,128)S(1)}, u32[]{:S(2)}, u32[]{:S(2)}) collective-permute-start(f32[32,4,1]{2,0,1:T(8,128)S(1)} %get-tuple-element.40), channel_id=1, source_target_pairs={{1,0},{2,1},{3,2},{4,3},{5,4},{6,5},{7,6},{9,8},{10,9},{11,10},{12... | collective-permute-start | bytes 1544 | tf_op jit(solution)/shard_map/ppermute | solution.py:23
  90.2 15.6 %collective-permute-start.6 = (f32[32,4,1]{2,0,1:T(8,128)S(1)}, f32[32,4,1]{2,0,1:T(8,128)S(1)}, u32[]{:S(2)}, u32[]{:S(2)}) collective-permute-start(f32[32,4,1]{2,0,1:T(8,128)S(1)} %get-tuple-element.35), channel_id=1, source_target_pairs={{0,1},{1,2},{2,3},{3,4},{4,5},{5,6},{6,7},{8,9},{9,10},{10,11},{11... | collective-permute-start | bytes 1544 | tf_op jit(solution)/shard_map/ppermute | solution.py:22
  94.2 11.6 %collective-permute-start.7 = (f32[32,4,1]{2,0,1:T(8,128)S(1)}, f32[32,4,1]{2,0,1:T(8,128)S(1)}, u32[]{:S(2)}, u32[]{:S(2)}) collective-permute-start(f32[32,4,1]{2,0,1:T(8,128)S(1)} %get-tuple-element.36), channel_id=1, source_target_pairs={{1,0},{2,1},{3,2},{4,3},{5,4},{6,5},{7,6},{9,8},{10,9},{11,10},{12... | collective-permute-start | bytes 1544 | tf_op jit(solution)/shard_map/ppermute | solution.py:23
  107.9 5.6 %collective-permute-start.8 = (f32[32,4,1]{2,0,1:T(8,128)S(1)}, f32[32,4,1]{2,0,1:T(8,128)S(1)}, u32[]{:S(2)}, u32[]{:S(2)}) collective-permute-start(f32[32,4,1]{2,0,1:T(8,128)S(1)} %get-tuple-element.31), channel_id=1, source_target_pairs={{0,1},{1,2},{2,3},{3,4},{4,5},{5,6},{6,7},{8,9},{9,10},{10,11},{11... | collective-permute-start | bytes 1544 | tf_op jit(solution)/shard_map/ppermute | solution.py:22
  111.9 5.4 %collective-permute-start.9 = (f32[32,4,1]{2,0,1:T(8,128)S(1)}, f32[32,4,1]{2,0,1:T(8,128)S(1)}, u32[]{:S(2)}, u32[]{:S(2)}) collective-permute-start(f32[32,4,1]{2,0,1:T(8,128)S(1)} %get-tuple-element.32), channel_id=1, source_target_pairs={{1,0},{2,1},{3,2},{4,3},{5,4},{6,5},{7,6},{9,8},{10,9},{11,10},{12... | collective-permute-start | bytes 1544 | tf_op jit(solution)/shard_map/ppermute | solution.py:23
  119.4 43.7 %all-to-all-start.2 = ((f32[8,32,1024]{2,1,0:T(8,128)}), f32[8,32,1024]{2,1,0:T(8,128)}, u32[]{:S(2)}, u32[]{:S(2)}) async-start(f32[8,32,1024]{2,1,0:T(8,128)} %bitcast.82), calls=%async_computation.2 | async-start | bytes 2097152 | tf_op jit(solution)/shard_map/all_to_all | solution.py:51
  171.4 35.8 %all-to-all-start.3 = ((f32[16,32,1024]{2,1,0:T(8,128)}), f32[16,32,1024]{2,1,0:T(8,128)}, u32[]{:S(2)}, u32[]{:S(2)}) async-start(f32[16,32,1024]{2,1,0:T(8,128)} %copy.60), calls=%async_computation.3 | async-start | bytes 4194304 | tf_op jit(solution)/shard_map/all_to_all | solution.py:51
  181.6 52.4 %collective-permute-start.10 = (f32[32,4,1]{2,0,1:T(8,128)}, f32[32,4,1]{2,0,1:T(8,128)}, u32[]{:S(2)}, u32[]{:S(2)}) collective-permute-start(f32[32,4,1]{2,0,1:T(8,128)} %get-tuple-element.27), channel_id=1, source_target_pairs={{0,1},{1,2},{2,3},{3,4},{4,5},{5,6},{6,7},{8,9},{9,10},{10,11},{11... | collective-permute-start | bytes 1544 | tf_op jit(solution)/shard_map/ppermute | solution.py:22
  185.9 48.2 %collective-permute-start.11 = (f32[32,4,1]{2,0,1:T(8,128)}, f32[32,4,1]{2,0,1:T(8,128)}, u32[]{:S(2)}, u32[]{:S(2)}) collective-permute-start(f32[32,4,1]{2,0,1:T(8,128)} %get-tuple-element.28), channel_id=1, source_target_pairs={{1,0},{2,1},{3,2},{4,3},{5,4},{6,5},{7,6},{9,8},{10,9},{11,10},{12... | collective-permute-start | bytes 1544 | tf_op jit(solution)/shard_map/ppermute | solution.py:23
  210.1 21.7 %all-to-all-start.4 = ((bf16[16,32,1024]{2,1,0:T(8,128)(2,1)}), bf16[16,32,1024]{2,1,0:T(8,128)(2,1)}, u32[]{:S(2)}, u32[]{:S(2)}) async-start(bf16[16,32,1024]{2,1,0:T(8,128)(2,1)} %broadcast_in_dim.56), calls=%async_computation.4 | async-start | bytes 2097152 | tf_op jit(solution)/shard_map/all_to_all | solution.py:30
  247.6 61.8 %all-to-all-start.5 = ((bf16[8,32,1024]{2,1,0:T(8,128)(2,1)}), bf16[8,32,1024]{2,1,0:T(8,128)(2,1)}, u32[]{:S(2)}, u32[]{:S(2)}) async-start(bf16[8,32,1024]{2,1,0:T(8,128)(2,1)} %broadcast_in_dim.57), calls=%async_computation.5 | async-start | bytes 1048576 | tf_op jit(solution)/shard_map/all_to_all | solution.py:30
  264.1 14.5 %collective-permute-start.12 = (f32[32,4,1]{2,0,1:T(8,128)S(1)}, f32[32,4,1]{2,0,1:T(8,128)S(1)}, u32[]{:S(2)}, u32[]{:S(2)}) collective-permute-start(f32[32,4,1]{2,0,1:T(8,128)S(1)} %copy-done.21), channel_id=1, source_target_pairs={{0,1},{1,2},{2,3},{3,4},{4,5},{5,6},{6,7},{8,9},{9,10},{10,11},{11... | collective-permute-start | bytes 1544 | tf_op jit(solution)/shard_map/ppermute | solution.py:22
  267.5 11.1 %collective-permute-start.13 = (f32[32,4,1]{2,0,1:T(8,128)S(1)}, f32[32,4,1]{2,0,1:T(8,128)S(1)}, u32[]{:S(2)}, u32[]{:S(2)}) collective-permute-start(f32[32,4,1]{2,0,1:T(8,128)S(1)} %copy-done.20), channel_id=1, source_target_pairs={{1,0},{2,1},{3,2},{4,3},{5,4},{6,5},{7,6},{9,8},{10,9},{11,10},{12... | collective-permute-start | bytes 1544 | tf_op jit(solution)/shard_map/ppermute | solution.py:23
  281.9 5.6 %collective-permute-start.14 = (f32[32,4,1]{2,0,1:T(8,128)S(1)}, f32[32,4,1]{2,0,1:T(8,128)S(1)}, u32[]{:S(2)}, u32[]{:S(2)}) collective-permute-start(f32[32,4,1]{2,0,1:T(8,128)S(1)} %get-tuple-element.19), channel_id=1, source_target_pairs={{0,1},{1,2},{2,3},{3,4},{4,5},{5,6},{6,7},{8,9},{9,10},{10,11},{11... | collective-permute-start | bytes 1544 | tf_op jit(solution)/shard_map/ppermute | solution.py:22
  294.6 6.8 %collective-permute-start.16 = (f32[32,4,1]{2,0,1:T(8,128)S(1)}, f32[32,4,1]{2,0,1:T(8,128)S(1)}, u32[]{:S(2)}, u32[]{:S(2)}) collective-permute-start(f32[32,4,1]{2,0,1:T(8,128)S(1)} %get-tuple-element.13), channel_id=1, source_target_pairs={{0,1},{1,2},{2,3},{3,4},{4,5},{5,6},{6,7},{8,9},{9,10},{10,11},{11... | collective-permute-start | bytes 1544 | tf_op jit(solution)/shard_map/ppermute | solution.py:22
  298.4 8.6 %collective-permute-start.17 = (f32[32,4,1]{2,0,1:T(8,128)S(1)}, f32[32,4,1]{2,0,1:T(8,128)S(1)}, u32[]{:S(2)}, u32[]{:S(2)}) collective-permute-start(f32[32,4,1]{2,0,1:T(8,128)S(1)} %get-tuple-element.14), channel_id=1, source_target_pairs={{1,0},{2,1},{3,2},{4,3},{5,4},{6,5},{7,6},{9,8},{10,9},{11,10},{12... | collective-permute-start | bytes 1544 | tf_op jit(solution)/shard_map/ppermute | solution.py:23
  309.5 37.5 %all-to-all-start.6 = ((f32[8,32,1024]{2,1,0:T(8,128)}), f32[8,32,1024]{2,1,0:T(8,128)}, u32[]{:S(2)}, u32[]{:S(2)}) async-start(f32[8,32,1024]{2,1,0:T(8,128)} %bitcast.81), calls=%async_computation.6 | async-start | bytes 2097152 | tf_op jit(solution)/shard_map/all_to_all | solution.py:51
  (39 other events, 1160.1 us)
where the time goes:
time: 396 us; the launch traced here: 390 us
  starting transfers between devices  121 us (31%)
  local copies, waits for them, and re-layouts  72.8 us (18%)
  matrix products  63.8 us (16%)
  waiting for transfers between devices  58.5 us (15%)
  other arithmetic  35.9 us (9%)
  blocking collectives  34.1 us (9%)
    ppermute x9, starting transfers between devices, padded(): before = lax.ppermute(last, axis, up)  34.6 us
    all_to_all x3, starting transfers between devices, summed_on_arrival(): parts = lax.all_to_all(in_blocks(x, dim, peers), axis, 0, 0, tiled=True)  34.5 us
    all_to_all x1, blocking collectives, summed_on_arrival(): parts = lax.all_to_all(in_blocks(x, dim, peers), axis, 0, 0, tiled=True)  34.1 us
    all_to_all x4, starting transfers between devices, from_everyone(): lax.all_to_all(jnp.broadcast_to(x[None], (peers, *x.shape)), axis, 0, 0,...  30.2 us
    all_to_all x4, waiting for transfers between devices, from_everyone(): lax.all_to_all(jnp.broadcast_to(x[None], (peers, *x.shape)), axis, 0, 0,...  25.7 us
    dot_general x2, matrix products, apply_slots(): jnp.einsum('rsk,sjk->srj', col_parts, panel_part, preferred_element_type=...  25.4 us
    ppermute x9, starting transfers between devices, padded(): after = lax.ppermute(first, axis, down)  21.9 us
    all_to_all x3, waiting for transfers between devices, summed_on_arrival(): parts = lax.all_to_all(in_blocks(x, dim, peers), axis, 0, 0, tiled=True)  20 us
  transfers between devices with their start and end apart: 25, of which 6 were waited for; matrix products, arithmetic and copies ran while one was open for 33% of the time, Pallas kernels for 0%

commit v1 on v0

v1 whole, which is shorter than its diff:
```python
import functools

import jax
import jax.numpy as jnp
from jax import lax
from jax.experimental import pallas as pl
from jax.experimental.pallas import tpu as pltpu
from jax.sharding import PartitionSpec as P

ITERS = 2
SWEEPS = 4
COUPLING_STEP = 0.3
JACOBI_WEIGHT = 0.8
CELL_MASS = 0.05

RHS = 32
TILE = 512
LANES = 128
N_COL = 16
N_ROW = 8
DENSE_COLS = 12
LAYERS = 4
SLOTS = 43
BAND_TILES = 32
WIN_TILES = 16
MID = 32
EXT = MID + 2
MIB = 1 << 20

VMEM = pl.BlockSpec(memory_space=pltpu.VMEM)
SMEM = pl.BlockSpec(memory_space=pltpu.SMEM)
ANY = pl.BlockSpec(memory_space=pl.ANY)
f32 = jnp.float32
bf16 = jnp.bfloat16


def exchange(x, axis):
    return lax.all_to_all(x, axis, 0, 0, tiled=True)


def put_everywhere(half_pair, out_ref, copies):
    for copy in range(copies):
        for half in range(2):
            out_ref[copy, half] = half_pair[half]


def start_body(trace_ref, out_ref):
    halves = [trace_ref[:, h * TILE : (h + 1) * TILE].astype(bf16) for h in range(2)]
    put_everywhere(halves, out_ref, N_COL)


def spread_start(trace_start):
    return pl.pallas_call(
        start_body,
        out_shape=jax.ShapeDtypeStruct((N_COL, 2, RHS, TILE), bf16),
        in_specs=[VMEM],
        out_specs=VMEM,
        name="spread_start",
    )(trace_start)


def row_body(scal_ref, band_ref, out_ref):
    halves = [band_ref[scal_ref[1]], band_ref[scal_ref[2]]]
    put_everywhere(halves, out_ref, N_ROW)


def spread_row(scal, band):
    return pl.pallas_call(
        row_body,
        out_shape=jax.ShapeDtypeStruct((N_ROW, 2, RHS, TILE), bf16),
        in_specs=[SMEM, VMEM],
        out_specs=VMEM,
        name="spread_row",
    )(scal, band)


def relax(scal_ref, band_ref, win_ref, coef_ref, state_ref, top_ref):
    first = scal_ref[3]
    row = scal_ref[4]
    before = jnp.maximum(row - 1, 0)
    after = jnp.minimum(row + 1, N_ROW - 1)
    top_ref[0] = win_ref[2 * before + 1, :, TILE - LANES :].astype(f32)
    top_ref[EXT - 1] = win_ref[2 * after, :, :LANES].astype(f32)
    for chunk in range(MID):
        lane = chunk % 4 * LANES
        top_ref[chunk + 1] = band_ref[first + chunk // 4, :, lane : lane + LANES].astype(f32)
    lane_id = lax.broadcasted_iota(jnp.int32, (RHS, LANES), 1)
    is_first = lane_id == 0
    is_last = lane_id == LANES - 1

    def sweep(source, target):
        def one_chunk(chunk, carry):
            top = top_ref[chunk]
            centre = [state_ref[source, chunk + 1, l] for l in range(LAYERS)]
            for l in range(LAYERS):
                prev = state_ref[source, chunk, l]
                nxt = state_ref[source, chunk + 2, l]
                left = pltpu.roll(jnp.where(is_last, prev, centre[l]), 1, 1)
                right = pltpu.roll(jnp.where(is_first, nxt, centre[l]), LANES - 1, 1)
                upper = top if l == 0 else centre[l - 1]
                value = (
                    (1.0 - JACOBI_WEIGHT) * centre[l]
                    + coef_ref[chunk, l : l + 1, :] * left
                    + coef_ref[chunk, 4 + l : 5 + l, :] * right
                    + coef_ref[chunk, 8 + l : 9 + l, :] * upper
                    + coef_ref[chunk, 16 + l : 17 + l, :]
                )
                if l + 1 < LAYERS:
                    value = value + coef_ref[chunk, 12 + l : 13 + l, :] * centre[l + 1]
                state_ref[target, chunk + 1, l] = value
            return carry

        lax.fori_loop(0, EXT, one_chunk, 0)

    for step in range(SWEEPS):
        sweep(step % 2, 1 - step % 2)


def work_body(
    first_iteration,
    ident_ref,
    scal_ref,
    band_ref,
    win_ref,
    coef_ref,
    panel_ref,
    *refs,
):
    if first_iteration:
        band_out, head_out, win_out, saved_ref = refs[:4]
        scratch = refs[4:]
    else:
        saved_ref, band_out, head_out, win_out = refs[:4]
        scratch = refs[4:]
    buffer_ref, band_acc, win_acc, state_ref, top_ref, panel_sems, state_sem = scratch
    is_volume = scal_ref[0] == 1

    def fetch(slot):
        return pltpu.make_async_copy(panel_ref.at[slot], buffer_ref.at[slot], panel_sems.at[slot])

    @pl.when(jnp.logical_not(is_volume))
    def _():
        def start(slot, carry):
            fetch(slot).start()
            return carry

        lax.fori_loop(0, SLOTS, start, 0)
        band_acc[...] = jnp.zeros_like(band_acc)
        win_acc[...] = jnp.zeros_like(win_acc)

        def one_tile(slot, carry):
            ident = ident_ref[slot]
            named = ident >= 0
            safe = jnp.maximum(ident, 0)
            row_tile = lax.shift_right_logical(safe, 8)
            col_tile = jnp.bitwise_and(safe, 15)
            band_tile = lax.shift_right_logical(row_tile, 4) * 2 + jnp.bitwise_and(row_tile, 1)
            band_to = jnp.where(named, band_tile, BAND_TILES)
            win_to = jnp.where(named, col_tile, WIN_TILES)
            fetch(slot).wait()
            panel = buffer_ref[slot]
            win_acc[win_to] += jnp.dot(band_ref[band_tile], panel, preferred_element_type=f32)
            band_acc[band_to] += lax.dot_general(
                win_ref[col_tile], panel, (((1,), (1,)), ((), ())), preferred_element_type=f32
            )
            return carry

        lax.fori_loop(0, SLOTS, one_tile, 0)
        band_out[...] = band_acc[:BAND_TILES].astype(bf16)
        head_out[...] = band_acc[:2]
        win_out[...] = win_acc[:WIN_TILES].astype(bf16)

    @pl.when(is_volume)
    def _():
        if first_iteration:
            state_ref[...] = jnp.zeros_like(state_ref)
        else:
            load = pltpu.make_async_copy(saved_ref, state_ref.at[0], state_sem)
            load.start()
            for guard in (0, EXT + 1):
                state_ref[1, guard] = jnp.zeros((LAYERS, RHS, LANES), f32)
            load.wait()
        relax(scal_ref, band_ref, win_ref, coef_ref, state_ref, top_ref)
        band_out[...] = jnp.zeros_like(band_out)
        head_out[...] = jnp.zeros_like(head_out)
        win_out[...] = jnp.zeros_like(win_out)
        first = scal_ref[3]
        for chunk in range(MID):
            lane = chunk % 4 * LANES
            flux = coef_ref[chunk + 1, 20:21, :] * (top_ref[chunk + 1] - state_ref[0, chunk + 2, 0])
            band_out[first + chunk // 4, :, lane : lane + LANES] = flux.astype(bf16)

            @pl.when(first + chunk // 4 < 2)
            def _():
                head_out[first + chunk // 4, :, lane : lane + LANES] = flux

        if first_iteration:
            save = pltpu.make_async_copy(state_ref.at[0], saved_ref, state_sem)
            save.start()
            save.wait()


def work(ident, scal, band, win, coefs, panel, saved):
    first_iteration = saved is None
    outs = [
        jax.ShapeDtypeStruct((BAND_TILES, RHS, TILE), bf16),
        jax.ShapeDtypeStruct((2, RHS, TILE), f32),
        jax.ShapeDtypeStruct((WIN_TILES, RHS, TILE), bf16),
    ]
    out_specs = [VMEM, VMEM, VMEM]
    in_specs = [SMEM, SMEM, VMEM, VMEM, VMEM, ANY]
    args = [ident, scal, band, win, coefs, panel]
    state = jax.ShapeDtypeStruct((EXT + 2, LAYERS, RHS, LANES), f32)
    if first_iteration:
        outs.append(state)
        out_specs.append(ANY)
    else:
        in_specs.append(ANY)
        args.append(saved)
    return pl.pallas_call(
        functools.partial(work_body, first_iteration),
        out_shape=outs,
        in_specs=in_specs,
        out_specs=out_specs,
        scratch_shapes=[
            pltpu.VMEM((SLOTS, TILE, TILE), bf16),
            pltpu.VMEM((BAND_TILES + 1, RHS, TILE), f32),
            pltpu.VMEM((WIN_TILES + 1, RHS, TILE), f32),
            pltpu.VMEM((2, EXT + 2, LAYERS, RHS, LANES), f32),
            pltpu.VMEM((EXT, RHS, LANES), f32),
            pltpu.SemaphoreType.DMA((SLOTS,)),
            pltpu.SemaphoreType.DMA(()),
        ],
        compiler_params=pltpu.CompilerParams(vmem_limit_bytes=46 * MIB),
        name="work_first" if first_iteration else "work_next",
    )(*args)


def head_body(parts_ref, head_ref, band_ref, out_ref):
    total = head_ref[...]
    for peer in range(N_ROW):
        total = total + parts_ref[peer].astype(f32)
    out_ref[0] = total.astype(bf16)


def add_head(parts, head, band):
    return pl.pallas_call(
        head_body,
        grid=(1,),
        out_shape=jax.ShapeDtypeStruct((N_COL, 2, RHS, TILE), bf16),
        in_specs=[
            pl.BlockSpec((N_ROW, 2, RHS, TILE), lambda i: (0, 0, 0, 0)),
            pl.BlockSpec((2, RHS, TILE), lambda i: (0, 0, 0)),
            ANY,
        ],
        out_specs=pl.BlockSpec((1, 2, RHS, TILE), lambda i: (0, 0, 0, 0)),
        input_output_aliases={2: 0},
        name="add_head",
    )(parts, head, band)


def update_body(last, parts_ref, trace_ref, load_ref, *outs):
    for half in range(2):
        lanes = slice(half * TILE, (half + 1) * TILE)
        total = parts_ref[0, half].astype(f32)
        for peer in range(1, N_COL):
            total = total + parts_ref[peer, half].astype(f32)
        trace = trace_ref[:, lanes]
        trace = trace + COUPLING_STEP * (load_ref[:, lanes] - trace - total)
        outs[0][:, lanes] = trace
        if last:
            outs[1][:, lanes] = total
        else:
            rounded = trace.astype(bf16)
            for copy in range(N_COL):
                outs[1][copy, half] = rounded


def update(parts, traces, load, last):
    whole = jax.ShapeDtypeStruct(traces.shape, f32)
    return pl.pallas_call(
        functools.partial(update_body, last),
        out_shape=[whole, whole if last else jax.ShapeDtypeStruct(parts.shape, bf16)],
        in_specs=[VMEM, VMEM, VMEM],
        out_specs=[VMEM, VMEM],
        name="update_last" if last else "update_next",
    )(parts, traces, load)


def volume_weights(coef_index, coef_table, vol_source, volume_line, row_index):
    indices = lax.dynamic_index_in_dim(coef_index, volume_line, 0, keepdims=False)
    source = lax.dynamic_index_in_dim(vol_source, volume_line, 0, keepdims=False)
    levels = jnp.arange(coef_table.shape[0], dtype=jnp.int32)
    k = jnp.sum(jnp.where(indices[..., None] == levels, coef_table, 0.0), axis=-1)
    both = jnp.concatenate([k, source], 0)
    up = [(i, i + 1) for i in range(N_ROW - 1)]
    down = [(i + 1, i) for i in range(N_ROW - 1)]
    before = lax.ppermute(both[:, -LANES:], "row", up)
    after = lax.ppermute(both[:, :LANES], "row", down)
    both = jnp.concatenate([before, both, after], 1)
    k, source = both[:LAYERS], both[LAYERS:]
    wide = jnp.pad(k, ((0, 0), (1, 1)))
    left = 0.5 * (k + wide[:, :-2])
    right = 0.5 * (k + wide[:, 2:])
    between = 0.5 * (k[:-1] + k[1:])
    upper = jnp.concatenate([k[:1], between], 0)
    lower = jnp.concatenate([between, jnp.zeros_like(k[:1])], 0)
    node = jnp.arange(k.shape[1], dtype=jnp.int32) - LANES
    inside = ((node >= 0) | (row_index > 0)) & ((node < MID * LANES) | (row_index < N_ROW - 1))
    scale = jnp.where(inside, JACOBI_WEIGHT / (left + right + upper + lower + CELL_MASS), 0.0)
    rows = jnp.concatenate(
        [left * scale, right * scale, upper * scale, lower * scale, source * scale, k], 0
    )
    return rows.reshape(24, EXT, LANES).transpose(1, 0, 2)


def local(
    trace_start, surface_load, panel_tiles, tile_list, surf_map, coef_index, coef_table, vol_source
):
    col_index = lax.axis_index("col")
    row_index = lax.axis_index("row")
    volume_line = jnp.maximum(col_index - DENSE_COLS, 0)
    is_volume = col_index >= DENSE_COLS
    volume_tile = volume_line * N_ROW + row_index
    tile_numbers = jnp.arange(surf_map.shape[0], dtype=jnp.int32)
    quarter = jnp.sum(jnp.where(surf_map == volume_tile, tile_numbers, 0)) % 4
    first = quarter * 8
    scal = jnp.stack(
        [
            is_volume.astype(jnp.int32),
            jnp.where(is_volume, first, 0),
            jnp.where(is_volume, first + 7, 1),
            first,
            row_index,
        ]
    ).astype(jnp.int32)
    traces = trace_start
    spread = spread_start(traces)
    coefs = volume_weights(coef_index, coef_table, vol_source, volume_line, row_index)
    saved = None
    for iteration in range(ITERS):
        last = iteration == ITERS - 1
        band = exchange(spread, "col").reshape(BAND_TILES, RHS, TILE)
        win = exchange(spread_row(scal, band), "row").reshape(WIN_TILES, RHS, TILE)
        made = work(tile_list, scal, band, win, coefs, panel_tiles, saved)
        band_part, head, win_part = made[:3]
        saved = None if last else made[3]
        win_parts = exchange(win_part.reshape(N_ROW, 2, RHS, TILE), "row")
        band_part = add_head(win_parts, head, band_part.reshape(N_COL, 2, RHS, TILE))
        traces, spread = update(exchange(band_part, "col"), traces, surface_load, last)
    return (traces, spread)


def solution(mesh):
    return jax.shard_map(
        local,
        mesh=mesh,
        in_specs=(
            P(None, ("col", "row")),
            P(None, ("col", "row")),
            P(("col", "row"), None, None),
            P(("col", "row")),
            P(),
            P(None, None, "row"),
            P(),
            P(None, None, "row"),
        ),
        out_specs=(P(None, ("col", "row")), P(None, ("col", "row"))),
        check_vma=False,
    )
```

time: 396 us -> 217 us (0.55); the launches traced: 390 us -> 216 us
  starting transfers between devices: 121 us -> 21.5 us
  blocking collectives: 34.1 us -> 105 us
  matrix products: 63.8 us -> 0 us
  local copies, waits for them, and re-layouts: 72.8 us -> 11.2 us
  Pallas kernels: 0 us -> 49.1 us
  waiting for transfers between devices: 58.5 us -> 23 us
  other arithmetic: 35.9 us -> 2.63 us
    all_to_all x1 -> x6, blocking collectives: 34.1 us -> 105 us  [exchange(): return lax.all_to_all(x, axis, 0, 0, tiled=True)]
    dot_general x8 -> x0, matrix products: 63.8 us -> none  [the longest x2 25.4 us: apply_slots(): jnp.einsum('rsk,sjk->srj', col_parts, panel_part, preferred_element_type=...]
    ppermute x18 -> x2, starting transfers between devices: 56.5 us -> 5.24 us  [the longest x1 3.94 us: volume_weights(): before = lax.ppermute(both[:, -LANES:], 'row', up)]
    pallas_call x0 -> x9, Pallas kernels: none -> 49.1 us  [the longest x2 34.7 us: work(): pl.pallas_call(functools.partial(work_body, first_iteration), out_shape=o...]
    all_to_all x7 -> x2, starting transfers between devices: 64.6 us -> 16.3 us  [exchange(): return lax.all_to_all(x, axis, 0, 0, tiled=True)]
    all_to_all x7 -> x2, waiting for transfers between devices: 45.7 us -> 23 us  [exchange(): return lax.all_to_all(x, axis, 0, 0, tiled=True)]
    another operation x14 -> x1, local copies, waits for them, and re-layouts: 21.8 us -> 0.61 us  [local(): jnp.stack([is_volume.astype(jnp.int32), jnp.where(is_volume, first, 0), j...]
    add x9 -> x0, other arithmetic: 19.2 us -> none  [the longest x6 15.8 us: relax_line(): return (1.0 - JACOBI_WEIGHT) * centre + JACOBI_WEIGHT * gathered / diagonal]
  transfers between devices with their start and end apart: 25 -> 4, of which waited for: 6 -> 2; matrix products, arithmetic and copies ran while one was open for 33% -> 1% of each run, Pallas kernels for 0% -> 1%
where the time goes in v1:
time: 217 us; the launch traced here: 216 us
  blocking collectives  105 us (48%)
  Pallas kernels  49.1 us (23%)
  waiting for transfers between devices  23 us (11%)
  starting transfers between devices  21.5 us (10%)
  local copies, waits for them, and re-layouts  11.2 us (5%)
  between operations  2.74 us (1%)
  other arithmetic  2.63 us (1%)
    all_to_all x6, blocking collectives, exchange(): return lax.all_to_all(x, axis, 0, 0, tiled=True)  105 us
    pallas_call x2, Pallas kernels, work(): pl.pallas_call(functools.partial(work_body, first_iteration), out_shape=o...  34.7 us
    all_to_all x2, waiting for transfers between devices, exchange(): return lax.all_to_all(x, axis, 0, 0, tiled=True)  23 us
    all_to_all x2, starting transfers between devices, exchange(): return lax.all_to_all(x, axis, 0, 0, tiled=True)  16.3 us
    unnamed x28, local copies, waits for them, and re-layouts  9.47 us
    pallas_call x2, Pallas kernels, update(): pl.pallas_call(functools.partial(update_body, last), out_shape=[whole, wh...  4.69 us
  transfers between devices with their start and end apart: 4, of which 2 were waited for; matrix products, arithmetic and copies ran while one was open for 1% of the time, Pallas kernels for 1%

profile of v1, /device:TPU:1, one launch (start us, length us, event | category | flops | bytes accessed | tf_op | source)
XLA Modules:
  0.0 215.6 jit_solution(8911552014399388381)
XLA Ops:
  3.4 3.9 %collective-permute-start = (f32[8,128]{1,0:T(8,128)S(1)}, f32[8,128]{1,0:T(8,128)S(1)}, u32[]{:S(2)}, u32[]{:S(2)}) collective-permute-start(f32[8,128]{1,0:T(8,128)S(1)} %get-tuple-element.26), channel_id=1, source_target_pairs={{0,1},{1,2},{2,3},{3,4},{4,5},{5,6},{6,7},{8,9},{9,10},{10,11},{11... | collective-permute-start | bytes 12296 | tf_op jit(solution)/shard_map/ppermute | solution.py:298
  7.4 1.3 collective-permute-start.1
  8.7 2.0 spread_start.1
  10.7 6.9 %all-to-all-start = ((bf16[16,2,32,512]{3,2,1,0:T(8,128)(2,1)}), bf16[16,2,32,512]{3,2,1,0:T(8,128)(2,1)S(1)}, u32[]{:S(2)}, u32[]{:S(2)}) async-start(bf16[16,2,32,512]{3,2,1,0:T(8,128)(2,1)} %spread_start.1), calls=%async_computation | async-start | bytes 2097152 | tf_op jit(solution)/shard_map/all_to_all | solution.py:38
  17.6 1.3 fusion.12
  21.7 11.7 %all-to-all-done = bf16[16,2,32,512]{3,2,1,0:T(8,128)(2,1)S(1)} async-done(((bf16[16,2,32,512]{3,2,1,0:T(8,128)(2,1)}), bf16[16,2,32,512]{3,2,1,0:T(8,128)(2,1)S(1)}, u32[]{:S(2)}, u32[]{:S(2)}) %all-to-all-start) | async-done | bytes 1048608 | tf_op jit(solution)/shard_map/all_to_all | solution.py:38
  34.4 2.1 spread_row.2
  36.5 9.3 %all-to-all-start.1 = ((bf16[8,2,32,512]{3,2,1,0:T(8,128)(2,1)}), bf16[8,2,32,512]{3,2,1,0:T(8,128)(2,1)S(1)}, u32[]{:S(2)}, u32[]{:S(2)}) async-start(bf16[8,2,32,512]{3,2,1,0:T(8,128)(2,1)} %spread_row.2), calls=%async_computation.1 | async-start | bytes 1048576 | tf_op jit(solution)/shard_map/all_to_all | solution.py:38
  46.3 11.3 %all-to-all-done.1 = bf16[8,2,32,512]{3,2,1,0:T(8,128)(2,1)S(1)} async-done(((bf16[8,2,32,512]{3,2,1,0:T(8,128)(2,1)}), bf16[8,2,32,512]{3,2,1,0:T(8,128)(2,1)S(1)}, u32[]{:S(2)}, u32[]{:S(2)}) %all-to-all-start.1) | async-done | bytes 524320 | tf_op jit(solution)/shard_map/all_to_all | solution.py:38
  58.4 1.2 copy-done.2
  61.9 17.4 %work_first.1 = (bf16[32,32,512]{2,1,0:T(8,128)(2,1)S(1)}, f32[2,32,512]{2,1,0:T(8,128)S(1)}, bf16[16,32,512]{2,1,0:T(8,128)(2,1)S(1)}, f32[36,4,32,128]{3,2,1,0:T(8,128)S(1)}) custom-call(s32[43]{0:T(128)S(1)} %copy-done.12, s32[5]{0:T(128)S(1)} %copy-done.10, bf16[32,32,512]{2,1,0:T(8,128)(2,1)S(1)} %bitcast.25, bf16[16,32,512]{2,1,0:T(8,128)(2,1)S(1)} %bitcast.30, ...), custom_call_target="tpu_custom_call" | custom-call | tf_op jit(solution)/shard_map/work_first/pallas_call | solution.py:220
  80.3 13.8 %all_to_all.40.parts_ref = bf16[8,2,32,512]{3,2,1,0:T(8,128)(2,1)} all-to-all(bf16[8,2,32,512]{3,2,1,0:T(8,128)(2,1)S(1)} %bitcast.33), channel_id=1, replica_groups=mesh['col'=16,'row'=8] {'row'}, dimensions={0} | all-to-all | bytes 1048576 | tf_op jit(solution)/shard_map/all_to_all | solution.py:38
  94.0 1.8 add_head.2
  95.8 21.6 %all_to_all.41.parts_ref = bf16[16,2,32,512]{3,2,1,0:T(8,128)(2,1)} all-to-all(bf16[16,2,32,512]{3,2,1,0:T(8,128)(2,1)} %add_head.2), channel_id=1, replica_groups=mesh['col'=16,'row'=8] {'col'}, dimensions={0} | all-to-all | bytes 2097152 | tf_op jit(solution)/shard_map/all_to_all | solution.py:38
  117.4 2.5 %update_next.1 = (f32[32,1024]{1,0:T(8,128)}, bf16[16,2,32,512]{3,2,1,0:T(8,128)(2,1)}) custom-call(bf16[16,2,32,512]{3,2,1,0:T(8,128)(2,1)} %all_to_all.41.parts_ref, f32[32,1024]{1,0:T(8,128)} %trace_ref.3, f32[32,1024]{1,0:T(8,128)} %load_ref.3), custom_call_target="tpu_custom_call" | custom-call | tf_op jit(solution)/shard_map/update_next/pallas_call | solution.py:281
  119.9 20.8 %all_to_all.42 = bf16[16,2,32,512]{3,2,1,0:T(8,128)(2,1)} all-to-all(bf16[16,2,32,512]{3,2,1,0:T(8,128)(2,1)} %get-tuple-element.14), channel_id=1, replica_groups=mesh['col'=16,'row'=8] {'col'}, dimensions={0} | all-to-all | bytes 2097152 | tf_op jit(solution)/shard_map/all_to_all | solution.py:38
  140.7 2.1 spread_row.3
  142.8 14.0 %all_to_all.43 = bf16[8,2,32,512]{3,2,1,0:T(8,128)(2,1)S(1)} all-to-all(bf16[8,2,32,512]{3,2,1,0:T(8,128)(2,1)} %spread_row.3), channel_id=1, replica_groups=mesh['col'=16,'row'=8] {'row'}, dimensions={0} | all-to-all | bytes 1048576 | tf_op jit(solution)/shard_map/all_to_all | solution.py:38
  156.8 1.2 copy-done.3
  158.0 17.3 %work_next.1 = (bf16[32,32,512]{2,1,0:T(8,128)(2,1)S(1)}, f32[2,32,512]{2,1,0:T(8,128)S(1)}, bf16[16,32,512]{2,1,0:T(8,128)(2,1)S(1)}) custom-call(s32[43]{0:T(128)S(1)} %copy-done.13, s32[5]{0:T(128)S(1)} %copy-done.11, bf16[32,32,512]{2,1,0:T(8,128)(2,1)S(1)} %bitcast.27, bf16[16,32,512]{2,1,0:T(8,128)(2,1)S(1)} %bitcast.31, ...), custom_call_target="tpu_custom_call" | custom-call | tf_op jit(solution)/shard_map/work_next/pallas_call | solution.py:220
  176.3 13.4 %all_to_all.44.parts_ref = bf16[8,2,32,512]{3,2,1,0:T(8,128)(2,1)} all-to-all(bf16[8,2,32,512]{3,2,1,0:T(8,128)(2,1)S(1)} %bitcast.32), channel_id=1, replica_groups=mesh['col'=16,'row'=8] {'row'}, dimensions={0} | all-to-all | bytes 1048576 | tf_op jit(solution)/shard_map/all_to_all | solution.py:38
  189.7 1.8 add_head.3
  191.5 22.0 %all_to_all.45.parts_ref = bf16[16,2,32,512]{3,2,1,0:T(8,128)(2,1)} all-to-all(bf16[16,2,32,512]{3,2,1,0:T(8,128)(2,1)} %add_head.3), channel_id=1, replica_groups=mesh['col'=16,'row'=8] {'col'}, dimensions={0} | all-to-all | bytes 2097152 | tf_op jit(solution)/shard_map/all_to_all | solution.py:38
  213.5 2.2 %update_last.1 = (f32[32,1024]{1,0:T(8,128)}, f32[32,1024]{1,0:T(8,128)}) custom-call(bf16[16,2,32,512]{3,2,1,0:T(8,128)(2,1)} %all_to_all.45.parts_ref, f32[32,1024]{1,0:T(8,128)} %get-tuple-element.19.trace_ref, f32[32,1024]{1,0:T(8,128)} %load_ref.3), custom_call_target="tpu_custom_call" | custom-call | tf_op jit(solution)/shard_map/update_last/pallas_call | solution.py:281
  (41 shorter events, 10.1 us)
Async XLA Ops:
  0.6 1.0 copy-start
  3.4 18.1 %collective-permute-start = (f32[8,128]{1,0:T(8,128)S(1)}, f32[8,128]{1,0:T(8,128)S(1)}, u32[]{:S(2)}, u32[]{:S(2)}) collective-permute-start(f32[8,128]{1,0:T(8,128)S(1)} %get-tuple-element.26), channel_id=1, source_target_pairs={{0,1},{1,2},{2,3},{3,4},{4,5},{5,6},{6,7},{8,9},{9,10},{10,11},{11... | collective-permute-start | bytes 12296 | tf_op jit(solution)/shard_map/ppermute | solution.py:298
  7.4 14.1 %collective-permute-start.1 = (f32[8,128]{1,0:T(8,128)S(1)}, f32[8,128]{1,0:T(8,128)S(1)}, u32[]{:S(2)}, u32[]{:S(2)}) collective-permute-start(f32[8,128]{1,0:T(8,128)S(1)} %get-tuple-element.27), channel_id=1, source_target_pairs={{1,0},{2,1},{3,2},{4,3},{5,4},{6,5},{7,6},{9,8},{10,9},{11,10},{12... | collective-permute-start | bytes 12296 | tf_op jit(solution)/shard_map/ppermute | solution.py:299
  10.7 146.1 %copy-start.13 = (s32[43]{0:T(128)S(1)}, s32[43]{0:T(128)}, u32[]{:S(2)}) copy-start(s32[43]{0:T(128)} %ident_ref.3) | copy-start | bytes 520
  10.7 22.8 %all-to-all-start = ((bf16[16,2,32,512]{3,2,1,0:T(8,128)(2,1)}), bf16[16,2,32,512]{3,2,1,0:T(8,128)(2,1)S(1)}, u32[]{:S(2)}, u32[]{:S(2)}) async-start(bf16[16,2,32,512]{3,2,1,0:T(8,128)(2,1)} %spread_start.1), calls=%async_computation | async-start | bytes 2097152 | tf_op jit(solution)/shard_map/all_to_all | solution.py:38
  21.5 135.3 %copy-start.11 = (s32[5]{0:T(128)S(1)}, s32[5]{0:T(128)}, u32[]{:S(2)}) copy-start(s32[5]{0:T(128)} %stack.27.scal_ref) | copy-start | bytes 64
  33.4 1.0 copy-start.1
  36.5 21.0 %all-to-all-start.1 = ((bf16[8,2,32,512]{3,2,1,0:T(8,128)(2,1)}), bf16[8,2,32,512]{3,2,1,0:T(8,128)(2,1)S(1)}, u32[]{:S(2)}, u32[]{:S(2)}) async-start(bf16[8,2,32,512]{3,2,1,0:T(8,128)(2,1)} %spread_row.2), calls=%async_computation.1 | async-start | bytes 1048576 | tf_op jit(solution)/shard_map/all_to_all | solution.py:38
  57.6 0.8 copy-start.6
  58.4 1.2 copy-start.2
  59.6 1.0 copy-start.7
  60.6 0.6 copy-start.10
  61.3 0.7 copy-start.12
  79.3 1.0 copy-start.5
  80.2 13.8 %copy-start.9 = (f32[2,32,512]{2,1,0:T(8,128)}, f32[2,32,512]{2,1,0:T(8,128)S(1)}, u32[]{:S(2)}) copy-start(f32[2,32,512]{2,1,0:T(8,128)S(1)} %get-tuple-element.12.head_ref) | copy-start | bytes 393220
  156.8 1.2 copy-start.3
  175.3 1.0 copy-start.4
  176.3 13.4 %copy-start.8 = (f32[2,32,512]{2,1,0:T(8,128)}, f32[2,32,512]{2,1,0:T(8,128)S(1)}, u32[]{:S(2)}) copy-start(f32[2,32,512]{2,1,0:T(8,128)S(1)} %get-tuple-element.17.head_ref) | copy-start | bytes 393220

commit v2 on v1

v2 whole, which is shorter than its diff:
```python
import functools

import jax
import jax.numpy as jnp
from jax import lax
from jax.experimental import pallas as pl
from jax.experimental.pallas import tpu as pltpu
from jax.sharding import PartitionSpec as P

ITERS = 2
SWEEPS = 4
COUPLING_STEP = 0.3
JACOBI_WEIGHT = 0.8
CELL_MASS = 0.05

RHS = 32
TILE = 512
LANES = 128
N_COL = 16
N_ROW = 8
DENSE_COLS = 12
LAYERS = 4
SLOTS = 43
GROUP = 4
COEFS = 16
BAND_TILES = 32
WIN_TILES = 16
MID = 32
EXT = MID + 2
MIB = 1 << 20

VMEM = pl.BlockSpec(memory_space=pltpu.VMEM)
SMEM = pl.BlockSpec(memory_space=pltpu.SMEM)
ANY = pl.BlockSpec(memory_space=pl.ANY)
f32 = jnp.float32
bf16 = jnp.bfloat16


def exchange(x, axis):
    return lax.all_to_all(x, axis, 0, 0, tiled=True)


def put_everywhere(half_pair, out_ref, copies):
    for copy in range(copies):
        for half in range(2):
            out_ref[copy, half] = half_pair[half]


def start_body(trace_ref, out_ref):
    halves = [trace_ref[:, h * TILE : (h + 1) * TILE].astype(bf16) for h in range(2)]
    put_everywhere(halves, out_ref, N_COL)


def spread_start(trace_start):
    return pl.pallas_call(
        start_body,
        out_shape=jax.ShapeDtypeStruct((N_COL, 2, RHS, TILE), bf16),
        in_specs=[VMEM],
        out_specs=VMEM,
        compiler_params=pltpu.CompilerParams(vmem_limit_bytes=6 * MIB),
        name="spread_start",
    )(trace_start)


def row_body(first_iteration, scal_ref, band_ref, *refs):
    out_ref = refs[-1]
    halves = [band_ref[scal_ref[1]], band_ref[scal_ref[2]]]
    put_everywhere(halves, out_ref, N_ROW)
    if first_iteration:

        @pl.when(scal_ref[0] == 1)
        def _():
            for peer in range(N_ROW):
                out_ref[peer, 0, :, LANES : 3 * LANES] = refs[0][...]


def spread_row(scal, band, edges):
    first_iteration = edges is not None
    args = [scal, band] + ([edges] if first_iteration else [])
    return pl.pallas_call(
        functools.partial(row_body, first_iteration),
        out_shape=jax.ShapeDtypeStruct((N_ROW, 2, RHS, TILE), bf16),
        in_specs=[SMEM] + [VMEM] * (len(args) - 1),
        out_specs=VMEM,
        compiler_params=pltpu.CompilerParams(vmem_limit_bytes=6 * MIB),
        name="spread_row",
    )(*args)


def for_slots(ident_ref, panel_ref, buffer_ref, sems, do_slot):
    def fetch(slot):
        return pltpu.make_async_copy(panel_ref.at[slot], buffer_ref.at[slot], sems.at[slot])

    def start(slot, carry):
        fetch(slot).start()
        return carry

    lax.fori_loop(0, SLOTS, start, 0)

    def place(slot):
        ident = ident_ref[slot]
        named = ident >= 0
        safe = jnp.maximum(ident, 0)
        row_tile = lax.shift_right_logical(safe, 8)
        col_tile = jnp.bitwise_and(safe, 15)
        band_tile = lax.shift_right_logical(row_tile, 4) * 2 + jnp.bitwise_and(row_tile, 1)
        do_slot(slot, named, band_tile, col_tile)

    def group(index, carry):
        for extra in range(GROUP):
            fetch(index * GROUP + extra).wait()
        for extra in range(GROUP):
            place(index * GROUP + extra)
        return carry

    lax.fori_loop(0, SLOTS // GROUP, group, 0)
    for slot in range(SLOTS // GROUP * GROUP, SLOTS):
        fetch(slot).wait()
        place(slot)


def window_body(ident_ref, scal_ref, band_ref, panel_ref, win_out, win_acc, buffer_ref, sems):
    win_acc[...] = jnp.zeros_like(win_acc)

    @pl.when(scal_ref[0] == 0)
    def _():
        def one_slot(slot, named, band_tile, col_tile):
            win_acc[jnp.where(named, col_tile, WIN_TILES)] += jnp.dot(
                band_ref[band_tile], buffer_ref[slot], preferred_element_type=f32
            )

        for_slots(ident_ref, panel_ref, buffer_ref, sems, one_slot)

    win_out[...] = win_acc[:WIN_TILES].astype(bf16)


def into_window(ident, scal, band, panel):
    return pl.pallas_call(
        window_body,
        out_shape=jax.ShapeDtypeStruct((WIN_TILES, RHS, TILE), bf16),
        in_specs=[SMEM, SMEM, VMEM, ANY],
        out_specs=VMEM,
        scratch_shapes=[
            pltpu.VMEM((WIN_TILES + 1, RHS, TILE), f32),
            pltpu.VMEM((SLOTS, TILE, TILE), bf16),
            pltpu.SemaphoreType.DMA((SLOTS,)),
        ],
        compiler_params=pltpu.CompilerParams(vmem_limit_bytes=44 * MIB),
        cost_estimate=pl.CostEstimate(flops=7 * 10**8, transcendentals=0, bytes_accessed=25 * 10**6),
        name="into_window",
    )(ident, scal, band, panel)


def weigh(scal_ref, table_ref, cells_ref, win_ref, cell_ref, coef_ref):
    row = scal_ref[4]
    before = jnp.maximum(row - 1, 0)
    after = jnp.minimum(row + 1, N_ROW - 1)
    layer = lax.broadcasted_iota(jnp.int32, (8, LANES), 0)
    lane = lax.broadcasted_iota(jnp.int32, (8, LANES), 1)
    nothing = jnp.zeros((8, LANES), f32)
    for chunk, source, start, here in (
        (0, 2 * before, 2 * LANES, row > 0),
        (EXT - 1, 2 * after, LANES, row < N_ROW - 1),
    ):
        sent = win_ref[source, :, start : start + LANES].astype(f32)
        k = nothing
        for level in range(COEFS):
            k = jnp.where(sent[0:8] == float(level), table_ref[level], k)
        cell_ref[chunk + 1, 0] = jnp.where((layer < LAYERS) & here, k, 0.0)
        cell_ref[chunk + 1, 1] = jnp.where(here, sent[8:16] + sent[16:24], 0.0)
    cell_ref[0, 0] = nothing
    cell_ref[EXT + 1, 0] = nothing

    for chunk in range(MID):
        cell_ref[chunk + 2] = cells_ref[chunk]

    def one_chunk(chunk, carry):
        k = cell_ref[chunk + 1, 0]
        left = pltpu.roll(jnp.where(lane == LANES - 1, cell_ref[chunk, 0], k), 1, 1)
        right = pltpu.roll(jnp.where(lane == 0, cell_ref[chunk + 2, 0], k), LANES - 1, 1)
        left = 0.5 * (k + left)
        right = 0.5 * (k + right)
        lower = jnp.where(layer < LAYERS - 1, 0.5 * (k + pltpu.roll(k, 7, 0)), 0.0)
        upper = jnp.where(layer == 0, k, pltpu.roll(lower, 1, 0))
        inside = ((chunk > 0) | (row > 0)) & ((chunk < EXT - 1) | (row < N_ROW - 1))
        scale = jnp.where(inside, JACOBI_WEIGHT / (left + right + upper + lower + CELL_MASS), 0.0)
        coef_ref[chunk, 0:8] = left * scale
        coef_ref[chunk, 8:16] = right * scale
        coef_ref[chunk, 16:24] = upper * scale
        coef_ref[chunk, 24:32] = lower * scale
        coef_ref[chunk, 32:40] = cell_ref[chunk + 1, 1] * scale
        coef_ref[chunk, 40:48] = k
        return carry

    lax.fori_loop(0, EXT, one_chunk, 0, unroll=2)


def relax(scal_ref, band_ref, win_ref, coef_ref, states, top_ref):
    first = scal_ref[3]
    row = scal_ref[4]
    before = jnp.maximum(row - 1, 0)
    after = jnp.minimum(row + 1, N_ROW - 1)
    top_ref[0] = win_ref[2 * before + 1, :, TILE - LANES :].astype(f32)
    top_ref[EXT - 1] = win_ref[2 * after, :, :LANES].astype(f32)
    for chunk in range(MID):
        start = chunk % 4 * LANES
        top_ref[chunk + 1] = band_ref[first + chunk // 4, :, start : start + LANES].astype(f32)
    lane = lax.broadcasted_iota(jnp.int32, (RHS, LANES), 1)
    is_first = lane == 0
    is_last = lane == LANES - 1

    def sweep(source_ref, target_ref):
        def one_chunk(chunk, carry):
            upper = top_ref[chunk]
            centre = source_ref[chunk + 1, 0]
            for l in range(LAYERS):
                left = pltpu.roll(jnp.where(is_last, source_ref[chunk, l], centre), 1, 1)
                right = pltpu.roll(jnp.where(is_first, source_ref[chunk + 2, l], centre), LANES - 1, 1)
                value = (
                    (1.0 - JACOBI_WEIGHT) * centre
                    + coef_ref[chunk, l : l + 1, :] * left
                    + coef_ref[chunk, 8 + l : 9 + l, :] * right
                    + coef_ref[chunk, 16 + l : 17 + l, :] * upper
                    + coef_ref[chunk, 32 + l : 33 + l, :]
                )
                if l + 1 < LAYERS:
                    below = source_ref[chunk + 1, l + 1]
                    value = value + coef_ref[chunk, 24 + l : 25 + l, :] * below
                    upper, centre = centre, below
                target_ref[chunk + 1, l] = value
            return carry

        lax.fori_loop(0, EXT, one_chunk, 0, unroll=2)

    for step in range(SWEEPS):
        sweep(states[step % 2], states[1 - step % 2])


def rows_body(first_iteration, ident_ref, scal_ref, band_ref, win_ref, panel_ref, *refs):
    if first_iteration:
        table_ref, cells_ref, band_out, head_out, state_out, coef_out = refs[:6]
        refs = refs[6:]
    else:
        state_in, coef_in, band_out, head_out = refs[:4]
        refs = refs[4:]
    band_acc, state_a, state_b, coef_ref, cell_ref, top_ref, sems, buffer_ref, panel_sems = refs
    is_volume = scal_ref[0] == 1

    @pl.when(jnp.logical_not(is_volume))
    def _():
        band_acc[...] = jnp.zeros_like(band_acc)

        def one_slot(slot, named, band_tile, col_tile):
            band_acc[jnp.where(named, band_tile, BAND_TILES)] += lax.dot_general(
                win_ref[col_tile],
                buffer_ref[slot],
                (((1,), (1,)), ((), ())),
                preferred_element_type=f32,
            )

        for_slots(ident_ref, panel_ref, buffer_ref, panel_sems, one_slot)
        band_out[...] = band_acc[:BAND_TILES].astype(bf16)
        head_out[...] = band_acc[:2]

    @pl.when(is_volume)
    def _():
        guard = jnp.zeros((LAYERS, RHS, LANES), f32)
        state_b[0] = guard
        state_b[EXT + 1] = guard
        if first_iteration:
            state_a[...] = jnp.zeros_like(state_a)
            weigh(scal_ref, table_ref, cells_ref, win_ref, cell_ref, coef_ref)
        else:
            loads = [
                pltpu.make_async_copy(state_in, state_a, sems.at[0]),
                pltpu.make_async_copy(coef_in, coef_ref, sems.at[1]),
            ]
            for load in loads:
                load.start()
            for load in loads:
                load.wait()
        relax(scal_ref, band_ref, win_ref, coef_ref, (state_a, state_b), top_ref)
        if first_iteration:
            saves = [
                pltpu.make_async_copy(state_a, state_out, sems.at[0]),
                pltpu.make_async_copy(coef_ref, coef_out, sems.at[1]),
            ]
            for save in saves:
                save.start()
        band_out[...] = jnp.zeros_like(band_out)
        head_out[...] = jnp.zeros_like(head_out)
        first = scal_ref[3]
        for chunk in range(MID):
            start = chunk % 4 * LANES
            flux = coef_ref[chunk + 1, 40:41, :] * (top_ref[chunk + 1] - state_a[chunk + 2, 0])
            band_out[first + chunk // 4, :, start : start + LANES] = flux.astype(bf16)
            if chunk < 8:

                @pl.when(first == 0)
                def _():
                    head_out[chunk // 4, :, start : start + LANES] = flux

        if first_iteration:
            for save in saves:
                save.wait()


def into_rows(ident, scal, band, win, panel, table, cells, saved):
    first_iteration = saved is None
    outs = [
        jax.ShapeDtypeStruct((BAND_TILES, RHS, TILE), bf16),
        jax.ShapeDtypeStruct((2, RHS, TILE), f32),
    ]
    out_specs = [VMEM, VMEM]
    in_specs = [SMEM, SMEM, VMEM, VMEM, ANY]
    args = [ident, scal, band, win, panel]
    state = (EXT + 2, LAYERS, RHS, LANES)
    coefs = (EXT, 48, LANES)
    if first_iteration:
        outs += [jax.ShapeDtypeStruct(state, f32), jax.ShapeDtypeStruct(coefs, f32)]
        out_specs += [ANY, ANY]
        in_specs += [SMEM, VMEM]
        args += [table, cells]
    else:
        in_specs += [ANY, ANY]
        args += saved
    return pl.pallas_call(
        functools.partial(rows_body, first_iteration),
        out_shape=outs,
        in_specs=in_specs,
        out_specs=out_specs,
        scratch_shapes=[
            pltpu.VMEM((BAND_TILES + 1, RHS, TILE), f32),
            pltpu.VMEM(state, f32),
            pltpu.VMEM(state, f32),
            pltpu.VMEM(coefs, f32),
            pltpu.VMEM((EXT + 2, 2, 8, LANES), f32),
            pltpu.VMEM((EXT, RHS, LANES), f32),
            pltpu.SemaphoreType.DMA((2,)),
            pltpu.VMEM((SLOTS, TILE, TILE), bf16),
            pltpu.SemaphoreType.DMA((SLOTS,)),
        ],
        compiler_params=pltpu.CompilerParams(vmem_limit_bytes=44 * MIB),
        cost_estimate=pl.CostEstimate(flops=7 * 10**8, transcendentals=0, bytes_accessed=30 * 10**6),
        name="into_rows_first" if first_iteration else "into_rows_next",
    )(*args)


def head_body(parts_ref, head_ref, band_ref, out_ref):
    total = head_ref[...]
    for peer in range(N_ROW):
        total = total + parts_ref[peer].astype(f32)
    out_ref[0] = total.astype(bf16)


def add_head(parts, head, band):
    return pl.pallas_call(
        head_body,
        grid=(1,),
        out_shape=jax.ShapeDtypeStruct((N_COL, 2, RHS, TILE), bf16),
        in_specs=[
            pl.BlockSpec((N_ROW, 2, RHS, TILE), lambda i: (0, 0, 0, 0)),
            pl.BlockSpec((2, RHS, TILE), lambda i: (0, 0, 0)),
            ANY,
        ],
        out_specs=pl.BlockSpec((1, 2, RHS, TILE), lambda i: (0, 0, 0, 0)),
        input_output_aliases={2: 0},
        compiler_params=pltpu.CompilerParams(vmem_limit_bytes=6 * MIB),
        name="add_head",
    )(parts, head, band)


def update_body(last, parts_ref, trace_ref, load_ref, *outs):
    for half in range(2):
        lanes = slice(half * TILE, (half + 1) * TILE)
        total = parts_ref[0, half].astype(f32)
        for peer in range(1, N_COL):
            total = total + parts_ref[peer, half].astype(f32)
        trace = trace_ref[:, lanes]
        trace = trace + COUPLING_STEP * (load_ref[:, lanes] - trace - total)
        outs[0][:, lanes] = trace
        if last:
            outs[1][:, lanes] = total
        else:
            rounded = trace.astype(bf16)
            for copy in range(N_COL):
                outs[1][copy, half] = rounded


def update(parts, traces, load, last):
    whole = jax.ShapeDtypeStruct(traces.shape, f32)
    return pl.pallas_call(
        functools.partial(update_body, last),
        out_shape=[whole, whole if last else jax.ShapeDtypeStruct(parts.shape, bf16)],
        in_specs=[VMEM, VMEM, VMEM],
        out_specs=[VMEM, VMEM],
        compiler_params=pltpu.CompilerParams(vmem_limit_bytes=8 * MIB),
        name="update_last" if last else "update_next",
    )(parts, traces, load)


def lookup(indices, table):
    levels = jnp.arange(table.shape[0], dtype=jnp.int32)
    return jnp.sum(jnp.where(indices[..., None] == levels, table, 0.0), axis=-1)


def volume_cells(coef_index, coef_table, vol_source, volume_line):
    indices = lax.dynamic_index_in_dim(coef_index, volume_line, 0, keepdims=False)
    source = lax.dynamic_index_in_dim(vol_source, volume_line, 0, keepdims=False)
    spare = ((0, 0), (0, 8 - LAYERS), (0, 0), (0, 0))
    cells = jnp.stack([lookup(indices, coef_table), source]).reshape(2, LAYERS, MID, LANES)
    cells = jnp.pad(cells, spare).transpose(2, 0, 1, 3)

    def ends(x):
        return jnp.concatenate([x[:, :LANES], x[:, -LANES:]], 1)

    high = ends(source).astype(bf16)
    low = (ends(source) - high.astype(f32)).astype(bf16)
    edges = [jnp.pad(e, ((0, 4), (0, 0))) for e in (ends(indices).astype(bf16), high, low)]
    return cells, jnp.pad(jnp.concatenate(edges, 0), ((0, 8), (0, 0)))


def local(
    trace_start, surface_load, panel_tiles, tile_list, surf_map, coef_index, coef_table, vol_source
):
    col_index = lax.axis_index("col")
    row_index = lax.axis_index("row")
    volume_line = jnp.maximum(col_index - DENSE_COLS, 0)
    is_volume = col_index >= DENSE_COLS
    volume_tile = volume_line * N_ROW + row_index
    tile_numbers = jnp.arange(surf_map.shape[0], dtype=jnp.int32)
    quarter = jnp.sum(jnp.where(surf_map == volume_tile, tile_numbers, 0)) % 4
    first = quarter * 8
    scal = jnp.stack(
        [
            is_volume.astype(jnp.int32),
            jnp.where(is_volume, first, 0),
            jnp.where(is_volume, first + 7, 1),
            first,
            row_index,
        ]
    ).astype(jnp.int32)
    traces = trace_start
    spread = spread_start(traces)
    cells, edges = volume_cells(coef_index, coef_table, vol_source, volume_line)
    panel = panel_tiles
    saved = None
    for iteration in range(ITERS):
        last = iteration == ITERS - 1
        band = exchange(spread, "col").reshape(BAND_TILES, RHS, TILE)
        row_spread = spread_row(scal, band, edges if iteration == 0 else None)
        win = exchange(row_spread, "row").reshape(WIN_TILES, RHS, TILE)
        win_part = into_window(tile_list, scal, band, panel)
        win_parts = exchange(win_part.reshape(N_ROW, 2, RHS, TILE), "row")
        made = into_rows(tile_list, scal, band, win, panel, coef_table, cells, saved)
        band_part, head = made[:2]
        saved = made[2:]
        band_part = add_head(win_parts, head, band_part.reshape(N_COL, 2, RHS, TILE))
        traces, spread = update(exchange(band_part, "col"), traces, surface_load, last)
    return (traces, spread)


def solution(mesh):
    return jax.shard_map(
        local,
        mesh=mesh,
        in_specs=(
            P(None, ("col", "row")),
            P(None, ("col", "row")),
            P(("col", "row"), None, None),
            P(("col", "row")),
            P(),
            P(None, None, "row"),
            P(),
            P(None, None, "row"),
        ),
        out_specs=(P(None, ("col", "row")), P(None, ("col", "row"))),
        check_vma=False,
    )
```

time: 217 us -> 164 us (0.76)
  blocking collectives: 105 us -> 58.7 us
  starting transfers between devices: 21.5 us -> 31.8 us
  waiting for transfers between devices: 23 us -> 13.5 us
  local copies, waits for them, and re-layouts: 11.2 us -> 7.69 us
  Pallas kernels: 49.1 us -> 46.5 us
    all_to_all x6 -> x3, blocking collectives: 105 us -> 58.7 us  [exchange(): return lax.all_to_all(x, axis, 0, 0, tiled=True)]
    all_to_all x2 -> x5, starting transfers between devices: 16.3 us -> 31.8 us  [exchange(): return lax.all_to_all(x, axis, 0, 0, tiled=True)]
    all_to_all x2 -> x5, waiting for transfers between devices: 23 us -> 13.5 us  [exchange(): return lax.all_to_all(x, axis, 0, 0, tiled=True)]
    pallas_call x4 -> x6, Pallas kernels: 38.9 us -> 44.2 us  [the longest x2 21.5 us: into_rows(): pl.pallas_call(functools.partial(rows_body, first_iteration), out_shape=o...]
    ppermute x2 -> x0, starting transfers between devices: 5.24 us -> none  [the longest x1 3.94 us: volume_weights(): before = lax.ppermute(both[:, -LANES:], 'row', up)]
    pallas_call x2, Pallas kernels: 4.69 us -> 1.05 us  [update(): pl.pallas_call(functools.partial(update_body, last), out_shape=[whole, wh...]
    pallas_call x2, Pallas kernels: 3.51 us -> 0.15 us  [add_head(): pl.pallas_call(head_body, grid=(1,), out_shape=jax.ShapeDtypeStruct((N_CO...]
    unnamed x28 -> x20, local copies, waits for them, and re-layouts: 9.47 us -> 6.72 us
  transfers between devices with their start and end apart: 4 -> 5, of which waited for: 2 -> 3; matrix products, arithmetic and copies ran while one was open for 1% -> 2% of each run, Pallas kernels for 1% -> 25%
where the time goes in v2:
time: 164 us; the launch traced here: 163 us
  blocking collectives  58.7 us (36%)
  Pallas kernels  46.5 us (28%)
  starting transfers between devices  31.8 us (19%)
  waiting for transfers between devices  13.5 us (8%)
  local copies, waits for them, and re-layouts  7.69 us (5%)
  between operations  2.77 us (2%)
  other arithmetic  2.52 us (2%)
    all_to_all x3, blocking collectives, exchange(): return lax.all_to_all(x, axis, 0, 0, tiled=True)  58.7 us
    all_to_all x5, starting transfers between devices, exchange(): return lax.all_to_all(x, axis, 0, 0, tiled=True)  31.8 us
    pallas_call x2, Pallas kernels, into_rows(): pl.pallas_call(functools.partial(rows_body, first_iteration), out_shape=o...  21.5 us
    pallas_call x2, Pallas kernels, into_window(): pl.pallas_call(window_body, out_shape=jax.ShapeDtypeStruct((WIN_TILES, RH...  19.9 us
    all_to_all x5, waiting for transfers between devices, exchange(): return lax.all_to_all(x, axis, 0, 0, tiled=True)  13.5 us
    unnamed x20, local copies, waits for them, and re-layouts  6.72 us
  transfers between devices with their start and end apart: 5, of which 3 were waited for; matrix products, arithmetic and copies ran while one was open for 2% of the time, Pallas kernels for 25%

profile of v2, /device:TPU:1, one launch (start us, length us, event | category | flops | bytes accessed | tf_op | source)
XLA Modules:
  0.0 163.4 jit_solution(14948143280740353836)
XLA Ops:
  0.6 0.9 copy-done.4
  1.5 1.1 spread_start.1
  2.6 7.3 %all-to-all-start = ((bf16[16,2,32,512]{3,2,1,0:T(8,128)(2,1)}), bf16[16,2,32,512]{3,2,1,0:T(8,128)(2,1)S(1)}, u32[]{:S(2)}, u32[]{:S(2)}) async-start(bf16[16,2,32,512]{3,2,1,0:T(8,128)(2,1)} %spread_start.1), calls=%async_computation | async-start | bytes 2097152 | tf_op jit(solution)/shard_map/all_to_all | solution.py:40
  10.0 1.3 fusion.10
  15.2 10.7 %all-to-all-done = bf16[16,2,32,512]{3,2,1,0:T(8,128)(2,1)S(1)} async-done(((bf16[16,2,32,512]{3,2,1,0:T(8,128)(2,1)}), bf16[16,2,32,512]{3,2,1,0:T(8,128)(2,1)S(1)}, u32[]{:S(2)}, u32[]{:S(2)}) %all-to-all-start) | async-done | bytes 1048608 | tf_op jit(solution)/shard_map/all_to_all | solution.py:40
  25.8 1.4 spread_row.2
  27.2 7.0 %all-to-all-start.2 = ((bf16[8,2,32,512]{3,2,1,0:T(8,128)(2,1)}), bf16[8,2,32,512]{3,2,1,0:T(8,128)(2,1)S(1)}, u32[]{:S(2)}, u32[]{:S(2)}) async-start(bf16[8,2,32,512]{3,2,1,0:T(8,128)(2,1)} %spread_row.2), calls=%async_computation.2 | async-start | bytes 1048576 | tf_op jit(solution)/shard_map/all_to_all | solution.py:40
  34.9 9.9 %into_window.2 = bf16[16,32,512]{2,1,0:T(8,128)(2,1)} custom-call(s32[43]{0:T(128)S(1)} %copy-done.7, s32[5]{0:T(128)S(1)} %stack.36.scal_ref, bf16[32,32,512]{2,1,0:T(8,128)(2,1)S(1)} %bitcast.27, bf16[43,512,512]{2,1,0:T(8,128)(2,1)} %panel_ref.7), custom_call_target="tpu_custom_call" | custom-call | flops 700000000 | bytes 25000000 | tf_op jit(solution)/shard_map/into_window/pallas_call | solution.py:138
  44.9 1.1 all-to-all-done.2
  45.9 5.6 %all-to-all-start.1 = ((bf16[8,2,32,512]{3,2,1,0:T(8,128)(2,1)}), bf16[8,2,32,512]{3,2,1,0:T(8,128)(2,1)S(1)}, u32[]{:S(2)}, u32[]{:S(2)}) async-start(bf16[8,2,32,512]{3,2,1,0:T(8,128)(2,1)} %bitcast.6), calls=%async_computation.1 | async-start | bytes 1048576 | tf_op jit(solution)/shard_map/all_to_all | solution.py:40
  51.9 10.8 %into_rows_first.1 = (bf16[32,32,512]{2,1,0:T(8,128)(2,1)S(1)}, f32[2,32,512]{2,1,0:T(8,128)S(1)}, f32[36,4,32,128]{3,2,1,0:T(8,128)S(1)}, f32[34,48,128]{2,1,0:T(8,128)S(1)}) custom-call(s32[43]{0:T(128)S(1)} %copy-done.8, s32[5]{0:T(128)S(1)} %stack.36.scal_ref, bf16[32,32,512]{2,1,0:T(8,128)(2,1)S(1)} %bitcast.28, bf16[16,32,512]{2,1,0:T(8,128)(2,1)S(1)} %bitcast.31, ...), custom_call_target="tpu_custom_call" | custom-call | flops 700000000 | bytes 30000000 | tf_op jit(solution)/shard_map/into_rows_first/pallas_call | solution.py:327
  62.7 1.4 copy-done
  64.1 0.9 copy-done.2
  65.1 19.6 %all_to_all.40.parts_ref = bf16[16,2,32,512]{3,2,1,0:T(8,128)(2,1)S(1)} all-to-all(bf16[16,2,32,512]{3,2,1,0:T(8,128)(2,1)S(1)} %add_head.2), channel_id=1, replica_groups=mesh['col'=16,'row'=8] {'col'}, dimensions={0} | all-to-all | bytes 2097152 | tf_op jit(solution)/shard_map/all_to_all | solution.py:40
  84.9 19.1 %all_to_all.41 = bf16[16,2,32,512]{3,2,1,0:T(8,128)(2,1)S(1)} all-to-all(bf16[16,2,32,512]{3,2,1,0:T(8,128)(2,1)S(1)} %get-tuple-element.12), channel_id=1, replica_groups=mesh['col'=16,'row'=8] {'col'}, dimensions={0} | all-to-all | bytes 2097152 | tf_op jit(solution)/shard_map/all_to_all | solution.py:40
  104.0 1.4 spread_row.3
  105.4 6.9 %all-to-all-start.6 = ((bf16[8,2,32,512]{3,2,1,0:T(8,128)(2,1)}), bf16[8,2,32,512]{3,2,1,0:T(8,128)(2,1)S(1)}, u32[]{:S(2)}, u32[]{:S(2)}) async-start(bf16[8,2,32,512]{3,2,1,0:T(8,128)(2,1)} %spread_row.3), calls=%async_computation.6 | async-start | bytes 1048576 | tf_op jit(solution)/shard_map/all_to_all | solution.py:40
  112.3 9.9 %into_window.3 = bf16[16,32,512]{2,1,0:T(8,128)(2,1)} custom-call(s32[43]{0:T(128)S(1)} %copy-done.8, s32[5]{0:T(128)S(1)} %stack.36.scal_ref, bf16[32,32,512]{2,1,0:T(8,128)(2,1)S(1)} %bitcast.24, bf16[43,512,512]{2,1,0:T(8,128)(2,1)} %panel_ref.7), custom_call_target="tpu_custom_call" | custom-call | flops 700000000 | bytes 25000000 | tf_op jit(solution)/shard_map/into_window/pallas_call | solution.py:138
  122.3 1.7 %all-to-all-done.6 = bf16[8,2,32,512]{3,2,1,0:T(8,128)(2,1)S(1)} async-done(((bf16[8,2,32,512]{3,2,1,0:T(8,128)(2,1)}), bf16[8,2,32,512]{3,2,1,0:T(8,128)(2,1)S(1)}, u32[]{:S(2)}, u32[]{:S(2)}) %all-to-all-start.6) | async-done | bytes 524320 | tf_op jit(solution)/shard_map/all_to_all | solution.py:40
  124.0 4.9 %all-to-all-start.5 = ((bf16[8,2,32,512]{3,2,1,0:T(8,128)(2,1)}), bf16[8,2,32,512]{3,2,1,0:T(8,128)(2,1)S(1)}, u32[]{:S(2)}, u32[]{:S(2)}) async-start(bf16[8,2,32,512]{3,2,1,0:T(8,128)(2,1)} %bitcast.15), calls=%async_computation.5 | async-start | bytes 1048576 | tf_op jit(solution)/shard_map/all_to_all | solution.py:40
  128.9 1.7 %copy-done.1 = f32[36,4,32,128]{3,2,1,0:T(8,128)S(1)} copy-done((f32[36,4,32,128]{3,2,1,0:T(8,128)S(1)}, f32[36,4,32,128]{3,2,1,0:T(8,128)}, u32[]{:S(2)}) %copy-start.1) | copy-done | bytes 2359320
  130.6 1.1 copy-done.3
  131.7 10.8 %into_rows_next.1 = (bf16[32,32,512]{2,1,0:T(8,128)(2,1)S(1)}, f32[2,32,512]{2,1,0:T(8,128)S(1)}) custom-call(s32[43]{0:T(128)S(1)} %copy-done.8, s32[5]{0:T(128)S(1)} %stack.36.scal_ref, bf16[32,32,512]{2,1,0:T(8,128)(2,1)S(1)} %bitcast.25, bf16[16,32,512]{2,1,0:T(8,128)(2,1)S(1)} %bitcast.32, bf16[43,512,512]{2,1,0:T(8,128)(2,1)} %panel_ref.7, ...), custom_call_target="tpu_custom_call" | custom-call | flops 700000000 | bytes 30000000 | tf_op jit(solution)/shard_map/into_rows_next/pallas_call | solution.py:327
  142.6 19.9 %all_to_all.42.parts_ref = bf16[16,2,32,512]{3,2,1,0:T(8,128)(2,1)S(1)} all-to-all(bf16[16,2,32,512]{3,2,1,0:T(8,128)(2,1)S(1)} %add_head.3), channel_id=1, replica_groups=mesh['col'=16,'row'=8] {'col'}, dimensions={0} | all-to-all | bytes 2097152 | tf_op jit(solution)/shard_map/all_to_all | solution.py:40
  (33 shorter events, 4.1 us)
Async XLA Ops:
  0.6 0.9 copy-start.4
  1.5 50.0 %copy-start.9 = (f32[16]{0:T(128)S(1)}, f32[16]{0:T(128)}, u32[]{:S(2)}) copy-start(f32[16]{0:T(128)} %refs_0_.1) | copy-start | bytes 196
  1.5 50.3 %copy-start.8 = (s32[43]{0:T(128)S(1)}, s32[43]{0:T(128)}, u32[]{:S(2)}) copy-start(s32[43]{0:T(128)} %ident_ref.7) | copy-start | bytes 520
  2.6 23.2 %all-to-all-start = ((bf16[16,2,32,512]{3,2,1,0:T(8,128)(2,1)}), bf16[16,2,32,512]{3,2,1,0:T(8,128)(2,1)S(1)}, u32[]{:S(2)}, u32[]{:S(2)}) async-start(bf16[16,2,32,512]{3,2,1,0:T(8,128)(2,1)} %spread_start.1), calls=%async_computation | async-start | bytes 2097152 | tf_op jit(solution)/shard_map/all_to_all | solution.py:40
  27.2 18.7 %all-to-all-start.2 = ((bf16[8,2,32,512]{3,2,1,0:T(8,128)(2,1)}), bf16[8,2,32,512]{3,2,1,0:T(8,128)(2,1)S(1)}, u32[]{:S(2)}, u32[]{:S(2)}) async-start(bf16[8,2,32,512]{3,2,1,0:T(8,128)(2,1)} %spread_row.2), calls=%async_computation.2 | async-start | bytes 1048576 | tf_op jit(solution)/shard_map/all_to_all | solution.py:40
  34.3 0.7 copy-start.7
  34.9 49.8 %copy-start.5 = (f32[32,1024]{1,0:T(8,128)S(1)}, f32[32,1024]{1,0:T(8,128)}, u32[]{:S(2)}) copy-start(f32[32,1024]{1,0:T(8,128)} %trace_ref.3) | copy-start | bytes 393220
  34.9 49.8 %copy-start.6 = (f32[32,1024]{1,0:T(8,128)S(1)}, f32[32,1024]{1,0:T(8,128)}, u32[]{:S(2)}) copy-start(f32[32,1024]{1,0:T(8,128)} %load_ref.3) | copy-start | bytes 393220
  45.9 19.1 %all-to-all-start.1 = ((bf16[8,2,32,512]{3,2,1,0:T(8,128)(2,1)}), bf16[8,2,32,512]{3,2,1,0:T(8,128)(2,1)S(1)}, u32[]{:S(2)}, u32[]{:S(2)}) async-start(bf16[8,2,32,512]{3,2,1,0:T(8,128)(2,1)} %bitcast.6), calls=%async_computation.1 | async-start | bytes 1048576 | tf_op jit(solution)/shard_map/all_to_all | solution.py:40
  62.7 1.4 copy-start
  64.1 0.9 copy-start.2
  105.4 18.6 %all-to-all-start.6 = ((bf16[8,2,32,512]{3,2,1,0:T(8,128)(2,1)}), bf16[8,2,32,512]{3,2,1,0:T(8,128)(2,1)S(1)}, u32[]{:S(2)}, u32[]{:S(2)}) async-start(bf16[8,2,32,512]{3,2,1,0:T(8,128)(2,1)} %spread_row.3), calls=%async_computation.6 | async-start | bytes 1048576 | tf_op jit(solution)/shard_map/all_to_all | solution.py:40
  124.0 18.5 %all-to-all-start.5 = ((bf16[8,2,32,512]{3,2,1,0:T(8,128)(2,1)}), bf16[8,2,32,512]{3,2,1,0:T(8,128)(2,1)S(1)}, u32[]{:S(2)}, u32[]{:S(2)}) async-start(bf16[8,2,32,512]{3,2,1,0:T(8,128)(2,1)} %bitcast.15), calls=%async_computation.5 | async-start | bytes 1048576 | tf_op jit(solution)/shard_map/all_to_all | solution.py:40
  128.9 1.7 %copy-start.1 = (f32[36,4,32,128]{3,2,1,0:T(8,128)S(1)}, f32[36,4,32,128]{3,2,1,0:T(8,128)}, u32[]{:S(2)}) copy-start(f32[36,4,32,128]{3,2,1,0:T(8,128)} %copy-done) | copy-start | bytes 7077892
  130.6 1.1 copy-start.3

commit v3 on v2

--- a/solution.py
+++ b/solution.py
@@ -22,6 +22,7 @@
 LAYERS = 4
 SLOTS = 43
 GROUP = 4
+UNROLL = 17
 COEFS = 16
 BAND_TILES = 32
 WIN_TILES = 16
@@ -34,6 +35,10 @@
 ANY = pl.BlockSpec(memory_space=pl.ANY)
 f32 = jnp.float32
 bf16 = jnp.bfloat16
+
+
+def in_hbm(x):
+    return pltpu.with_memory_space_constraint(x, pltpu.HBM)
 
 
 def exchange(x, axis):
@@ -64,11 +69,11 @@
 
 def row_body(first_iteration, scal_ref, band_ref, *refs):
     out_ref = refs[-1]
-    halves = [band_ref[scal_ref[1]], band_ref[scal_ref[2]]]
+    halves = [band_ref[scal_ref[SLOTS + 1]], band_ref[scal_ref[SLOTS + 2]]]
     put_everywhere(halves, out_ref, N_ROW)
     if first_iteration:
 
-        @pl.when(scal_ref[0] == 1)
+        @pl.when(scal_ref[SLOTS] == 1)
         def _():
             for peer in range(N_ROW):
                 out_ref[peer, 0, :, LANES : 3 * LANES] = refs[0][...]
@@ -87,7 +92,7 @@
     )(*args)
 
 
-def for_slots(ident_ref, panel_ref, buffer_ref, sems, do_slot):
+def for_slots(scal_ref, panel_ref, buffer_ref, sems, acc_ref, do_slot):
     def fetch(slot):
         return pltpu.make_async_copy(panel_ref.at[slot], buffer_ref.at[slot], sems.at[slot])
 
@@ -96,9 +101,10 @@
         return carry
 
     lax.fori_loop(0, SLOTS, start, 0)
+    acc_ref[...] = jnp.zeros_like(acc_ref)
 
     def place(slot):
-        ident = ident_ref[slot]
+        ident = scal_ref[slot]
         named = ident >= 0
         safe = jnp.maximum(ident, 0)
         row_tile = lax.shift_right_logical(safe, 8)
@@ -119,26 +125,30 @@
         place(slot)
 
 
-def window_body(ident_ref, scal_ref, band_ref, panel_ref, win_out, win_acc, buffer_ref, sems):
-    win_acc[...] = jnp.zeros_like(win_acc)
-
-    @pl.when(scal_ref[0] == 0)
+def window_body(scal_ref, band_ref, panel_ref, win_out, win_acc, buffer_ref, sems):
+    is_volume = scal_ref[SLOTS] == 1
+
+    @pl.when(jnp.logical_not(is_volume))
     def _():
         def one_slot(slot, named, band_tile, col_tile):
             win_acc[jnp.where(named, col_tile, WIN_TILES)] += jnp.dot(
                 band_ref[band_tile], buffer_ref[slot], preferred_element_type=f32
             )
 
-        for_slots(ident_ref, panel_ref, buffer_ref, sems, one_slot)
-
-    win_out[...] = win_acc[:WIN_TILES].astype(bf16)
-
-
-def into_window(ident, scal, band, panel):
+        for_slots(scal_ref, panel_ref, buffer_ref, sems, win_acc, one_slot)
+
+        win_out[...] = win_acc[:WIN_TILES].astype(bf16)
+
+    @pl.when(is_volume)
+    def _():
+        win_out[...] = jnp.zeros_like(win_out)
+
+
+def into_window(scal, band, panel):
     return pl.pallas_call(
         window_body,
         out_shape=jax.ShapeDtypeStruct((WIN_TILES, RHS, TILE), bf16),
-        in_specs=[SMEM, SMEM, VMEM, ANY],
+        in_specs=[SMEM, VMEM, ANY],
         out_specs=VMEM,
         scratch_shapes=[
             pltpu.VMEM((WIN_TILES + 1, RHS, TILE), f32),
@@ -148,11 +158,11 @@
         compiler_params=pltpu.CompilerParams(vmem_limit_bytes=44 * MIB),
         cost_estimate=pl.CostEstimate(flops=7 * 10**8, transcendentals=0, bytes_accessed=25 * 10**6),
         name="into_window",
-    )(ident, scal, band, panel)
+    )(scal, band, panel)
 
 
 def weigh(scal_ref, table_ref, cells_ref, win_ref, cell_ref, coef_ref):
-    row = scal_ref[4]
+    row = scal_ref[SLOTS + 4]
     before = jnp.maximum(row - 1, 0)
     after = jnp.minimum(row + 1, N_ROW - 1)
     layer = lax.broadcasted_iota(jnp.int32, (8, LANES), 0)
@@ -196,15 +206,16 @@
 
 
 def relax(scal_ref, band_ref, win_ref, coef_ref, states, top_ref):
-    first = scal_ref[3]
-    row = scal_ref[4]
+    first = scal_ref[SLOTS + 3]
+    row = scal_ref[SLOTS + 4]
     before = jnp.maximum(row - 1, 0)
     after = jnp.minimum(row + 1, N_ROW - 1)
     top_ref[0] = win_ref[2 * before + 1, :, TILE - LANES :].astype(f32)
     top_ref[EXT - 1] = win_ref[2 * after, :, :LANES].astype(f32)
     for chunk in range(MID):
         start = chunk % 4 * LANES
-        top_ref[chunk + 1] = band_ref[first + chunk // 4, :, start : start + LANES].astype(f32)
+        top = band_ref[first + chunk // 4, :, start : start + LANES]
+        top_ref[chunk + 1] = top.astype(f32)
     lane = lax.broadcasted_iota(jnp.int32, (RHS, LANES), 1)
     is_first = lane == 0
     is_last = lane == LANES - 1
@@ -218,7 +229,7 @@
                 right = pltpu.roll(jnp.where(is_first, source_ref[chunk + 2, l], centre), LANES - 1, 1)
                 value = (
                     (1.0 - JACOBI_WEIGHT) * centre
-                    + coef_ref[chunk, l : l + 1, :] * left
+                    + coef_ref[chunk, l : 1 + l, :] * left
                     + coef_ref[chunk, 8 + l : 9 + l, :] * right
                     + coef_ref[chunk, 16 + l : 17 + l, :] * upper
                     + coef_ref[chunk, 32 + l : 33 + l, :]
@@ -230,13 +241,13 @@
                 target_ref[chunk + 1, l] = value
             return carry
 
-        lax.fori_loop(0, EXT, one_chunk, 0, unroll=2)
+        lax.fori_loop(0, EXT, one_chunk, 0, unroll=UNROLL)
 
     for step in range(SWEEPS):
         sweep(states[step % 2], states[1 - step % 2])
 
 
-def rows_body(first_iteration, ident_ref, scal_ref, band_ref, win_ref, panel_ref, *refs):
+def rows_body(first_iteration, scal_ref, band_ref, win_ref, panel_ref, *refs):
     if first_iteration:
         table_ref, cells_ref, band_out, head_out, state_out, coef_out = refs[:6]
         refs = refs[6:]
@@ -244,12 +255,10 @@
         state_in, coef_in, band_out, head_out = refs[:4]
         refs = refs[4:]
     band_acc, state_a, state_b, coef_ref, cell_ref, top_ref, sems, buffer_ref, panel_sems = refs
-    is_volume = scal_ref[0] == 1
+    is_volume = scal_ref[SLOTS] == 1
 
     @pl.when(jnp.logical_not(is_volume))
     def _():
-        band_acc[...] = jnp.zeros_like(band_acc)
-
         def one_slot(slot, named, band_tile, col_tile):
             band_acc[jnp.where(named, band_tile, BAND_TILES)] += lax.dot_general(
                 win_ref[col_tile],
@@ -258,7 +267,7 @@
                 preferred_element_type=f32,
             )
 
-        for_slots(ident_ref, panel_ref, buffer_ref, panel_sems, one_slot)
+        for_slots(scal_ref, panel_ref, buffer_ref, panel_sems, band_acc, one_slot)
         band_out[...] = band_acc[:BAND_TILES].astype(bf16)
         head_out[...] = band_acc[:2]
 
@@ -289,10 +298,11 @@
                 save.start()
         band_out[...] = jnp.zeros_like(band_out)
         head_out[...] = jnp.zeros_like(head_out)
-        first = scal_ref[3]
+        first = scal_ref[SLOTS + 3]
         for chunk in range(MID):
             start = chunk % 4 * LANES
-            flux = coef_ref[chunk + 1, 40:41, :] * (top_ref[chunk + 1] - state_a[chunk + 2, 0])
+            flux = (top_ref[chunk + 1] - state_a[chunk + 2, 0])
+            flux = coef_ref[chunk + 1, 40:41, :] * flux
             band_out[first + chunk // 4, :, start : start + LANES] = flux.astype(bf16)
             if chunk < 8:
 
@@ -305,25 +315,25 @@
                 save.wait()
 
 
-def into_rows(ident, scal, band, win, panel, table, cells, saved):
+def into_rows(scal, band, win, panel, table, cells, saved):
     first_iteration = saved is None
     outs = [
         jax.ShapeDtypeStruct((BAND_TILES, RHS, TILE), bf16),
         jax.ShapeDtypeStruct((2, RHS, TILE), f32),
     ]
     out_specs = [VMEM, VMEM]
-    in_specs = [SMEM, SMEM, VMEM, VMEM, ANY]
-    args = [ident, scal, band, win, panel]
+    in_specs = [SMEM, VMEM, VMEM, ANY]
+    args = [scal, band, win, panel]
     state = (EXT + 2, LAYERS, RHS, LANES)
     coefs = (EXT, 48, LANES)
     if first_iteration:
-        outs += [jax.ShapeDtypeStruct(state, f32), jax.ShapeDtypeStruct(coefs, f32)]
+        outs += [pltpu.HBM(state, f32), pltpu.HBM(coefs, f32)]
         out_specs += [ANY, ANY]
         in_specs += [SMEM, VMEM]
         args += [table, cells]
     else:
         in_specs += [ANY, ANY]
-        args += saved
+        args += [in_hbm(x) for x in saved]
     return pl.pallas_call(
         functools.partial(rows_body, first_iteration),
         out_shape=outs,
@@ -431,28 +441,21 @@
     tile_numbers = jnp.arange(surf_map.shape[0], dtype=jnp.int32)
     quarter = jnp.sum(jnp.where(surf_map == volume_tile, tile_numbers, 0)) % 4
     first = quarter * 8
-    scal = jnp.stack(
-        [
-            is_volume.astype(jnp.int32),
-            jnp.where(is_volume, first, 0),
-            jnp.where(is_volume, first + 7, 1),
-            first,
-            row_index,
-        ]
-    ).astype(jnp.int32)
+    own = [is_volume, jnp.where(is_volume, first, 0), jnp.where(is_volume, first + 7, 1), first, row_index]
+    scal = jnp.concatenate([tile_list, jnp.stack([x.astype(jnp.int32) for x in own])])
     traces = trace_start
     spread = spread_start(traces)
     cells, edges = volume_cells(coef_index, coef_table, vol_source, volume_line)
-    panel = panel_tiles
+    panel = in_hbm(panel_tiles)
     saved = None
     for iteration in range(ITERS):
         last = iteration == ITERS - 1
         band = exchange(spread, "col").reshape(BAND_TILES, RHS, TILE)
         row_spread = spread_row(scal, band, edges if iteration == 0 else None)
         win = exchange(row_spread, "row").reshape(WIN_TILES, RHS, TILE)
-        win_part = into_window(tile_list, scal, band, panel)
+        win_part = into_window(scal, band, panel)
         win_parts = exchange(win_part.reshape(N_ROW, 2, RHS, TILE), "row")
-        made = into_rows(tile_list, scal, band, win, panel, coef_table, cells, saved)
+        made = into_rows(scal, band, win, panel, coef_table, cells, saved)
         band_part, head = made[:2]
         saved = made[2:]
         band_part = add_head(win_parts, head, band_part.reshape(N_COL, 2, RHS, TILE))

time: 164 us -> 158 us (0.963)
  local copies, waits for them, and re-layouts: 7.69 us -> 2.53 us
    unnamed x20 -> x8, local copies, waits for them, and re-layouts: 6.72 us -> 0.91 us
  transfers between devices with their start and end apart: 5 -> 5, of which waited for: 3 -> 5; matrix products, arithmetic and copies ran while one was open for 2% -> 3% of each run, Pallas kernels for 25% -> 26%
where the time goes in v3:
time: 158 us; the launch traced here: 157 us
  blocking collectives  57.7 us (37%)
  Pallas kernels  46 us (29%)
  starting transfers between devices  31 us (20%)
  waiting for transfers between devices  14.6 us (9%)
  between operations  2.74 us (2%)
  local copies, waits for them, and re-layouts  2.53 us (2%)
  other arithmetic  2.52 us (2%)
    all_to_all x3, blocking collectives, exchange(): return lax.all_to_all(x, axis, 0, 0, tiled=True)  57.7 us
    all_to_all x5, starting transfers between devices, exchange(): return lax.all_to_all(x, axis, 0, 0, tiled=True)  31 us
    pallas_call x2, Pallas kernels, into_rows(): pl.pallas_call(functools.partial(rows_body, first_iteration), out_shape=o...  21.2 us
    pallas_call x2, Pallas kernels, into_window(): pl.pallas_call(window_body, out_shape=jax.ShapeDtypeStruct((WIN_TILES, RH...  19.7 us
    all_to_all x5, waiting for transfers between devices, exchange(): return lax.all_to_all(x, axis, 0, 0, tiled=True)  14.6 us
  transfers between devices with their start and end apart: 5, of which 5 were waited for; matrix products, arithmetic and copies ran while one was open for 3% of the time, Pallas kernels for 26%

profile of v3, /device:TPU:1, one launch (start us, length us, event | category | flops | bytes accessed | tf_op | source)
XLA Modules:
  0.0 157.1 jit_solution(15836278818172519182)
XLA Ops:
  0.6 0.9 copy-done
  1.5 1.1 spread_start.1
  2.6 7.3 %all-to-all-start = ((bf16[16,2,32,512]{3,2,1,0:T(8,128)(2,1)}), bf16[16,2,32,512]{3,2,1,0:T(8,128)(2,1)S(1)}, u32[]{:S(2)}, u32[]{:S(2)}) async-start(bf16[16,2,32,512]{3,2,1,0:T(8,128)(2,1)} %spread_start.1), calls=%async_computation | async-start | bytes 2097152 | tf_op jit(solution)/shard_map/all_to_all | solution.py:45
  10.0 1.3 fusion.10
  13.2 0.9 dynamic-slice_bitcast_fusion.1
  14.1 0.9 fusion.11
  15.1 0.7 concatenate.15.scal_ref
  15.8 10.0 %all-to-all-done = bf16[16,2,32,512]{3,2,1,0:T(8,128)(2,1)S(1)} async-done(((bf16[16,2,32,512]{3,2,1,0:T(8,128)(2,1)}), bf16[16,2,32,512]{3,2,1,0:T(8,128)(2,1)S(1)}, u32[]{:S(2)}, u32[]{:S(2)}) %all-to-all-start) | async-done | bytes 1048608 | tf_op jit(solution)/shard_map/all_to_all | solution.py:45
  25.8 1.4 spread_row.2
  27.2 7.0 %all-to-all-start.2 = ((bf16[8,2,32,512]{3,2,1,0:T(8,128)(2,1)}), bf16[8,2,32,512]{3,2,1,0:T(8,128)(2,1)S(1)}, u32[]{:S(2)}, u32[]{:S(2)}) async-start(bf16[8,2,32,512]{3,2,1,0:T(8,128)(2,1)} %spread_row.2), calls=%async_computation.2 | async-start | bytes 1048576 | tf_op jit(solution)/shard_map/all_to_all | solution.py:45
  34.2 9.9 %into_window.2 = bf16[16,32,512]{2,1,0:T(8,128)(2,1)} custom-call(s32[48]{0:T(128)S(1)} %concatenate.15.scal_ref, bf16[32,32,512]{2,1,0:T(8,128)(2,1)S(1)} %bitcast.24, bf16[43,512,512]{2,1,0:T(8,128)(2,1)} %panel_ref.7), custom_call_target="tpu_custom_call" | custom-call | flops 700000000 | bytes 25000000 | tf_op jit(solution)/shard_map/into_window/pallas_call | solution.py:148
  44.1 1.8 %all-to-all-done.2 = bf16[8,2,32,512]{3,2,1,0:T(8,128)(2,1)S(1)} async-done(((bf16[8,2,32,512]{3,2,1,0:T(8,128)(2,1)}), bf16[8,2,32,512]{3,2,1,0:T(8,128)(2,1)S(1)}, u32[]{:S(2)}, u32[]{:S(2)}) %all-to-all-start.2) | async-done | bytes 524320 | tf_op jit(solution)/shard_map/all_to_all | solution.py:45
  45.9 4.9 %all-to-all-start.1 = ((bf16[8,2,32,512]{3,2,1,0:T(8,128)(2,1)}), bf16[8,2,32,512]{3,2,1,0:T(8,128)(2,1)S(1)}, u32[]{:S(2)}, u32[]{:S(2)}) async-start(bf16[8,2,32,512]{3,2,1,0:T(8,128)(2,1)} %bitcast.6), calls=%async_computation.1 | async-start | bytes 1048576 | tf_op jit(solution)/shard_map/all_to_all | solution.py:45
  51.1 10.6 %into_rows_first.1 = (bf16[32,32,512]{2,1,0:T(8,128)(2,1)S(1)}, f32[2,32,512]{2,1,0:T(8,128)S(1)}, f32[36,4,32,128]{3,2,1,0:T(8,128)}, f32[34,48,128]{2,1,0:T(8,128)}) custom-call(s32[48]{0:T(128)S(1)} %concatenate.15.scal_ref, bf16[32,32,512]{2,1,0:T(8,128)(2,1)S(1)} %bitcast.25, bf16[16,32,512]{2,1,0:T(8,128)(2,1)S(1)} %bitcast.31, ...), custom_call_target="tpu_custom_call" | custom-call | flops 700000000 | bytes 30000000 | tf_op jit(solution)/shard_map/into_rows_first/pallas_call | solution.py:337
  62.3 19.1 %all_to_all.40.parts_ref = bf16[16,2,32,512]{3,2,1,0:T(8,128)(2,1)S(1)} all-to-all(bf16[16,2,32,512]{3,2,1,0:T(8,128)(2,1)S(1)} %add_head.2), channel_id=1, replica_groups=mesh['col'=16,'row'=8] {'col'}, dimensions={0} | all-to-all | bytes 2097152 | tf_op jit(solution)/shard_map/all_to_all | solution.py:45
  81.7 19.1 %all_to_all.41 = bf16[16,2,32,512]{3,2,1,0:T(8,128)(2,1)S(1)} all-to-all(bf16[16,2,32,512]{3,2,1,0:T(8,128)(2,1)S(1)} %get-tuple-element.12), channel_id=1, replica_groups=mesh['col'=16,'row'=8] {'col'}, dimensions={0} | all-to-all | bytes 2097152 | tf_op jit(solution)/shard_map/all_to_all | solution.py:45
  100.8 1.4 spread_row.3
  102.1 6.9 %all-to-all-start.6 = ((bf16[8,2,32,512]{3,2,1,0:T(8,128)(2,1)}), bf16[8,2,32,512]{3,2,1,0:T(8,128)(2,1)S(1)}, u32[]{:S(2)}, u32[]{:S(2)}) async-start(bf16[8,2,32,512]{3,2,1,0:T(8,128)(2,1)} %spread_row.3), calls=%async_computation.6 | async-start | bytes 1048576 | tf_op jit(solution)/shard_map/all_to_all | solution.py:45
  109.1 9.9 %into_window.3 = bf16[16,32,512]{2,1,0:T(8,128)(2,1)} custom-call(s32[48]{0:T(128)S(1)} %concatenate.15.scal_ref, bf16[32,32,512]{2,1,0:T(8,128)(2,1)S(1)} %bitcast.27, bf16[43,512,512]{2,1,0:T(8,128)(2,1)} %panel_ref.7), custom_call_target="tpu_custom_call" | custom-call | flops 700000000 | bytes 25000000 | tf_op jit(solution)/shard_map/into_window/pallas_call | solution.py:148
  118.9 1.8 %all-to-all-done.6 = bf16[8,2,32,512]{3,2,1,0:T(8,128)(2,1)S(1)} async-done(((bf16[8,2,32,512]{3,2,1,0:T(8,128)(2,1)}), bf16[8,2,32,512]{3,2,1,0:T(8,128)(2,1)S(1)}, u32[]{:S(2)}, u32[]{:S(2)}) %all-to-all-start.6) | async-done | bytes 524320 | tf_op jit(solution)/shard_map/all_to_all | solution.py:45
  120.8 4.9 %all-to-all-start.5 = ((bf16[8,2,32,512]{3,2,1,0:T(8,128)(2,1)}), bf16[8,2,32,512]{3,2,1,0:T(8,128)(2,1)S(1)}, u32[]{:S(2)}, u32[]{:S(2)}) async-start(bf16[8,2,32,512]{3,2,1,0:T(8,128)(2,1)} %bitcast.15), calls=%async_computation.5 | async-start | bytes 1048576 | tf_op jit(solution)/shard_map/all_to_all | solution.py:45
  125.6 10.6 %into_rows_next.1 = (bf16[32,32,512]{2,1,0:T(8,128)(2,1)S(1)}, f32[2,32,512]{2,1,0:T(8,128)S(1)}) custom-call(s32[48]{0:T(128)S(1)} %concatenate.15.scal_ref, bf16[32,32,512]{2,1,0:T(8,128)(2,1)S(1)} %bitcast.28, bf16[16,32,512]{2,1,0:T(8,128)(2,1)S(1)} %bitcast.32, bf16[43,512,512]{2,1,0:T(8,128)(2,1)} %panel_ref.7, ...), custom_call_target="tpu_custom_call" | custom-call | flops 700000000 | bytes 30000000 | tf_op jit(solution)/shard_map/into_rows_next/pallas_call | solution.py:337
  136.8 19.5 %all_to_all.42.parts_ref = bf16[16,2,32,512]{3,2,1,0:T(8,128)(2,1)S(1)} all-to-all(bf16[16,2,32,512]{3,2,1,0:T(8,128)(2,1)S(1)} %add_head.3), channel_id=1, replica_groups=mesh['col'=16,'row'=8] {'col'}, dimensions={0} | all-to-all | bytes 2097152 | tf_op jit(solution)/shard_map/all_to_all | solution.py:45
  156.3 0.9 update_last.1
  (21 shorter events, 1.7 us)
Async XLA Ops:
  0.6 0.9 copy-start
  1.5 49.2 %copy-start.3 = (f32[16]{0:T(128)S(1)}, f32[16]{0:T(128)}, u32[]{:S(2)}) copy-start(f32[16]{0:T(128)} %refs_0_.1) | copy-start | bytes 196
  2.6 23.2 %all-to-all-start = ((bf16[16,2,32,512]{3,2,1,0:T(8,128)(2,1)}), bf16[16,2,32,512]{3,2,1,0:T(8,128)(2,1)S(1)}, u32[]{:S(2)}, u32[]{:S(2)}) async-start(bf16[16,2,32,512]{3,2,1,0:T(8,128)(2,1)} %spread_start.1), calls=%async_computation | async-start | bytes 2097152 | tf_op jit(solution)/shard_map/all_to_all | solution.py:45
  27.2 18.7 %all-to-all-start.2 = ((bf16[8,2,32,512]{3,2,1,0:T(8,128)(2,1)}), bf16[8,2,32,512]{3,2,1,0:T(8,128)(2,1)S(1)}, u32[]{:S(2)}, u32[]{:S(2)}) async-start(bf16[8,2,32,512]{3,2,1,0:T(8,128)(2,1)} %spread_row.2), calls=%async_computation.2 | async-start | bytes 1048576 | tf_op jit(solution)/shard_map/all_to_all | solution.py:45
  34.2 47.2 %copy-start.1 = (f32[32,1024]{1,0:T(8,128)S(1)}, f32[32,1024]{1,0:T(8,128)}, u32[]{:S(2)}) copy-start(f32[32,1024]{1,0:T(8,128)} %trace_ref.3) | copy-start | bytes 393220
  34.2 47.2 %copy-start.2 = (f32[32,1024]{1,0:T(8,128)S(1)}, f32[32,1024]{1,0:T(8,128)}, u32[]{:S(2)}) copy-start(f32[32,1024]{1,0:T(8,128)} %load_ref.3) | copy-start | bytes 393220
  45.9 16.3 %all-to-all-start.1 = ((bf16[8,2,32,512]{3,2,1,0:T(8,128)(2,1)}), bf16[8,2,32,512]{3,2,1,0:T(8,128)(2,1)S(1)}, u32[]{:S(2)}, u32[]{:S(2)}) async-start(bf16[8,2,32,512]{3,2,1,0:T(8,128)(2,1)} %bitcast.6), calls=%async_computation.1 | async-start | bytes 1048576 | tf_op jit(solution)/shard_map/all_to_all | solution.py:45
  102.1 18.6 %all-to-all-start.6 = ((bf16[8,2,32,512]{3,2,1,0:T(8,128)(2,1)}), bf16[8,2,32,512]{3,2,1,0:T(8,128)(2,1)S(1)}, u32[]{:S(2)}, u32[]{:S(2)}) async-start(bf16[8,2,32,512]{3,2,1,0:T(8,128)(2,1)} %spread_row.3), calls=%async_computation.6 | async-start | bytes 1048576 | tf_op jit(solution)/shard_map/all_to_all | solution.py:45
  120.8 15.9 %all-to-all-start.5 = ((bf16[8,2,32,512]{3,2,1,0:T(8,128)(2,1)}), bf16[8,2,32,512]{3,2,1,0:T(8,128)(2,1)S(1)}, u32[]{:S(2)}, u32[]{:S(2)}) async-start(bf16[8,2,32,512]{3,2,1,0:T(8,128)(2,1)} %bitcast.15), calls=%async_computation.5 | async-start | bytes 1048576 | tf_op jit(solution)/shard_map/all_to_all | solution.py:45

commit v4 on v3

--- a/solution.py
+++ b/solution.py
@@ -18,6 +18,9 @@
 LANES = 128
 N_COL = 16
 N_ROW = 8
+CORES = 2
+CHIPS = N_COL // CORES
+TILES = 2 * CHIPS
 DENSE_COLS = 12
 LAYERS = 4
 SLOTS = 43
@@ -45,6 +48,19 @@
     return lax.all_to_all(x, axis, 0, 0, tiled=True)
 
 
+def between_chips(x):
+    groups = [list(range(core, N_COL, CORES)) for core in range(CORES)]
+    return lax.all_to_all(x, "col", 0, 0, axis_index_groups=groups, tiled=True)
+
+
+def from_mate(x):
+    return lax.ppermute(x, "col", [(i, i ^ 1) for i in range(N_COL)])
+
+
+def pick(near_ref, far_ref, is_far, index):
+    return jnp.where(is_far == 0, near_ref[index], far_ref[index])
+
+
 def put_everywhere(half_pair, out_ref, copies):
     for copy in range(copies):
         for half in range(2):
@@ -53,13 +69,13 @@
 
 def start_body(trace_ref, out_ref):
     halves = [trace_ref[:, h * TILE : (h + 1) * TILE].astype(bf16) for h in range(2)]
-    put_everywhere(halves, out_ref, N_COL)
+    put_everywhere(halves, out_ref, CHIPS)
 
 
 def spread_start(trace_start):
     return pl.pallas_call(
         start_body,
-        out_shape=jax.ShapeDtypeStruct((N_COL, 2, RHS, TILE), bf16),
+        out_shape=jax.ShapeDtypeStruct((CHIPS, 2, RHS, TILE), bf16),
         in_specs=[VMEM],
         out_specs=VMEM,
         compiler_params=pltpu.CompilerParams(vmem_limit_bytes=6 * MIB),
@@ -67,9 +83,13 @@
     )(trace_start)
 
 
-def row_body(first_iteration, scal_ref, band_ref, *refs):
+def row_body(first_iteration, scal_ref, near_ref, far_ref, *refs):
     out_ref = refs[-1]
-    halves = [band_ref[scal_ref[SLOTS + 1]], band_ref[scal_ref[SLOTS + 2]]]
+    core = scal_ref[SLOTS + 6]
+    halves = [
+        pick(near_ref, far_ref, core, scal_ref[SLOTS + 1]),
+        pick(near_ref, far_ref, scal_ref[SLOTS + 5], scal_ref[SLOTS + 2]),
+    ]
     put_everywhere(halves, out_ref, N_ROW)
     if first_iteration:
 
@@ -79,9 +99,9 @@
                 out_ref[peer, 0, :, LANES : 3 * LANES] = refs[0][...]
 
 
-def spread_row(scal, band, edges):
+def spread_row(scal, near, far, edges):
     first_iteration = edges is not None
-    args = [scal, band] + ([edges] if first_iteration else [])
+    args = [scal, near, far] + ([edges] if first_iteration else [])
     return pl.pallas_call(
         functools.partial(row_body, first_iteration),
         out_shape=jax.ShapeDtypeStruct((N_ROW, 2, RHS, TILE), bf16),
@@ -109,8 +129,8 @@
         safe = jnp.maximum(ident, 0)
         row_tile = lax.shift_right_logical(safe, 8)
         col_tile = jnp.bitwise_and(safe, 15)
-        band_tile = lax.shift_right_logical(row_tile, 4) * 2 + jnp.bitwise_and(row_tile, 1)
-        do_slot(slot, named, band_tile, col_tile)
+        shard = lax.shift_right_logical(row_tile, 4)
+        do_slot(slot, named, shard, jnp.bitwise_and(row_tile, 1), col_tile)
 
     def group(index, carry):
         for extra in range(GROUP):
@@ -125,14 +145,20 @@
         place(slot)
 
 
-def window_body(scal_ref, band_ref, panel_ref, win_out, win_acc, buffer_ref, sems):
+def window_body(scal_ref, near_ref, far_ref, panel_ref, win_out, win_acc, buffer_ref, sems):
     is_volume = scal_ref[SLOTS] == 1
 
     @pl.when(jnp.logical_not(is_volume))
     def _():
-        def one_slot(slot, named, band_tile, col_tile):
+        core = scal_ref[SLOTS + 6]
+
+        def one_slot(slot, named, shard, half, col_tile):
+            is_far = jnp.bitwise_xor(jnp.bitwise_and(shard, 1), core)
+            index = lax.shift_right_logical(shard, 1) * 2 + half
             win_acc[jnp.where(named, col_tile, WIN_TILES)] += jnp.dot(
-                band_ref[band_tile], buffer_ref[slot], preferred_element_type=f32
+                pick(near_ref, far_ref, is_far, index),
+                buffer_ref[slot],
+                preferred_element_type=f32,
             )
 
         for_slots(scal_ref, panel_ref, buffer_ref, sems, win_acc, one_slot)
@@ -144,11 +170,11 @@
         win_out[...] = jnp.zeros_like(win_out)
 
 
-def into_window(scal, band, panel):
+def into_window(scal, near, far, panel):
     return pl.pallas_call(
         window_body,
         out_shape=jax.ShapeDtypeStruct((WIN_TILES, RHS, TILE), bf16),
-        in_specs=[SMEM, VMEM, ANY],
+        in_specs=[SMEM, VMEM, VMEM, ANY],
         out_specs=VMEM,
         scratch_shapes=[
             pltpu.VMEM((WIN_TILES + 1, RHS, TILE), f32),
@@ -158,7 +184,7 @@
         compiler_params=pltpu.CompilerParams(vmem_limit_bytes=44 * MIB),
         cost_estimate=pl.CostEstimate(flops=7 * 10**8, transcendentals=0, bytes_accessed=25 * 10**6),
         name="into_window",
-    )(scal, band, panel)
+    )(scal, near, far, panel)
 
 
 def weigh(scal_ref, table_ref, cells_ref, win_ref, cell_ref, coef_ref):
@@ -205,17 +231,19 @@
     lax.fori_loop(0, EXT, one_chunk, 0, unroll=2)
 
 
-def relax(scal_ref, band_ref, win_ref, coef_ref, states, top_ref):
-    first = scal_ref[SLOTS + 3]
+def relax(scal_ref, near_ref, far_ref, win_ref, coef_ref, states, top_ref):
+    quarter = scal_ref[SLOTS + 3]
     row = scal_ref[SLOTS + 4]
+    core = scal_ref[SLOTS + 6]
     before = jnp.maximum(row - 1, 0)
     after = jnp.minimum(row + 1, N_ROW - 1)
     top_ref[0] = win_ref[2 * before + 1, :, TILE - LANES :].astype(f32)
     top_ref[EXT - 1] = win_ref[2 * after, :, :LANES].astype(f32)
-    for chunk in range(MID):
-        start = chunk % 4 * LANES
-        top = band_ref[first + chunk // 4, :, start : start + LANES]
-        top_ref[chunk + 1] = top.astype(f32)
+    for tile in range(8):
+        is_far = jnp.bitwise_xor(tile // 2 % 2, core)
+        tops = pick(near_ref, far_ref, is_far, 4 * quarter + tile // 4 * 2 + tile % 2)
+        for part in range(4):
+            top_ref[4 * tile + part + 1] = tops[:, part * LANES : (part + 1) * LANES].astype(f32)
     lane = lax.broadcasted_iota(jnp.int32, (RHS, LANES), 1)
     is_first = lane == 0
     is_last = lane == LANES - 1
@@ -247,20 +275,20 @@
         sweep(states[step % 2], states[1 - step % 2])
 
 
-def rows_body(first_iteration, scal_ref, band_ref, win_ref, panel_ref, *refs):
+def rows_body(first_iteration, scal_ref, near_ref, far_ref, win_ref, panel_ref, *refs):
     if first_iteration:
-        table_ref, cells_ref, band_out, head_out, state_out, coef_out = refs[:6]
-        refs = refs[6:]
+        table_ref, cells_ref, own_out, mate_out, head_out, state_out, coef_out = refs[:7]
+        refs = refs[7:]
     else:
-        state_in, coef_in, band_out, head_out = refs[:4]
-        refs = refs[4:]
+        state_in, coef_in, own_out, mate_out, head_out = refs[:5]
+        refs = refs[5:]
     band_acc, state_a, state_b, coef_ref, cell_ref, top_ref, sems, buffer_ref, panel_sems = refs
     is_volume = scal_ref[SLOTS] == 1
 
     @pl.when(jnp.logical_not(is_volume))
     def _():
-        def one_slot(slot, named, band_tile, col_tile):
-            band_acc[jnp.where(named, band_tile, BAND_TILES)] += lax.dot_general(
+        def one_slot(slot, named, shard, half, col_tile):
+            band_acc[jnp.where(named, 2 * shard + half, BAND_TILES)] += lax.dot_general(
                 win_ref[col_tile],
                 buffer_ref[slot],
                 (((1,), (1,)), ((), ())),
@@ -268,8 +296,6 @@
             )
 
         for_slots(scal_ref, panel_ref, buffer_ref, panel_sems, band_acc, one_slot)
-        band_out[...] = band_acc[:BAND_TILES].astype(bf16)
-        head_out[...] = band_acc[:2]
 
     @pl.when(is_volume)
     def _():
@@ -288,7 +314,7 @@
                 load.start()
             for load in loads:
                 load.wait()
-        relax(scal_ref, band_ref, win_ref, coef_ref, (state_a, state_b), top_ref)
+        relax(scal_ref, near_ref, far_ref, win_ref, coef_ref, (state_a, state_b), top_ref)
         if first_iteration:
             saves = [
                 pltpu.make_async_copy(state_a, state_out, sems.at[0]),
@@ -296,34 +322,34 @@
             ]
             for save in saves:
                 save.start()
-        band_out[...] = jnp.zeros_like(band_out)
-        head_out[...] = jnp.zeros_like(head_out)
-        first = scal_ref[SLOTS + 3]
+        band_acc[...] = jnp.zeros_like(band_acc)
+        first = 8 * scal_ref[SLOTS + 3]
         for chunk in range(MID):
             start = chunk % 4 * LANES
-            flux = (top_ref[chunk + 1] - state_a[chunk + 2, 0])
-            flux = coef_ref[chunk + 1, 40:41, :] * flux
-            band_out[first + chunk // 4, :, start : start + LANES] = flux.astype(bf16)
-            if chunk < 8:
-
-                @pl.when(first == 0)
-                def _():
-                    head_out[chunk // 4, :, start : start + LANES] = flux
+            flux = coef_ref[chunk + 1, 40:41, :] * (top_ref[chunk + 1] - state_a[chunk + 2, 0])
+            band_acc[first + chunk // 4, :, start : start + LANES] = flux
 
         if first_iteration:
             for save in saves:
                 save.wait()
 
-
-def into_rows(scal, band, win, panel, table, cells, saved):
+    core = scal_ref[SLOTS + 6]
+    for chip in range(CHIPS):
+        own_out[chip] = band_acc[pl.ds(4 * chip + 2 * core, 2)]
+        mate_out[chip] = band_acc[pl.ds(4 * chip + 2 - 2 * core, 2)].astype(bf16)
+    head_out[...] = band_acc[:2]
+
+
+def into_rows(scal, near, far, win, panel, table, cells, saved):
     first_iteration = saved is None
     outs = [
-        jax.ShapeDtypeStruct((BAND_TILES, RHS, TILE), bf16),
+        jax.ShapeDtypeStruct((CHIPS, 2, RHS, TILE), f32),
+        jax.ShapeDtypeStruct((CHIPS, 2, RHS, TILE), bf16),
         jax.ShapeDtypeStruct((2, RHS, TILE), f32),
     ]
-    out_specs = [VMEM, VMEM]
-    in_specs = [SMEM, VMEM, VMEM, ANY]
-    args = [scal, band, win, panel]
+    out_specs = [VMEM, VMEM, VMEM]
+    in_specs = [SMEM, VMEM, VMEM, VMEM, ANY]
+    args = [scal, near, far, win, panel]
     state = (EXT + 2, LAYERS, RHS, LANES)
     coefs = (EXT, 48, LANES)
     if first_iteration:
@@ -356,35 +382,54 @@
     )(*args)
 
 
-def head_body(parts_ref, head_ref, band_ref, out_ref):
-    total = head_ref[...]
-    for peer in range(N_ROW):
-        total = total + parts_ref[peer].astype(f32)
-    out_ref[0] = total.astype(bf16)
-
-
-def add_head(parts, head, band):
-    return pl.pallas_call(
-        head_body,
-        grid=(1,),
-        out_shape=jax.ShapeDtypeStruct((N_COL, 2, RHS, TILE), bf16),
-        in_specs=[
-            pl.BlockSpec((N_ROW, 2, RHS, TILE), lambda i: (0, 0, 0, 0)),
-            pl.BlockSpec((2, RHS, TILE), lambda i: (0, 0, 0)),
-            ANY,
-        ],
-        out_specs=pl.BlockSpec((1, 2, RHS, TILE), lambda i: (0, 0, 0, 0)),
-        input_output_aliases={2: 0},
+def mate_body(scal_ref, parts_ref, head_ref, mate_ref, out_ref):
+    out_ref[...] = mate_ref[...]
+
+    @pl.when(scal_ref[SLOTS + 6] == 1)
+    def _():
+        total = head_ref[...]
+        for peer in range(N_ROW):
+            total = total + parts_ref[peer].astype(f32)
+        out_ref[0] = total.astype(bf16)
+
+
+def for_mate(scal, parts, head, mate):
+    return pl.pallas_call(
+        mate_body,
+        out_shape=jax.ShapeDtypeStruct(mate.shape, bf16),
+        in_specs=[SMEM, VMEM, VMEM, VMEM],
+        out_specs=VMEM,
         compiler_params=pltpu.CompilerParams(vmem_limit_bytes=6 * MIB),
-        name="add_head",
-    )(parts, head, band)
+        name="for_mate",
+    )(scal, parts, head, mate)
+
+
+def pair_body(scal_ref, parts_ref, own_ref, got_ref, out_ref):
+    for chip in range(1, CHIPS):
+        out_ref[chip] = (own_ref[chip] + got_ref[chip].astype(f32)).astype(bf16)
+    total = own_ref[0] + got_ref[0].astype(f32)
+    share = parts_ref[0].astype(f32)
+    for peer in range(1, N_ROW):
+        share = share + parts_ref[peer].astype(f32)
+    out_ref[0] = (total + jnp.where(scal_ref[SLOTS + 6] == 0, share, 0.0)).astype(bf16)
+
+
+def pair_sum(scal, parts, own, got):
+    return pl.pallas_call(
+        pair_body,
+        out_shape=jax.ShapeDtypeStruct(got.shape, bf16),
+        in_specs=[SMEM, VMEM, VMEM, VMEM],
+        out_specs=VMEM,
+        compiler_params=pltpu.CompilerParams(vmem_limit_bytes=6 * MIB),
+        name="pair_sum",
+    )(scal, parts, own, got)
 
 
 def update_body(last, parts_ref, trace_ref, load_ref, *outs):
     for half in range(2):
         lanes = slice(half * TILE, (half + 1) * TILE)
         total = parts_ref[0, half].astype(f32)
-        for peer in range(1, N_COL):
+        for peer in range(1, CHIPS):
             total = total + parts_ref[peer, half].astype(f32)
         trace = trace_ref[:, lanes]
         trace = trace + COUPLING_STEP * (load_ref[:, lanes] - trace - total)
@@ -393,7 +438,7 @@
             outs[1][:, lanes] = total
         else:
             rounded = trace.astype(bf16)
-            for copy in range(N_COL):
+            for copy in range(CHIPS):
                 outs[1][copy, half] = rounded
 
 
@@ -440,8 +485,16 @@
     volume_tile = volume_line * N_ROW + row_index
     tile_numbers = jnp.arange(surf_map.shape[0], dtype=jnp.int32)
     quarter = jnp.sum(jnp.where(surf_map == volume_tile, tile_numbers, 0)) % 4
-    first = quarter * 8
-    own = [is_volume, jnp.where(is_volume, first, 0), jnp.where(is_volume, first + 7, 1), first, row_index]
+    core = col_index % CORES
+    own = [
+        is_volume,
+        jnp.where(is_volume, 4 * quarter, 0),
+        jnp.where(is_volume, 4 * quarter + 3, 1),
+        quarter,
+        row_index,
+        jnp.where(is_volume, 1 - core, core),
+        core,
+    ]
     scal = jnp.concatenate([tile_list, jnp.stack([x.astype(jnp.int32) for x in own])])
     traces = trace_start
     spread = spread_start(traces)
@@ -450,16 +503,19 @@
     saved = None
     for iteration in range(ITERS):
         last = iteration == ITERS - 1
-        band = exchange(spread, "col").reshape(BAND_TILES, RHS, TILE)
-        row_spread = spread_row(scal, band, edges if iteration == 0 else None)
+        near = between_chips(spread)
+        far = from_mate(near)
+        near, far = near.reshape(TILES, RHS, TILE), far.reshape(TILES, RHS, TILE)
+        row_spread = spread_row(scal, near, far, edges if iteration == 0 else None)
         win = exchange(row_spread, "row").reshape(WIN_TILES, RHS, TILE)
-        win_part = into_window(scal, band, panel)
-        win_parts = exchange(win_part.reshape(N_ROW, 2, RHS, TILE), "row")
-        made = into_rows(scal, band, win, panel, coef_table, cells, saved)
-        band_part, head = made[:2]
-        saved = made[2:]
-        band_part = add_head(win_parts, head, band_part.reshape(N_COL, 2, RHS, TILE))
-        traces, spread = update(exchange(band_part, "col"), traces, surface_load, last)
+        win_part = into_window(scal, near, far, panel)
+        parts = exchange(win_part.reshape(N_ROW, 2, RHS, TILE), "row")
+        own, mate, head, *saved = into_rows(
+            scal, near, far, win, panel, coef_table, cells, saved
+        )
+        got = from_mate(for_mate(scal, parts, head, mate))
+        summed = between_chips(pair_sum(scal, parts, own, got))
+        traces, spread = update(summed, traces, surface_load, last)
     return (traces, spread)
 
 

time: 158 us -> 147 us (0.930)
  blocking collectives: 57.7 us -> 36.9 us
  starting transfers between devices: 31 us -> 34.9 us
  local copies, waits for them, and re-layouts: 2.53 us -> 6.17 us
  Pallas kernels: 46 us -> 48.3 us
    all_to_all x3, blocking collectives: 57.7 us -> 36.9 us  [between_chips(): return lax.all_to_all(x, 'col', 0, 0, axis_index_groups=groups, tiled=True)]
    all_to_all x5 -> x4, waiting for transfers between devices: 14.6 us -> 3.87 us  [exchange(): return lax.all_to_all(x, axis, 0, 0, tiled=True)]
    all_to_all x5 -> x4, starting transfers between devices: 31 us -> 23.6 us  [exchange(): return lax.all_to_all(x, axis, 0, 0, tiled=True)]
    all_to_all x0 -> x1, starting transfers between devices: none -> 6.37 us  [between_chips(): return lax.all_to_all(x, 'col', 0, 0, axis_index_groups=groups, tiled=True)]
    ppermute x0 -> x4, waiting for transfers between devices: none -> 5.35 us  [from_mate(): return lax.ppermute(x, 'col', [(i, i ^ 1) for i in range(N_COL)])]
    all_to_all x0 -> x1, waiting for transfers between devices: none -> 5.18 us  [between_chips(): return lax.all_to_all(x, 'col', 0, 0, axis_index_groups=groups, tiled=True)]
    ppermute x0 -> x4, starting transfers between devices: none -> 4.95 us  [from_mate(): return lax.ppermute(x, 'col', [(i, i ^ 1) for i in range(N_COL)])]
    unnamed x8 -> x16, local copies, waits for them, and re-layouts: 0.91 us -> 4.56 us
  transfers between devices with their start and end apart: 5 -> 9, of which waited for: 5 -> 8; matrix products, arithmetic and copies ran while one was open for 3% -> 3% of each run, Pallas kernels for 26% -> 28%
where the time goes in v4:
time: 147 us; the launch traced here: 146 us
  Pallas kernels  48.3 us (33%)
  blocking collectives  36.9 us (25%)
  starting transfers between devices  34.9 us (24%)
  waiting for transfers between devices  14.4 us (10%)
  local copies, waits for them, and re-layouts  6.17 us (4%)
  between operations  2.77 us (2%)
  other arithmetic  2.52 us (2%)
    all_to_all x3, blocking collectives, between_chips(): return lax.all_to_all(x, 'col', 0, 0, axis_index_groups=groups, tiled=True)  36.9 us
    all_to_all x4, starting transfers between devices, exchange(): return lax.all_to_all(x, axis, 0, 0, tiled=True)  23.6 us
    pallas_call x2, Pallas kernels, into_rows(): pl.pallas_call(functools.partial(rows_body, first_iteration), out_shape=o...  21.4 us
    pallas_call x2, Pallas kernels, into_window(): pl.pallas_call(window_body, out_shape=jax.ShapeDtypeStruct((WIN_TILES, RH...  19.7 us
    all_to_all x1, starting transfers between devices, between_chips(): return lax.all_to_all(x, 'col', 0, 0, axis_index_groups=groups, tiled=True)  6.37 us
    ppermute x4, waiting for transfers between devices, from_mate(): return lax.ppermute(x, 'col', [(i, i ^ 1) for i in range(N_COL)])  5.35 us
    all_to_all x1, waiting for transfers between devices, between_chips(): return lax.all_to_all(x, 'col', 0, 0, axis_index_groups=groups, tiled=True)  5.18 us
    ppermute x4, starting transfers between devices, from_mate(): return lax.ppermute(x, 'col', [(i, i ^ 1) for i in range(N_COL)])  4.95 us
  transfers between devices with their start and end apart: 9, of which 8 were waited for; matrix products, arithmetic and copies ran while one was open for 3% of the time, Pallas kernels for 28%

profile of v4, /device:TPU:1, one launch (start us, length us, event | category | flops | bytes accessed | tf_op | source)
XLA Modules:
  0.0 146.0 jit_solution(11530233802041434903)
XLA Ops:
  2.4 6.4 %all-to-all-start = ((bf16[8,2,32,512]{3,2,1,0:T(8,128)(2,1)}), bf16[8,2,32,512]{3,2,1,0:T(8,128)(2,1)S(1)}, u32[]{:S(2)}, u32[]{:S(2)}) async-start(bf16[8,2,32,512]{3,2,1,0:T(8,128)(2,1)} %spread_start.1), calls=%async_computation | async-start | bytes 1048576 | tf_op jit(solution)/shard_map/all_to_all | solution.py:53
  9.6 1.3 fusion.10
  13.8 5.2 %all-to-all-done = bf16[8,2,32,512]{3,2,1,0:T(8,128)(2,1)S(1)} async-done(((bf16[8,2,32,512]{3,2,1,0:T(8,128)(2,1)}), bf16[8,2,32,512]{3,2,1,0:T(8,128)(2,1)S(1)}, u32[]{:S(2)}, u32[]{:S(2)}) %all-to-all-start) | async-done | bytes 524320 | tf_op jit(solution)/shard_map/all_to_all | solution.py:53
  21.3 1.4 spread_row.2
  22.7 7.0 %all-to-all-start.2 = ((bf16[8,2,32,512]{3,2,1,0:T(8,128)(2,1)}), bf16[8,2,32,512]{3,2,1,0:T(8,128)(2,1)S(1)}, u32[]{:S(2)}, u32[]{:S(2)}) async-start(bf16[8,2,32,512]{3,2,1,0:T(8,128)(2,1)} %spread_row.2), calls=%async_computation.2 | async-start | bytes 1048576 | tf_op jit(solution)/shard_map/all_to_all | solution.py:48
  29.8 9.9 %into_window.2 = bf16[16,32,512]{2,1,0:T(8,128)(2,1)} custom-call(s32[50]{0:T(128)S(1)} %concatenate.15.scal_ref, bf16[16,32,512]{2,1,0:T(8,128)(2,1)S(1)} %bitcast.26, bf16[16,32,512]{2,1,0:T(8,128)(2,1)S(1)} %bitcast.32, bf16[43,512,512]{2,1,0:T(8,128)(2,1)} %panel_ref.7), custom_call_target="tpu_custom_call" | custom-call | flops 700000000 | bytes 25000000 | tf_op jit(solution)/shard_map/into_window/pallas_call | solution.py:174
  39.7 1.8 %all-to-all-done.2 = bf16[8,2,32,512]{3,2,1,0:T(8,128)(2,1)S(1)} async-done(((bf16[8,2,32,512]{3,2,1,0:T(8,128)(2,1)}), bf16[8,2,32,512]{3,2,1,0:T(8,128)(2,1)S(1)}, u32[]{:S(2)}, u32[]{:S(2)}) %all-to-all-start.2) | async-done | bytes 524320 | tf_op jit(solution)/shard_map/all_to_all | solution.py:48
  41.5 4.8 %all-to-all-start.1 = ((bf16[8,2,32,512]{3,2,1,0:T(8,128)(2,1)}), bf16[8,2,32,512]{3,2,1,0:T(8,128)(2,1)S(1)}, u32[]{:S(2)}, u32[]{:S(2)}) async-start(bf16[8,2,32,512]{3,2,1,0:T(8,128)(2,1)} %bitcast.9), calls=%async_computation.1 | async-start | bytes 1048576 | tf_op jit(solution)/shard_map/all_to_all | solution.py:48
  46.7 10.6 %into_rows_first.1 = (f32[8,2,32,512]{3,2,1,0:T(8,128)S(1)}, bf16[8,2,32,512]{3,2,1,0:T(8,128)(2,1)S(1)}, f32[2,32,512]{2,1,0:T(8,128)S(1)}, f32[36,4,32,128]{3,2,1,0:T(8,128)}, f32[34,48,128]{2,1,0:T(8,128)}) custom-call(s32[50]{0:T(128)S(1)} %concatenate.15.scal_ref, bf16[16,32,512]{2,1,0:T(8,128)(2,1)S(1)} %bitcast.27, bf16[16,32,512]{2,1,0:T(8,128)(2,1)S(1)} %bitcast.33, ...), custom_call_target="tpu_custom_call" | custom-call | flops 700000000 | bytes 30000000 | tf_op jit(solution)/shard_map/into_rows_first/pallas_call | solution.py:363
  59.8 1.2 collective-permute-start.1
  61.0 1.5 %collective-permute-done.1.got_ref = bf16[8,2,32,512]{3,2,1,0:T(8,128)(2,1)S(1)} collective-permute-done((bf16[8,2,32,512]{3,2,1,0:T(8,128)(2,1)S(1)}, bf16[8,2,32,512]{3,2,1,0:T(8,128)(2,1)S(1)}, u32[]{:S(2)}, u32[]{:S(2)}) %collective-permute-start.1) | collective-permute-done | bytes 524320 | tf_op jit(solution)/shard_map/ppermute | solution.py:57
  63.2 12.6 %all_to_all.40.parts_ref = bf16[8,2,32,512]{3,2,1,0:T(8,128)(2,1)S(1)} all-to-all(bf16[8,2,32,512]{3,2,1,0:T(8,128)(2,1)S(1)} %pair_sum.2), channel_id=1, replica_groups={{0,16,32,48,64,80,96,112},{8,24,40,56,72,88,104,120},{1,17,33,49,65,81,..., dimensions={0} | all-to-all | bytes 1048576 | tf_op jit(solution)/shard_map/all_to_all | solution.py:53
  76.0 11.6 %all_to_all.41 = bf16[8,2,32,512]{3,2,1,0:T(8,128)(2,1)S(1)} all-to-all(bf16[8,2,32,512]{3,2,1,0:T(8,128)(2,1)S(1)} %get-tuple-element.15), channel_id=1, replica_groups={{0,16,32,48,64,80,96,112},{8,24,40,56,72,88,104,120},{1,17,33,49,65,81,..., dimensions={0} | all-to-all | bytes 1048576 | tf_op jit(solution)/shard_map/all_to_all | solution.py:53
  87.6 1.8 %collective-permute-start.2 = (bf16[8,2,32,512]{3,2,1,0:T(8,128)(2,1)S(1)}, bf16[8,2,32,512]{3,2,1,0:T(8,128)(2,1)S(1)}, u32[]{:S(2)}, u32[]{:S(2)}) collective-permute-start(bf16[8,2,32,512]{3,2,1,0:T(8,128)(2,1)S(1)} %all_to_all.41), channel_id=1, source_target_pairs={{0,8},{8,0},{16,24},{24,16},{32,40},{40,32},{48,56},{56,48},{64,72... | collective-permute-start | bytes 1572872 | tf_op jit(solution)/shard_map/ppermute | solution.py:57
  89.5 1.5 %collective-permute-done.2 = bf16[8,2,32,512]{3,2,1,0:T(8,128)(2,1)S(1)} collective-permute-done((bf16[8,2,32,512]{3,2,1,0:T(8,128)(2,1)S(1)}, bf16[8,2,32,512]{3,2,1,0:T(8,128)(2,1)S(1)}, u32[]{:S(2)}, u32[]{:S(2)}) %collective-permute-start.2) | collective-permute-done | bytes 524320 | tf_op jit(solution)/shard_map/ppermute | solution.py:57
  91.0 1.4 spread_row.3
  92.3 6.9 %all-to-all-start.6 = ((bf16[8,2,32,512]{3,2,1,0:T(8,128)(2,1)}), bf16[8,2,32,512]{3,2,1,0:T(8,128)(2,1)S(1)}, u32[]{:S(2)}, u32[]{:S(2)}) async-start(bf16[8,2,32,512]{3,2,1,0:T(8,128)(2,1)} %spread_row.3), calls=%async_computation.6 | async-start | bytes 1048576 | tf_op jit(solution)/shard_map/all_to_all | solution.py:48
  99.3 9.9 %into_window.3 = bf16[16,32,512]{2,1,0:T(8,128)(2,1)} custom-call(s32[50]{0:T(128)S(1)} %concatenate.15.scal_ref, bf16[16,32,512]{2,1,0:T(8,128)(2,1)S(1)} %bitcast.29, bf16[16,32,512]{2,1,0:T(8,128)(2,1)S(1)} %bitcast.35, bf16[43,512,512]{2,1,0:T(8,128)(2,1)} %panel_ref.7), custom_call_target="tpu_custom_call" | custom-call | flops 700000000 | bytes 25000000 | tf_op jit(solution)/shard_map/into_window/pallas_call | solution.py:174
  109.2 1.9 %all-to-all-done.6 = bf16[8,2,32,512]{3,2,1,0:T(8,128)(2,1)S(1)} async-done(((bf16[8,2,32,512]{3,2,1,0:T(8,128)(2,1)}), bf16[8,2,32,512]{3,2,1,0:T(8,128)(2,1)S(1)}, u32[]{:S(2)}, u32[]{:S(2)}) %all-to-all-start.6) | async-done | bytes 524320 | tf_op jit(solution)/shard_map/all_to_all | solution.py:48
  111.0 4.8 %all-to-all-start.5 = ((bf16[8,2,32,512]{3,2,1,0:T(8,128)(2,1)}), bf16[8,2,32,512]{3,2,1,0:T(8,128)(2,1)S(1)}, u32[]{:S(2)}, u32[]{:S(2)}) async-start(bf16[8,2,32,512]{3,2,1,0:T(8,128)(2,1)} %bitcast.18), calls=%async_computation.5 | async-start | bytes 1048576 | tf_op jit(solution)/shard_map/all_to_all | solution.py:48
  115.8 10.7 %into_rows_next.1 = (f32[8,2,32,512]{3,2,1,0:T(8,128)S(1)}, bf16[8,2,32,512]{3,2,1,0:T(8,128)(2,1)S(1)}, f32[2,32,512]{2,1,0:T(8,128)S(1)}) custom-call(s32[50]{0:T(128)S(1)} %concatenate.15.scal_ref, bf16[16,32,512]{2,1,0:T(8,128)(2,1)S(1)} %bitcast.30, bf16[16,32,512]{2,1,0:T(8,128)(2,1)S(1)} %bitcast.36, bf16[16,32,512]{2,1,0:T(8,128)(2,1)S(1)} %bitcast.38, ...), custom_call_target="tpu_custom_call" | custom-call | flops 700000000 | bytes 30000000 | tf_op jit(solution)/shard_map/into_rows_next/pallas_call | solution.py:363
  129.2 1.1 collective-permute-start.3
  130.3 1.5 %collective-permute-done.3.got_ref = bf16[8,2,32,512]{3,2,1,0:T(8,128)(2,1)S(1)} collective-permute-done((bf16[8,2,32,512]{3,2,1,0:T(8,128)(2,1)S(1)}, bf16[8,2,32,512]{3,2,1,0:T(8,128)(2,1)S(1)}, u32[]{:S(2)}, u32[]{:S(2)}) %collective-permute-start.3) | collective-permute-done | bytes 524320 | tf_op jit(solution)/shard_map/ppermute | solution.py:57
  132.5 12.6 %all_to_all.42.parts_ref = bf16[8,2,32,512]{3,2,1,0:T(8,128)(2,1)S(1)} all-to-all(bf16[8,2,32,512]{3,2,1,0:T(8,128)(2,1)S(1)} %pair_sum.3), channel_id=1, replica_groups={{0,16,32,48,64,80,96,112},{8,24,40,56,72,88,104,120},{1,17,33,49,65,81,..., dimensions={0} | all-to-all | bytes 1048576 | tf_op jit(solution)/shard_map/all_to_all | solution.py:53
  (39 shorter events, 13.6 us)
Async XLA Ops:
  0.6 0.9 copy-start.4
  1.5 44.8 %copy-start.7 = (f32[16]{0:T(128)S(1)}, f32[16]{0:T(128)}, u32[]{:S(2)}) copy-start(f32[16]{0:T(128)} %refs_0_.1) | copy-start | bytes 196
  2.4 16.6 %all-to-all-start = ((bf16[8,2,32,512]{3,2,1,0:T(8,128)(2,1)}), bf16[8,2,32,512]{3,2,1,0:T(8,128)(2,1)S(1)}, u32[]{:S(2)}, u32[]{:S(2)}) async-start(bf16[8,2,32,512]{3,2,1,0:T(8,128)(2,1)} %spread_start.1), calls=%async_computation | async-start | bytes 1048576 | tf_op jit(solution)/shard_map/all_to_all | solution.py:53
  18.9 2.4 %collective-permute-start = (bf16[8,2,32,512]{3,2,1,0:T(8,128)(2,1)S(1)}, bf16[8,2,32,512]{3,2,1,0:T(8,128)(2,1)S(1)}, u32[]{:S(2)}, u32[]{:S(2)}) collective-permute-start(bf16[8,2,32,512]{3,2,1,0:T(8,128)(2,1)S(1)} %all-to-all-done), channel_id=1, source_target_pairs={{0,8},{8,0},{16,24},{24,16},{32,40},{40,32},{48,56},{56,48},{64,72... | collective-permute-start | bytes 1572872 | tf_op jit(solution)/shard_map/ppermute | solution.py:57
  22.7 18.8 %all-to-all-start.2 = ((bf16[8,2,32,512]{3,2,1,0:T(8,128)(2,1)}), bf16[8,2,32,512]{3,2,1,0:T(8,128)(2,1)S(1)}, u32[]{:S(2)}, u32[]{:S(2)}) async-start(bf16[8,2,32,512]{3,2,1,0:T(8,128)(2,1)} %spread_row.2), calls=%async_computation.2 | async-start | bytes 1048576 | tf_op jit(solution)/shard_map/all_to_all | solution.py:48
  29.8 46.1 %copy-start.5 = (f32[32,1024]{1,0:T(8,128)S(1)}, f32[32,1024]{1,0:T(8,128)}, u32[]{:S(2)}) copy-start(f32[32,1024]{1,0:T(8,128)} %trace_ref.3) | copy-start | bytes 393220
  29.8 46.1 %copy-start.6 = (f32[32,1024]{1,0:T(8,128)S(1)}, f32[32,1024]{1,0:T(8,128)}, u32[]{:S(2)}) copy-start(f32[32,1024]{1,0:T(8,128)} %load_ref.3) | copy-start | bytes 393220
  41.5 16.6 %all-to-all-start.1 = ((bf16[8,2,32,512]{3,2,1,0:T(8,128)(2,1)}), bf16[8,2,32,512]{3,2,1,0:T(8,128)(2,1)S(1)}, u32[]{:S(2)}, u32[]{:S(2)}) async-start(bf16[8,2,32,512]{3,2,1,0:T(8,128)(2,1)} %bitcast.9), calls=%async_computation.1 | async-start | bytes 1048576 | tf_op jit(solution)/shard_map/all_to_all | solution.py:48
  57.3 0.8 copy-start
  58.1 1.0 copy-start.1
  59.8 2.8 %collective-permute-start.1 = (bf16[8,2,32,512]{3,2,1,0:T(8,128)(2,1)S(1)}, bf16[8,2,32,512]{3,2,1,0:T(8,128)(2,1)S(1)}, u32[]{:S(2)}, u32[]{:S(2)}) collective-permute-start(bf16[8,2,32,512]{3,2,1,0:T(8,128)(2,1)S(1)} %for_mate.2), channel_id=1, source_target_pairs={{0,8},{8,0},{16,24},{24,16},{32,40},{40,32},{48,56},{56,48},{64,72... | collective-permute-start | bytes 1572872 | tf_op jit(solution)/shard_map/ppermute | solution.py:57
  87.6 3.4 %collective-permute-start.2 = (bf16[8,2,32,512]{3,2,1,0:T(8,128)(2,1)S(1)}, bf16[8,2,32,512]{3,2,1,0:T(8,128)(2,1)S(1)}, u32[]{:S(2)}, u32[]{:S(2)}) collective-permute-start(bf16[8,2,32,512]{3,2,1,0:T(8,128)(2,1)S(1)} %all_to_all.41), channel_id=1, source_target_pairs={{0,8},{8,0},{16,24},{24,16},{32,40},{40,32},{48,56},{56,48},{64,72... | collective-permute-start | bytes 1572872 | tf_op jit(solution)/shard_map/ppermute | solution.py:57
  92.3 18.7 %all-to-all-start.6 = ((bf16[8,2,32,512]{3,2,1,0:T(8,128)(2,1)}), bf16[8,2,32,512]{3,2,1,0:T(8,128)(2,1)S(1)}, u32[]{:S(2)}, u32[]{:S(2)}) async-start(bf16[8,2,32,512]{3,2,1,0:T(8,128)(2,1)} %spread_row.3), calls=%async_computation.6 | async-start | bytes 1048576 | tf_op jit(solution)/shard_map/all_to_all | solution.py:48
  111.0 16.5 %all-to-all-start.5 = ((bf16[8,2,32,512]{3,2,1,0:T(8,128)(2,1)}), bf16[8,2,32,512]{3,2,1,0:T(8,128)(2,1)S(1)}, u32[]{:S(2)}, u32[]{:S(2)}) async-start(bf16[8,2,32,512]{3,2,1,0:T(8,128)(2,1)} %bitcast.18), calls=%async_computation.5 | async-start | bytes 1048576 | tf_op jit(solution)/shard_map/all_to_all | solution.py:48
  126.6 0.8 copy-start.2
  127.5 1.0 copy-start.3
  129.2 2.6 %collective-permute-start.3 = (bf16[8,2,32,512]{3,2,1,0:T(8,128)(2,1)S(1)}, bf16[8,2,32,512]{3,2,1,0:T(8,128)(2,1)S(1)}, u32[]{:S(2)}, u32[]{:S(2)}) collective-permute-start(bf16[8,2,32,512]{3,2,1,0:T(8,128)(2,1)S(1)} %for_mate.3), channel_id=1, source_target_pairs={{0,8},{8,0},{16,24},{24,16},{32,40},{40,32},{48,56},{56,48},{64,72... | collective-permute-start | bytes 1572872 | tf_op jit(solution)/shard_map/ppermute | solution.py:57

commit v5 on v4

--- a/solution.py
+++ b/solution.py
@@ -61,15 +61,11 @@
     return jnp.where(is_far == 0, near_ref[index], far_ref[index])
 
 
-def put_everywhere(half_pair, out_ref, copies):
-    for copy in range(copies):
-        for half in range(2):
-            out_ref[copy, half] = half_pair[half]
-
-
 def start_body(trace_ref, out_ref):
-    halves = [trace_ref[:, h * TILE : (h + 1) * TILE].astype(bf16) for h in range(2)]
-    put_everywhere(halves, out_ref, CHIPS)
+    for half in range(2):
+        rounded = trace_ref[:, half * TILE : (half + 1) * TILE].astype(bf16)
+        for copy in range(CHIPS):
+            out_ref[copy, half] = rounded
 
 
 def spread_start(trace_start):
@@ -85,18 +81,17 @@
 
 def row_body(first_iteration, scal_ref, near_ref, far_ref, *refs):
     out_ref = refs[-1]
-    core = scal_ref[SLOTS + 6]
-    halves = [
-        pick(near_ref, far_ref, core, scal_ref[SLOTS + 1]),
-        pick(near_ref, far_ref, scal_ref[SLOTS + 5], scal_ref[SLOTS + 2]),
-    ]
-    put_everywhere(halves, out_ref, N_ROW)
+    mine = pick(near_ref, far_ref, scal_ref[SLOTS + 5], scal_ref[SLOTS + 1])
+    tail = pick(near_ref, far_ref, scal_ref[SLOTS + 7], scal_ref[SLOTS + 2])
+    for peer in range(N_ROW):
+        out_ref[peer, :, : 3 * LANES] = mine[:, : 3 * LANES]
+        out_ref[peer, :, 3 * LANES :] = tail[:, 3 * LANES :]
     if first_iteration:
 
         @pl.when(scal_ref[SLOTS] == 1)
         def _():
             for peer in range(N_ROW):
-                out_ref[peer, 0, :, LANES : 3 * LANES] = refs[0][...]
+                out_ref[peer, :, LANES : 3 * LANES] = refs[0][...]
 
 
 def spread_row(scal, near, far, edges):
@@ -104,7 +99,7 @@
     args = [scal, near, far] + ([edges] if first_iteration else [])
     return pl.pallas_call(
         functools.partial(row_body, first_iteration),
-        out_shape=jax.ShapeDtypeStruct((N_ROW, 2, RHS, TILE), bf16),
+        out_shape=jax.ShapeDtypeStruct((N_ROW, RHS, TILE), bf16),
         in_specs=[SMEM] + [VMEM] * (len(args) - 1),
         out_specs=VMEM,
         compiler_params=pltpu.CompilerParams(vmem_limit_bytes=6 * MIB),
@@ -195,8 +190,8 @@
     lane = lax.broadcasted_iota(jnp.int32, (8, LANES), 1)
     nothing = jnp.zeros((8, LANES), f32)
     for chunk, source, start, here in (
-        (0, 2 * before, 2 * LANES, row > 0),
-        (EXT - 1, 2 * after, LANES, row < N_ROW - 1),
+        (0, before, 2 * LANES, row > 0),
+        (EXT - 1, after, LANES, row < N_ROW - 1),
     ):
         sent = win_ref[source, :, start : start + LANES].astype(f32)
         k = nothing
@@ -237,8 +232,8 @@
     core = scal_ref[SLOTS + 6]
     before = jnp.maximum(row - 1, 0)
     after = jnp.minimum(row + 1, N_ROW - 1)
-    top_ref[0] = win_ref[2 * before + 1, :, TILE - LANES :].astype(f32)
-    top_ref[EXT - 1] = win_ref[2 * after, :, :LANES].astype(f32)
+    top_ref[0] = win_ref[before, :, TILE - LANES :].astype(f32)
+    top_ref[EXT - 1] = win_ref[after, :, :LANES].astype(f32)
     for tile in range(8):
         is_far = jnp.bitwise_xor(tile // 2 % 2, core)
         tops = pick(near_ref, far_ref, is_far, 4 * quarter + tile // 4 * 2 + tile % 2)
@@ -275,21 +270,23 @@
         sweep(states[step % 2], states[1 - step % 2])
 
 
-def rows_body(first_iteration, scal_ref, near_ref, far_ref, win_ref, panel_ref, *refs):
+def rows_body(first_iteration, scal_ref, near_ref, far_ref, win_ref, mate_win_ref, panel_ref, *refs):
     if first_iteration:
-        table_ref, cells_ref, own_out, mate_out, head_out, state_out, coef_out = refs[:7]
-        refs = refs[7:]
+        table_ref, cells_ref, own_out, mate_out, state_out, coef_out = refs[:6]
+        refs = refs[6:]
     else:
-        state_in, coef_in, own_out, mate_out, head_out = refs[:5]
-        refs = refs[5:]
+        state_in, coef_in, own_out, mate_out = refs[:4]
+        refs = refs[4:]
     band_acc, state_a, state_b, coef_ref, cell_ref, top_ref, sems, buffer_ref, panel_sems = refs
     is_volume = scal_ref[SLOTS] == 1
+    core = scal_ref[SLOTS + 6]
 
     @pl.when(jnp.logical_not(is_volume))
     def _():
         def one_slot(slot, named, shard, half, col_tile):
+            is_far = jnp.bitwise_xor(jnp.bitwise_and(col_tile, 1), core)
             band_acc[jnp.where(named, 2 * shard + half, BAND_TILES)] += lax.dot_general(
-                win_ref[col_tile],
+                pick(win_ref, mate_win_ref, is_far, lax.shift_right_logical(col_tile, 1)),
                 buffer_ref[slot],
                 (((1,), (1,)), ((), ())),
                 preferred_element_type=f32,
@@ -333,23 +330,20 @@
             for save in saves:
                 save.wait()
 
-    core = scal_ref[SLOTS + 6]
     for chip in range(CHIPS):
         own_out[chip] = band_acc[pl.ds(4 * chip + 2 * core, 2)]
         mate_out[chip] = band_acc[pl.ds(4 * chip + 2 - 2 * core, 2)].astype(bf16)
-    head_out[...] = band_acc[:2]
-
-
-def into_rows(scal, near, far, win, panel, table, cells, saved):
+
+
+def into_rows(scal, near, far, win, mate_win, panel, table, cells, saved):
     first_iteration = saved is None
     outs = [
         jax.ShapeDtypeStruct((CHIPS, 2, RHS, TILE), f32),
         jax.ShapeDtypeStruct((CHIPS, 2, RHS, TILE), bf16),
-        jax.ShapeDtypeStruct((2, RHS, TILE), f32),
     ]
-    out_specs = [VMEM, VMEM, VMEM]
-    in_specs = [SMEM, VMEM, VMEM, VMEM, ANY]
-    args = [scal, near, far, win, panel]
+    out_specs = [VMEM, VMEM]
+    in_specs = [SMEM, VMEM, VMEM, VMEM, VMEM, ANY]
+    args = [scal, near, far, win, mate_win, panel]
     state = (EXT + 2, LAYERS, RHS, LANES)
     coefs = (EXT, 48, LANES)
     if first_iteration:
@@ -382,47 +376,41 @@
     )(*args)
 
 
-def mate_body(scal_ref, parts_ref, head_ref, mate_ref, out_ref):
-    out_ref[...] = mate_ref[...]
-
-    @pl.when(scal_ref[SLOTS + 6] == 1)
-    def _():
-        total = head_ref[...]
-        for peer in range(N_ROW):
-            total = total + parts_ref[peer].astype(f32)
-        out_ref[0] = total.astype(bf16)
-
-
-def for_mate(scal, parts, head, mate):
-    return pl.pallas_call(
-        mate_body,
-        out_shape=jax.ShapeDtypeStruct(mate.shape, bf16),
-        in_specs=[SMEM, VMEM, VMEM, VMEM],
+def share_body(parts_ref, out_ref):
+    share = parts_ref[0].astype(f32)
+    for peer in range(1, N_ROW):
+        share = share + parts_ref[peer].astype(f32)
+    out_ref[...] = share
+
+
+def window_share(parts):
+    return pl.pallas_call(
+        share_body,
+        out_shape=jax.ShapeDtypeStruct(parts.shape[1:], f32),
+        in_specs=[VMEM],
         out_specs=VMEM,
         compiler_params=pltpu.CompilerParams(vmem_limit_bytes=6 * MIB),
-        name="for_mate",
-    )(scal, parts, head, mate)
-
-
-def pair_body(scal_ref, parts_ref, own_ref, got_ref, out_ref):
+        name="window_share",
+    )(parts)
+
+
+def pair_body(scal_ref, own_ref, got_ref, share_ref, got_share_ref, out_ref):
     for chip in range(1, CHIPS):
         out_ref[chip] = (own_ref[chip] + got_ref[chip].astype(f32)).astype(bf16)
     total = own_ref[0] + got_ref[0].astype(f32)
-    share = parts_ref[0].astype(f32)
-    for peer in range(1, N_ROW):
-        share = share + parts_ref[peer].astype(f32)
+    share = share_ref[...] + got_share_ref[...]
     out_ref[0] = (total + jnp.where(scal_ref[SLOTS + 6] == 0, share, 0.0)).astype(bf16)
 
 
-def pair_sum(scal, parts, own, got):
+def pair_sum(scal, own, got, share, got_share):
     return pl.pallas_call(
         pair_body,
         out_shape=jax.ShapeDtypeStruct(got.shape, bf16),
-        in_specs=[SMEM, VMEM, VMEM, VMEM],
+        in_specs=[SMEM, VMEM, VMEM, VMEM, VMEM],
         out_specs=VMEM,
         compiler_params=pltpu.CompilerParams(vmem_limit_bytes=6 * MIB),
         name="pair_sum",
-    )(scal, parts, own, got)
+    )(scal, own, got, share, got_share)
 
 
 def update_body(last, parts_ref, trace_ref, load_ref, *outs):
@@ -488,18 +476,20 @@
     core = col_index % CORES
     own = [
         is_volume,
-        jnp.where(is_volume, 4 * quarter, 0),
-        jnp.where(is_volume, 4 * quarter + 3, 1),
+        jnp.where(is_volume, 4 * quarter, core),
+        jnp.where(is_volume, 4 * quarter + 3, core),
         quarter,
         row_index,
+        core,
+        core,
         jnp.where(is_volume, 1 - core, core),
-        core,
     ]
     scal = jnp.concatenate([tile_list, jnp.stack([x.astype(jnp.int32) for x in own])])
     traces = trace_start
     spread = spread_start(traces)
     cells, edges = volume_cells(coef_index, coef_table, vol_source, volume_line)
     panel = in_hbm(panel_tiles)
+    cells, edges = lax.optimization_barrier((cells, edges))
     saved = None
     for iteration in range(ITERS):
         last = iteration == ITERS - 1
@@ -507,14 +497,17 @@
         far = from_mate(near)
         near, far = near.reshape(TILES, RHS, TILE), far.reshape(TILES, RHS, TILE)
         row_spread = spread_row(scal, near, far, edges if iteration == 0 else None)
-        win = exchange(row_spread, "row").reshape(WIN_TILES, RHS, TILE)
+        win = exchange(row_spread, "row")
         win_part = into_window(scal, near, far, panel)
+        win, _ = lax.optimization_barrier((win, win_part))
+        mate_win = from_mate(win)
         parts = exchange(win_part.reshape(N_ROW, 2, RHS, TILE), "row")
-        own, mate, head, *saved = into_rows(
-            scal, near, far, win, panel, coef_table, cells, saved
+        own, mate, *saved = into_rows(
+            scal, near, far, win, mate_win, panel, coef_table, cells, saved
         )
-        got = from_mate(for_mate(scal, parts, head, mate))
-        summed = between_chips(pair_sum(scal, parts, own, got))
+        got = from_mate(mate)
+        share = window_share(parts)
+        summed = between_chips(pair_sum(scal, own, got, share, from_mate(share)))
         traces, spread = update(summed, traces, surface_load, last)
     return (traces, spread)
 

time: 147 us -> 147 us (level)
  starting transfers between devices: 34.9 us -> 39.7 us
  waiting for transfers between devices: 14.4 us -> 11.2 us
  local copies, waits for them, and re-layouts: 6.17 us -> 4.17 us
    all_to_all x4, starting transfers between devices: 23.6 us -> 27.7 us  [exchange(): return lax.all_to_all(x, axis, 0, 0, tiled=True)]
    all_to_all x4, waiting for transfers between devices: 3.87 us -> 0.01 us  [exchange(): return lax.all_to_all(x, axis, 0, 0, tiled=True)]
    unnamed x16 -> x12, local copies, waits for them, and re-layouts: 4.56 us -> 2.56 us
    all_to_all x1, waiting for transfers between devices: 5.18 us -> 7.14 us  [between_chips(): return lax.all_to_all(x, 'col', 0, 0, axis_index_groups=groups, tiled=True)]
    pallas_call x2, Pallas kernels: 21.4 us -> 22.9 us  [into_rows(): pl.pallas_call(functools.partial(rows_body, first_iteration), out_shape=o...]
    ppermute x4 -> x8, waiting for transfers between devices: 5.35 us -> 4.01 us  [from_mate(): return lax.ppermute(x, 'col', [(i, i ^ 1) for i in range(N_COL)])]
    ppermute x4 -> x8, starting transfers between devices: 4.95 us -> 5.55 us  [from_mate(): return lax.ppermute(x, 'col', [(i, i ^ 1) for i in range(N_COL)])]
  transfers between devices with their start and end apart: 9 -> 13, of which waited for: 8 -> 4; matrix products, arithmetic and copies ran while one was open for 3% -> 3% of each run, Pallas kernels for 28% -> 29%
where the time goes in v5:
time: 147 us; the launch traced here: 146 us
  Pallas kernels  48.4 us (33%)
  starting transfers between devices  39.7 us (27%)
  blocking collectives  36.9 us (25%)
  waiting for transfers between devices  11.2 us (8%)
  local copies, waits for them, and re-layouts  4.17 us (3%)
  other arithmetic  3.17 us (2%)
  between operations  2.78 us (2%)
    all_to_all x3, blocking collectives, between_chips(): return lax.all_to_all(x, 'col', 0, 0, axis_index_groups=groups, tiled=True)  36.9 us
    all_to_all x4, starting transfers between devices, exchange(): return lax.all_to_all(x, axis, 0, 0, tiled=True)  27.7 us
    pallas_call x2, Pallas kernels, into_rows(): pl.pallas_call(functools.partial(rows_body, first_iteration), out_shape=o...  22.9 us
    pallas_call x2, Pallas kernels, into_window(): pl.pallas_call(window_body, out_shape=jax.ShapeDtypeStruct((WIN_TILES, RH...  19.8 us
    all_to_all x1, waiting for transfers between devices, between_chips(): return lax.all_to_all(x, 'col', 0, 0, axis_index_groups=groups, tiled=True)  7.14 us
    all_to_all x1, starting transfers between devices, between_chips(): return lax.all_to_all(x, 'col', 0, 0, axis_index_groups=groups, tiled=True)  6.37 us
    ppermute x8, starting transfers between devices, from_mate(): return lax.ppermute(x, 'col', [(i, i ^ 1) for i in range(N_COL)])  5.55 us
    ppermute x8, waiting for transfers between devices, from_mate(): return lax.ppermute(x, 'col', [(i, i ^ 1) for i in range(N_COL)])  4.01 us
  transfers between devices with their start and end apart: 13, of which 4 were waited for; matrix products, arithmetic and copies ran while one was open for 3% of the time, Pallas kernels for 29%

profile of v5, /device:TPU:1, one launch (start us, length us, event | category | flops | bytes accessed | tf_op | source)
XLA Modules:
  0.0 146.2 jit_solution(12203512337690949572)
XLA Ops:
  0.6 0.9 copy-done
  2.4 6.4 %all-to-all-start = ((bf16[8,2,32,512]{3,2,1,0:T(8,128)(2,1)}), bf16[8,2,32,512]{3,2,1,0:T(8,128)(2,1)S(1)}, u32[]{:S(2)}, u32[]{:S(2)}) async-start(bf16[8,2,32,512]{3,2,1,0:T(8,128)(2,1)} %spread_start.1), calls=%async_computation | async-start | bytes 1048576 | tf_op jit(solution)/shard_map/all_to_all | solution.py:53
  9.6 0.9 dynamic-slice_bitcast_fusion.1
  10.5 1.3 fusion.10
  11.8 7.1 %all-to-all-done = bf16[8,2,32,512]{3,2,1,0:T(8,128)(2,1)S(1)} async-done(((bf16[8,2,32,512]{3,2,1,0:T(8,128)(2,1)}), bf16[8,2,32,512]{3,2,1,0:T(8,128)(2,1)S(1)}, u32[]{:S(2)}, u32[]{:S(2)}) %all-to-all-start) | async-done | bytes 524320 | tf_op jit(solution)/shard_map/all_to_all | solution.py:53
  21.8 1.0 select_reduce_fusion
  23.6 1.3 spread_row.2
  24.8 7.0 %all-to-all-start.1 = ((bf16[8,32,512]{2,1,0:T(8,128)(2,1)}), bf16[8,32,512]{2,1,0:T(8,128)(2,1)S(1)}, u32[]{:S(2)}, u32[]{:S(2)}) async-start(bf16[8,32,512]{2,1,0:T(8,128)(2,1)} %spread_row.2), calls=%async_computation.1 | async-start | bytes 524288 | tf_op jit(solution)/shard_map/all_to_all | solution.py:48
  31.9 9.9 %into_window.2 = bf16[16,32,512]{2,1,0:T(8,128)(2,1)} custom-call(s32[51]{0:T(128)S(1)} %concatenate.15.scal_ref, bf16[16,32,512]{2,1,0:T(8,128)(2,1)S(1)} %bitcast.24, bf16[16,32,512]{2,1,0:T(8,128)(2,1)S(1)} %bitcast.30, bf16[43,512,512]{2,1,0:T(8,128)(2,1)} %panel_ref.7), custom_call_target="tpu_custom_call" | custom-call | flops 700000000 | bytes 25000000 | tf_op jit(solution)/shard_map/into_window/pallas_call | solution.py:169
  42.2 6.9 %all-to-all-start.2 = ((bf16[8,2,32,512]{3,2,1,0:T(8,128)(2,1)}), bf16[8,2,32,512]{3,2,1,0:T(8,128)(2,1)S(1)}, u32[]{:S(2)}, u32[]{:S(2)}) async-start(bf16[8,2,32,512]{3,2,1,0:T(8,128)(2,1)} %bitcast.14), calls=%async_computation.2 | async-start | bytes 1048576 | tf_op jit(solution)/shard_map/all_to_all | solution.py:48
  49.8 0.9 copy-done.4
  50.7 11.4 %into_rows_first.1 = (f32[8,2,32,512]{3,2,1,0:T(8,128)S(1)}, bf16[8,2,32,512]{3,2,1,0:T(8,128)(2,1)}, f32[36,4,32,128]{3,2,1,0:T(8,128)}, f32[34,48,128]{2,1,0:T(8,128)}) custom-call(s32[51]{0:T(128)S(1)} %concatenate.15.scal_ref, bf16[16,32,512]{2,1,0:T(8,128)(2,1)S(1)} %bitcast.25, bf16[16,32,512]{2,1,0:T(8,128)(2,1)S(1)} %bitcast.31, ...), custom_call_target="tpu_custom_call" | custom-call | flops 700000000 | bytes 30000000 | tf_op jit(solution)/shard_map/into_rows_first/pallas_call | solution.py:357
  62.9 1.4 collective-permute-done.3.got_share_ref
  65.0 12.6 %all_to_all.40.parts_ref = bf16[8,2,32,512]{3,2,1,0:T(8,128)(2,1)S(1)} all-to-all(bf16[8,2,32,512]{3,2,1,0:T(8,128)(2,1)S(1)} %pair_sum.2), channel_id=1, replica_groups={{0,16,32,48,64,80,96,112},{8,24,40,56,72,88,104,120},{1,17,33,49,65,81,..., dimensions={0} | all-to-all | bytes 1048576 | tf_op jit(solution)/shard_map/all_to_all | solution.py:53
  77.8 11.6 %all_to_all.41 = bf16[8,2,32,512]{3,2,1,0:T(8,128)(2,1)S(1)} all-to-all(bf16[8,2,32,512]{3,2,1,0:T(8,128)(2,1)S(1)} %get-tuple-element.19), channel_id=1, replica_groups={{0,16,32,48,64,80,96,112},{8,24,40,56,72,88,104,120},{1,17,33,49,65,81,..., dimensions={0} | all-to-all | bytes 1048576 | tf_op jit(solution)/shard_map/all_to_all | solution.py:53
  89.4 1.8 %collective-permute-start.4 = (bf16[8,2,32,512]{3,2,1,0:T(8,128)(2,1)S(1)}, bf16[8,2,32,512]{3,2,1,0:T(8,128)(2,1)S(1)}, u32[]{:S(2)}, u32[]{:S(2)}) collective-permute-start(bf16[8,2,32,512]{3,2,1,0:T(8,128)(2,1)S(1)} %all_to_all.41), channel_id=1, source_target_pairs={{0,8},{8,0},{16,24},{24,16},{32,40},{40,32},{48,56},{56,48},{64,72... | collective-permute-start | bytes 1572872 | tf_op jit(solution)/shard_map/ppermute | solution.py:57
  91.2 1.5 %collective-permute-done.4 = bf16[8,2,32,512]{3,2,1,0:T(8,128)(2,1)S(1)} collective-permute-done((bf16[8,2,32,512]{3,2,1,0:T(8,128)(2,1)S(1)}, bf16[8,2,32,512]{3,2,1,0:T(8,128)(2,1)S(1)}, u32[]{:S(2)}, u32[]{:S(2)}) %collective-permute-start.4) | collective-permute-done | bytes 524320 | tf_op jit(solution)/shard_map/ppermute | solution.py:57
  92.8 1.3 spread_row.3
  94.0 6.9 %all-to-all-start.5 = ((bf16[8,32,512]{2,1,0:T(8,128)(2,1)}), bf16[8,32,512]{2,1,0:T(8,128)(2,1)S(1)}, u32[]{:S(2)}, u32[]{:S(2)}) async-start(bf16[8,32,512]{2,1,0:T(8,128)(2,1)} %spread_row.3), calls=%async_computation.5 | async-start | bytes 524288 | tf_op jit(solution)/shard_map/all_to_all | solution.py:48
  100.9 9.9 %into_window.3 = bf16[16,32,512]{2,1,0:T(8,128)(2,1)} custom-call(s32[51]{0:T(128)S(1)} %concatenate.15.scal_ref, bf16[16,32,512]{2,1,0:T(8,128)(2,1)S(1)} %bitcast.27, bf16[16,32,512]{2,1,0:T(8,128)(2,1)S(1)} %bitcast.33, bf16[43,512,512]{2,1,0:T(8,128)(2,1)} %panel_ref.7), custom_call_target="tpu_custom_call" | custom-call | flops 700000000 | bytes 25000000 | tf_op jit(solution)/shard_map/into_window/pallas_call | solution.py:169
  111.5 6.9 %all-to-all-start.6 = ((bf16[8,2,32,512]{3,2,1,0:T(8,128)(2,1)}), bf16[8,2,32,512]{3,2,1,0:T(8,128)(2,1)S(1)}, u32[]{:S(2)}, u32[]{:S(2)}) async-start(bf16[8,2,32,512]{3,2,1,0:T(8,128)(2,1)} %bitcast.17), calls=%async_computation.6 | async-start | bytes 1048576 | tf_op jit(solution)/shard_map/all_to_all | solution.py:48
  118.5 11.5 %into_rows_next.1 = (f32[8,2,32,512]{3,2,1,0:T(8,128)S(1)}, bf16[8,2,32,512]{3,2,1,0:T(8,128)(2,1)}) custom-call(s32[51]{0:T(128)S(1)} %concatenate.15.scal_ref, bf16[16,32,512]{2,1,0:T(8,128)(2,1)S(1)} %bitcast.28, bf16[16,32,512]{2,1,0:T(8,128)(2,1)S(1)} %bitcast.34, bf16[8,32,512]{2,1,0:T(8,128)(2,1)S(1)} %all-to-all-done.5.win_ref, ...), custom_call_target="tpu_custom_call" | custom-call | flops 700000000 | bytes 30000000 | tf_op jit(solution)/shard_map/into_rows_next/pallas_call | solution.py:357
  131.1 1.0 collective-permute-done.7.got_share_ref
  132.8 12.6 %all_to_all.42.parts_ref = bf16[8,2,32,512]{3,2,1,0:T(8,128)(2,1)S(1)} all-to-all(bf16[8,2,32,512]{3,2,1,0:T(8,128)(2,1)S(1)} %pair_sum.3), channel_id=1, replica_groups={{0,16,32,48,64,80,96,112},{8,24,40,56,72,88,104,120},{1,17,33,49,65,81,..., dimensions={0} | all-to-all | bytes 1048576 | tf_op jit(solution)/shard_map/all_to_all | solution.py:53
  (43 shorter events, 9.3 us)
Async XLA Ops:
  0.6 0.9 copy-start
  1.5 48.3 %copy-start.5 = (f32[16]{0:T(128)S(1)}, f32[16]{0:T(128)}, u32[]{:S(2)}) copy-start(f32[16]{0:T(128)} %refs_0_.1) | copy-start | bytes 196
  2.4 16.6 %all-to-all-start = ((bf16[8,2,32,512]{3,2,1,0:T(8,128)(2,1)}), bf16[8,2,32,512]{3,2,1,0:T(8,128)(2,1)S(1)}, u32[]{:S(2)}, u32[]{:S(2)}) async-start(bf16[8,2,32,512]{3,2,1,0:T(8,128)(2,1)} %spread_start.1), calls=%async_computation | async-start | bytes 1048576 | tf_op jit(solution)/shard_map/all_to_all | solution.py:53
  18.9 4.6 %collective-permute-start = (bf16[8,2,32,512]{3,2,1,0:T(8,128)(2,1)S(1)}, bf16[8,2,32,512]{3,2,1,0:T(8,128)(2,1)S(1)}, u32[]{:S(2)}, u32[]{:S(2)}) collective-permute-start(bf16[8,2,32,512]{3,2,1,0:T(8,128)(2,1)S(1)} %all-to-all-done), channel_id=1, source_target_pairs={{0,8},{8,0},{16,24},{24,16},{32,40},{40,32},{48,56},{56,48},{64,72... | collective-permute-start | bytes 1572872 | tf_op jit(solution)/shard_map/ppermute | solution.py:57
  24.8 17.0 %all-to-all-start.1 = ((bf16[8,32,512]{2,1,0:T(8,128)(2,1)}), bf16[8,32,512]{2,1,0:T(8,128)(2,1)S(1)}, u32[]{:S(2)}, u32[]{:S(2)}) async-start(bf16[8,32,512]{2,1,0:T(8,128)(2,1)} %spread_row.2), calls=%async_computation.1 | async-start | bytes 524288 | tf_op jit(solution)/shard_map/all_to_all | solution.py:48
  31.9 45.8 %copy-start.1 = (f32[32,1024]{1,0:T(8,128)S(1)}, f32[32,1024]{1,0:T(8,128)}, u32[]{:S(2)}) copy-start(f32[32,1024]{1,0:T(8,128)} %trace_ref.3) | copy-start | bytes 393220
  31.9 45.8 %copy-start.2 = (f32[32,1024]{1,0:T(8,128)S(1)}, f32[32,1024]{1,0:T(8,128)}, u32[]{:S(2)}) copy-start(f32[32,1024]{1,0:T(8,128)} %load_ref.3) | copy-start | bytes 393220
  41.8 7.3 %collective-permute-start.1 = (bf16[8,32,512]{2,1,0:T(8,128)(2,1)S(1)}, bf16[8,32,512]{2,1,0:T(8,128)(2,1)S(1)}, u32[]{:S(2)}, u32[]{:S(2)}) collective-permute-start(bf16[8,32,512]{2,1,0:T(8,128)(2,1)S(1)} %all-to-all-done.1.win_ref), channel_id=1, source_target_pairs={{0,8},{8,0},{16,24},{24,16},{32,40},{40,32},{48,56},{56,48},{64,72... | collective-permute-start | bytes 786440 | tf_op jit(solution)/shard_map/ppermute | solution.py:57
  42.2 20.4 %all-to-all-start.2 = ((bf16[8,2,32,512]{3,2,1,0:T(8,128)(2,1)}), bf16[8,2,32,512]{3,2,1,0:T(8,128)(2,1)S(1)}, u32[]{:S(2)}, u32[]{:S(2)}) async-start(bf16[8,2,32,512]{3,2,1,0:T(8,128)(2,1)} %bitcast.14), calls=%async_computation.2 | async-start | bytes 1048576 | tf_op jit(solution)/shard_map/all_to_all | solution.py:48
  49.1 0.7 copy-start.3
  49.8 1.0 copy-start.4
  62.2 2.2 %collective-permute-start.2 = (bf16[8,2,32,512]{3,2,1,0:T(8,128)(2,1)}, bf16[8,2,32,512]{3,2,1,0:T(8,128)(2,1)S(1)}, u32[]{:S(2)}, u32[]{:S(2)}) collective-permute-start(bf16[8,2,32,512]{3,2,1,0:T(8,128)(2,1)} %get-tuple-element.18), channel_id=1, source_target_pairs={{0,8},{8,0},{16,24},{24,16},{32,40},{40,32},{48,56},{56,48},{64,72... | collective-permute-start | bytes 1572872 | tf_op jit(solution)/shard_map/ppermute | solution.py:57
  62.6 1.7 %collective-permute-start.3 = (f32[2,32,512]{2,1,0:T(8,128)S(1)}, f32[2,32,512]{2,1,0:T(8,128)S(1)}, u32[]{:S(2)}, u32[]{:S(2)}) collective-permute-start(f32[2,32,512]{2,1,0:T(8,128)S(1)} %window_share.2.share_ref), channel_id=1, source_target_pairs={{0,8},{8,0},{16,24},{24,16},{32,40},{40,32},{48,56},{56,48},{64,72... | collective-permute-start | bytes 393224 | tf_op jit(solution)/shard_map/ppermute | solution.py:57
  89.4 3.4 %collective-permute-start.4 = (bf16[8,2,32,512]{3,2,1,0:T(8,128)(2,1)S(1)}, bf16[8,2,32,512]{3,2,1,0:T(8,128)(2,1)S(1)}, u32[]{:S(2)}, u32[]{:S(2)}) collective-permute-start(bf16[8,2,32,512]{3,2,1,0:T(8,128)(2,1)S(1)} %all_to_all.41), channel_id=1, source_target_pairs={{0,8},{8,0},{16,24},{24,16},{32,40},{40,32},{48,56},{56,48},{64,72... | collective-permute-start | bytes 1572872 | tf_op jit(solution)/shard_map/ppermute | solution.py:57
  94.0 16.7 %all-to-all-start.5 = ((bf16[8,32,512]{2,1,0:T(8,128)(2,1)}), bf16[8,32,512]{2,1,0:T(8,128)(2,1)S(1)}, u32[]{:S(2)}, u32[]{:S(2)}) async-start(bf16[8,32,512]{2,1,0:T(8,128)(2,1)} %spread_row.3), calls=%async_computation.5 | async-start | bytes 524288 | tf_op jit(solution)/shard_map/all_to_all | solution.py:48
  110.8 7.7 %collective-permute-start.5 = (bf16[8,32,512]{2,1,0:T(8,128)(2,1)S(1)}, bf16[8,32,512]{2,1,0:T(8,128)(2,1)S(1)}, u32[]{:S(2)}, u32[]{:S(2)}) collective-permute-start(bf16[8,32,512]{2,1,0:T(8,128)(2,1)S(1)} %all-to-all-done.5.win_ref), channel_id=1, source_target_pairs={{0,8},{8,0},{16,24},{24,16},{32,40},{40,32},{48,56},{56,48},{64,72... | collective-permute-start | bytes 786440 | tf_op jit(solution)/shard_map/ppermute | solution.py:57
  111.5 18.8 %all-to-all-start.6 = ((bf16[8,2,32,512]{3,2,1,0:T(8,128)(2,1)}), bf16[8,2,32,512]{3,2,1,0:T(8,128)(2,1)S(1)}, u32[]{:S(2)}, u32[]{:S(2)}) async-start(bf16[8,2,32,512]{3,2,1,0:T(8,128)(2,1)} %bitcast.17), calls=%async_computation.6 | async-start | bytes 1048576 | tf_op jit(solution)/shard_map/all_to_all | solution.py:48
  130.0 2.2 %collective-permute-start.6 = (bf16[8,2,32,512]{3,2,1,0:T(8,128)(2,1)}, bf16[8,2,32,512]{3,2,1,0:T(8,128)(2,1)S(1)}, u32[]{:S(2)}, u32[]{:S(2)}) collective-permute-start(bf16[8,2,32,512]{3,2,1,0:T(8,128)(2,1)} %get-tuple-element.24), channel_id=1, source_target_pairs={{0,8},{8,0},{16,24},{24,16},{32,40},{40,32},{48,56},{56,48},{64,72... | collective-permute-start | bytes 1572872 | tf_op jit(solution)/shard_map/ppermute | solution.py:57
  130.4 1.7 %collective-permute-start.7 = (f32[2,32,512]{2,1,0:T(8,128)S(1)}, f32[2,32,512]{2,1,0:T(8,128)S(1)}, u32[]{:S(2)}, u32[]{:S(2)}) collective-permute-start(f32[2,32,512]{2,1,0:T(8,128)S(1)} %window_share.3.share_ref), channel_id=1, source_target_pairs={{0,8},{8,0},{16,24},{24,16},{32,40},{40,32},{48,56},{56,48},{64,72... | collective-permute-start | bytes 393224 | tf_op jit(solution)/shard_map/ppermute | solution.py:57

commit v6 on v5

--- a/solution.py
+++ b/solution.py
@@ -107,7 +107,14 @@
     )(*args)
 
 
-def for_slots(scal_ref, panel_ref, buffer_ref, sems, acc_ref, do_slot):
+def interleave(near_ref, far_ref, core, run, out_ref):
+    for index in range(near_ref.shape[0]):
+        block, part = index // run, index % run
+        out_ref[(2 * block + core) * run + part] = near_ref[index]
+        out_ref[(2 * block + 1 - core) * run + part] = far_ref[index]
+
+
+def for_slots(scal_ref, panel_ref, buffer_ref, sems, acc_ref, prepare, do_slot):
     def fetch(slot):
         return pltpu.make_async_copy(panel_ref.at[slot], buffer_ref.at[slot], sems.at[slot])
 
@@ -117,6 +124,7 @@
 
     lax.fori_loop(0, SLOTS, start, 0)
     acc_ref[...] = jnp.zeros_like(acc_ref)
+    prepare()
 
     def place(slot):
         ident = scal_ref[slot]
@@ -140,7 +148,7 @@
         place(slot)
 
 
-def window_body(scal_ref, near_ref, far_ref, panel_ref, win_out, win_acc, buffer_ref, sems):
+def window_body(scal_ref, near_ref, far_ref, panel_ref, win_out, win_acc, buffer_ref, sems, traces_ref):
     is_volume = scal_ref[SLOTS] == 1
 
     @pl.when(jnp.logical_not(is_volume))
@@ -148,15 +156,12 @@
         core = scal_ref[SLOTS + 6]
 
         def one_slot(slot, named, shard, half, col_tile):
-            is_far = jnp.bitwise_xor(jnp.bitwise_and(shard, 1), core)
-            index = lax.shift_right_logical(shard, 1) * 2 + half
             win_acc[jnp.where(named, col_tile, WIN_TILES)] += jnp.dot(
-                pick(near_ref, far_ref, is_far, index),
-                buffer_ref[slot],
-                preferred_element_type=f32,
+                traces_ref[2 * shard + half], buffer_ref[slot], preferred_element_type=f32
             )
 
-        for_slots(scal_ref, panel_ref, buffer_ref, sems, win_acc, one_slot)
+        prepare = functools.partial(interleave, near_ref, far_ref, core, 2, traces_ref)
+        for_slots(scal_ref, panel_ref, buffer_ref, sems, win_acc, prepare, one_slot)
 
         win_out[...] = win_acc[:WIN_TILES].astype(bf16)
 
@@ -175,6 +180,7 @@
             pltpu.VMEM((WIN_TILES + 1, RHS, TILE), f32),
             pltpu.VMEM((SLOTS, TILE, TILE), bf16),
             pltpu.SemaphoreType.DMA((SLOTS,)),
+            pltpu.VMEM((BAND_TILES, RHS, TILE), bf16),
         ],
         compiler_params=pltpu.CompilerParams(vmem_limit_bytes=44 * MIB),
         cost_estimate=pl.CostEstimate(flops=7 * 10**8, transcendentals=0, bytes_accessed=25 * 10**6),
@@ -182,13 +188,14 @@
     )(scal, near, far, panel)
 
 
-def weigh(scal_ref, table_ref, cells_ref, win_ref, cell_ref, coef_ref):
+def weigh(scal_ref, table_ref, index_ref, source_ref, win_ref, cell_ref, coef_ref):
     row = scal_ref[SLOTS + 4]
     before = jnp.maximum(row - 1, 0)
     after = jnp.minimum(row + 1, N_ROW - 1)
     layer = lax.broadcasted_iota(jnp.int32, (8, LANES), 0)
     lane = lax.broadcasted_iota(jnp.int32, (8, LANES), 1)
     nothing = jnp.zeros((8, LANES), f32)
+    cell_ref[...] = jnp.zeros_like(cell_ref)
     for chunk, source, start, here in (
         (0, before, 2 * LANES, row > 0),
         (EXT - 1, after, LANES, row < N_ROW - 1),
@@ -199,11 +206,15 @@
             k = jnp.where(sent[0:8] == float(level), table_ref[level], k)
         cell_ref[chunk + 1, 0] = jnp.where((layer < LAYERS) & here, k, 0.0)
         cell_ref[chunk + 1, 1] = jnp.where(here, sent[8:16] + sent[16:24], 0.0)
-    cell_ref[0, 0] = nothing
-    cell_ref[EXT + 1, 0] = nothing
 
     for chunk in range(MID):
-        cell_ref[chunk + 2] = cells_ref[chunk]
+        lanes = slice(chunk * LANES, (chunk + 1) * LANES)
+        indices = index_ref[:, lanes]
+        k = jnp.zeros((LAYERS, LANES), f32)
+        for level in range(COEFS):
+            k = jnp.where(indices == level, table_ref[level], k)
+        cell_ref[chunk + 2, 0, :LAYERS] = k
+        cell_ref[chunk + 2, 1, :LAYERS] = source_ref[:, lanes]
 
     def one_chunk(chunk, carry):
         k = cell_ref[chunk + 1, 0]
@@ -272,27 +283,29 @@
 
 def rows_body(first_iteration, scal_ref, near_ref, far_ref, win_ref, mate_win_ref, panel_ref, *refs):
     if first_iteration:
-        table_ref, cells_ref, own_out, mate_out, state_out, coef_out = refs[:6]
-        refs = refs[6:]
+        table_ref, all_index_ref, all_source_ref, own_out, mate_out, state_out, coef_out = refs[:7]
+        refs = refs[7:]
     else:
         state_in, coef_in, own_out, mate_out = refs[:4]
         refs = refs[4:]
-    band_acc, state_a, state_b, coef_ref, cell_ref, top_ref, sems, buffer_ref, panel_sems = refs
+    band_acc, state_a, state_b, coef_ref, cell_ref, top_ref, sems, buffer_ref, panel_sems, traces_ref = refs[:10]
+    if first_iteration:
+        index_ref, source_ref = refs[10:]
     is_volume = scal_ref[SLOTS] == 1
     core = scal_ref[SLOTS + 6]
 
     @pl.when(jnp.logical_not(is_volume))
     def _():
         def one_slot(slot, named, shard, half, col_tile):
-            is_far = jnp.bitwise_xor(jnp.bitwise_and(col_tile, 1), core)
             band_acc[jnp.where(named, 2 * shard + half, BAND_TILES)] += lax.dot_general(
-                pick(win_ref, mate_win_ref, is_far, lax.shift_right_logical(col_tile, 1)),
+                traces_ref[col_tile],
                 buffer_ref[slot],
                 (((1,), (1,)), ((), ())),
                 preferred_element_type=f32,
             )
 
-        for_slots(scal_ref, panel_ref, buffer_ref, panel_sems, band_acc, one_slot)
+        prepare = functools.partial(interleave, win_ref, mate_win_ref, core, 1, traces_ref)
+        for_slots(scal_ref, panel_ref, buffer_ref, panel_sems, band_acc, prepare, one_slot)
 
     @pl.when(is_volume)
     def _():
@@ -300,8 +313,17 @@
         state_b[0] = guard
         state_b[EXT + 1] = guard
         if first_iteration:
+            line = scal_ref[SLOTS + 8]
+            loads = [
+                pltpu.make_async_copy(all_index_ref.at[line], index_ref, sems.at[0]),
+                pltpu.make_async_copy(all_source_ref.at[line], source_ref, sems.at[1]),
+            ]
+            for load in loads:
+                load.start()
             state_a[...] = jnp.zeros_like(state_a)
-            weigh(scal_ref, table_ref, cells_ref, win_ref, cell_ref, coef_ref)
+            for load in loads:
+                load.wait()
+            weigh(scal_ref, table_ref, index_ref, source_ref, win_ref, cell_ref, coef_ref)
         else:
             loads = [
                 pltpu.make_async_copy(state_in, state_a, sems.at[0]),
@@ -335,7 +357,7 @@
         mate_out[chip] = band_acc[pl.ds(4 * chip + 2 - 2 * core, 2)].astype(bf16)
 
 
-def into_rows(scal, near, far, win, mate_win, panel, table, cells, saved):
+def into_rows(scal, near, far, win, mate_win, panel, table, indices, sources, saved):
     first_iteration = saved is None
     outs = [
         jax.ShapeDtypeStruct((CHIPS, 2, RHS, TILE), f32),
@@ -349,11 +371,13 @@
     if first_iteration:
         outs += [pltpu.HBM(state, f32), pltpu.HBM(coefs, f32)]
         out_specs += [ANY, ANY]
-        in_specs += [SMEM, VMEM]
-        args += [table, cells]
+        in_specs += [SMEM, ANY, ANY]
+        args += [table, in_hbm(indices), in_hbm(sources)]
     else:
         in_specs += [ANY, ANY]
         args += [in_hbm(x) for x in saved]
+    cells = (LAYERS, MID * LANES)
+    lines = [pltpu.VMEM(cells, jnp.int32), pltpu.VMEM(cells, f32)] if first_iteration else []
     return pl.pallas_call(
         functools.partial(rows_body, first_iteration),
         out_shape=outs,
@@ -369,6 +393,8 @@
             pltpu.SemaphoreType.DMA((2,)),
             pltpu.VMEM((SLOTS, TILE, TILE), bf16),
             pltpu.SemaphoreType.DMA((SLOTS,)),
+            pltpu.VMEM((WIN_TILES, RHS, TILE), bf16),
+            *lines,
         ],
         compiler_params=pltpu.CompilerParams(vmem_limit_bytes=44 * MIB),
         cost_estimate=pl.CostEstimate(flops=7 * 10**8, transcendentals=0, bytes_accessed=30 * 10**6),
@@ -442,17 +468,9 @@
     )(parts, traces, load)
 
 
-def lookup(indices, table):
-    levels = jnp.arange(table.shape[0], dtype=jnp.int32)
-    return jnp.sum(jnp.where(indices[..., None] == levels, table, 0.0), axis=-1)
-
-
-def volume_cells(coef_index, coef_table, vol_source, volume_line):
+def volume_edges(coef_index, vol_source, volume_line):
     indices = lax.dynamic_index_in_dim(coef_index, volume_line, 0, keepdims=False)
     source = lax.dynamic_index_in_dim(vol_source, volume_line, 0, keepdims=False)
-    spare = ((0, 0), (0, 8 - LAYERS), (0, 0), (0, 0))
-    cells = jnp.stack([lookup(indices, coef_table), source]).reshape(2, LAYERS, MID, LANES)
-    cells = jnp.pad(cells, spare).transpose(2, 0, 1, 3)
 
     def ends(x):
         return jnp.concatenate([x[:, :LANES], x[:, -LANES:]], 1)
@@ -460,7 +478,7 @@
     high = ends(source).astype(bf16)
     low = (ends(source) - high.astype(f32)).astype(bf16)
     edges = [jnp.pad(e, ((0, 4), (0, 0))) for e in (ends(indices).astype(bf16), high, low)]
-    return cells, jnp.pad(jnp.concatenate(edges, 0), ((0, 8), (0, 0)))
+    return jnp.pad(jnp.concatenate(edges, 0), ((0, 8), (0, 0)))
 
 
 def local(
@@ -483,13 +501,13 @@
         core,
         core,
         jnp.where(is_volume, 1 - core, core),
+        volume_line,
     ]
     scal = jnp.concatenate([tile_list, jnp.stack([x.astype(jnp.int32) for x in own])])
     traces = trace_start
     spread = spread_start(traces)
-    cells, edges = volume_cells(coef_index, coef_table, vol_source, volume_line)
+    edges = volume_edges(coef_index, vol_source, volume_line)
     panel = in_hbm(panel_tiles)
-    cells, edges = lax.optimization_barrier((cells, edges))
     saved = None
     for iteration in range(ITERS):
         last = iteration == ITERS - 1
@@ -503,7 +521,7 @@
         mate_win = from_mate(win)
         parts = exchange(win_part.reshape(N_ROW, 2, RHS, TILE), "row")
         own, mate, *saved = into_rows(
-            scal, near, far, win, mate_win, panel, coef_table, cells, saved
+            scal, near, far, win, mate_win, panel, coef_table, coef_index, vol_source, saved
         )
         got = from_mate(mate)
         share = window_share(parts)

time: 147 us -> 144 us (0.980)
  waiting for transfers between devices: 11.2 us -> 9.51 us
  local copies, waits for them, and re-layouts: 4.17 us -> 2.51 us
    all_to_all x1, waiting for transfers between devices: 7.14 us -> 5.21 us  [between_chips(): return lax.all_to_all(x, 'col', 0, 0, axis_index_groups=groups, tiled=True)]
    unnamed x12 -> x8, local copies, waits for them, and re-layouts: 2.56 us -> 0.91 us
  transfers between devices with their start and end apart: 13 -> 13, of which waited for: 4 -> 5; matrix products, arithmetic and copies ran while one was open for 3% -> 3% of each run, Pallas kernels for 29% -> 30%
where the time goes in v6:
time: 144 us; the launch traced here: 143 us
  Pallas kernels  48.3 us (34%)
  starting transfers between devices  40.5 us (28%)
  blocking collectives  36.9 us (26%)
  waiting for transfers between devices  9.51 us (7%)
  between operations  2.75 us (2%)
  local copies, waits for them, and re-layouts  2.51 us (2%)
  other arithmetic  2.18 us (2%)
    all_to_all x3, blocking collectives, between_chips(): return lax.all_to_all(x, 'col', 0, 0, axis_index_groups=groups, tiled=True)  36.9 us
    all_to_all x4, starting transfers between devices, exchange(): return lax.all_to_all(x, axis, 0, 0, tiled=True)  27.7 us
    pallas_call x2, Pallas kernels, into_rows(): pl.pallas_call(functools.partial(rows_body, first_iteration), out_shape=o...  22.9 us
    pallas_call x2, Pallas kernels, into_window(): pl.pallas_call(window_body, out_shape=jax.ShapeDtypeStruct((WIN_TILES, RH...  19.7 us
    ppermute x8, starting transfers between devices, from_mate(): return lax.ppermute(x, 'col', [(i, i ^ 1) for i in range(N_COL)])  6.42 us
    all_to_all x1, starting transfers between devices, between_chips(): return lax.all_to_all(x, 'col', 0, 0, axis_index_groups=groups, tiled=True)  6.37 us
    all_to_all x1, waiting for transfers between devices, between_chips(): return lax.all_to_all(x, 'col', 0, 0, axis_index_groups=groups, tiled=True)  5.21 us
    ppermute x8, waiting for transfers between devices, from_mate(): return lax.ppermute(x, 'col', [(i, i ^ 1) for i in range(N_COL)])  4.29 us
  transfers between devices with their start and end apart: 13, of which 5 were waited for; matrix products, arithmetic and copies ran while one was open for 3% of the time, Pallas kernels for 30%

profile of v6, /device:TPU:1, one launch (start us, length us, event | category | flops | bytes accessed | tf_op | source)
XLA Modules:
  0.0 142.7 jit_solution(11045394634167301462)
XLA Ops:
  0.6 0.9 copy-done
  1.5 0.8 spread_start.1
  2.4 6.4 %all-to-all-start = ((bf16[8,2,32,512]{3,2,1,0:T(8,128)(2,1)}), bf16[8,2,32,512]{3,2,1,0:T(8,128)(2,1)S(1)}, u32[]{:S(2)}, u32[]{:S(2)}) async-start(bf16[8,2,32,512]{3,2,1,0:T(8,128)(2,1)} %spread_start.1), calls=%async_computation | async-start | bytes 1048576 | tf_op jit(solution)/shard_map/all_to_all | solution.py:53
  9.6 1.3 fusion.10
  12.9 0.9 fusion
  13.7 5.2 %all-to-all-done = bf16[8,2,32,512]{3,2,1,0:T(8,128)(2,1)S(1)} async-done(((bf16[8,2,32,512]{3,2,1,0:T(8,128)(2,1)}), bf16[8,2,32,512]{3,2,1,0:T(8,128)(2,1)S(1)}, u32[]{:S(2)}, u32[]{:S(2)}) %all-to-all-start) | async-done | bytes 524320 | tf_op jit(solution)/shard_map/all_to_all | solution.py:53
  19.0 0.8 collective-permute-start
  21.3 1.3 spread_row.2
  22.6 7.0 %all-to-all-start.1 = ((bf16[8,32,512]{2,1,0:T(8,128)(2,1)}), bf16[8,32,512]{2,1,0:T(8,128)(2,1)S(1)}, u32[]{:S(2)}, u32[]{:S(2)}) async-start(bf16[8,32,512]{2,1,0:T(8,128)(2,1)} %spread_row.2), calls=%async_computation.1 | async-start | bytes 524288 | tf_op jit(solution)/shard_map/all_to_all | solution.py:48
  29.7 9.9 %into_window.2 = bf16[16,32,512]{2,1,0:T(8,128)(2,1)} custom-call(s32[52]{0:T(128)S(1)} %concatenate.14.scal_ref, bf16[16,32,512]{2,1,0:T(8,128)(2,1)S(1)} %bitcast.19, bf16[16,32,512]{2,1,0:T(8,128)(2,1)S(1)} %bitcast.25, bf16[43,512,512]{2,1,0:T(8,128)(2,1)} %panel_ref.7), custom_call_target="tpu_custom_call" | custom-call | flops 700000000 | bytes 25000000 | tf_op jit(solution)/shard_map/into_window/pallas_call | solution.py:174
  40.3 6.9 %all-to-all-start.2 = ((bf16[8,2,32,512]{3,2,1,0:T(8,128)(2,1)}), bf16[8,2,32,512]{3,2,1,0:T(8,128)(2,1)S(1)}, u32[]{:S(2)}, u32[]{:S(2)}) async-start(bf16[8,2,32,512]{3,2,1,0:T(8,128)(2,1)} %bitcast.12), calls=%async_computation.2 | async-start | bytes 1048576 | tf_op jit(solution)/shard_map/all_to_all | solution.py:48
  47.2 11.4 %into_rows_first.1 = (f32[8,2,32,512]{3,2,1,0:T(8,128)S(1)}, bf16[8,2,32,512]{3,2,1,0:T(8,128)(2,1)}, f32[36,4,32,128]{3,2,1,0:T(8,128)}, f32[34,48,128]{2,1,0:T(8,128)}) custom-call(s32[52]{0:T(128)S(1)} %concatenate.14.scal_ref, bf16[16,32,512]{2,1,0:T(8,128)(2,1)S(1)} %bitcast.20, bf16[16,32,512]{2,1,0:T(8,128)(2,1)S(1)} %bitcast.26, ...), custom_call_target="tpu_custom_call" | custom-call | flops 700000000 | bytes 30000000 | tf_op jit(solution)/shard_map/into_rows_first/pallas_call | solution.py:381
  59.9 1.0 collective-permute-done.3.got_share_ref
  61.5 12.6 %all_to_all.40.parts_ref = bf16[8,2,32,512]{3,2,1,0:T(8,128)(2,1)S(1)} all-to-all(bf16[8,2,32,512]{3,2,1,0:T(8,128)(2,1)S(1)} %pair_sum.2), channel_id=1, replica_groups={{0,16,32,48,64,80,96,112},{8,24,40,56,72,88,104,120},{1,17,33,49,65,81,..., dimensions={0} | all-to-all | bytes 1048576 | tf_op jit(solution)/shard_map/all_to_all | solution.py:53
  74.3 11.6 %all_to_all.41 = bf16[8,2,32,512]{3,2,1,0:T(8,128)(2,1)S(1)} all-to-all(bf16[8,2,32,512]{3,2,1,0:T(8,128)(2,1)S(1)} %get-tuple-element.15), channel_id=1, replica_groups={{0,16,32,48,64,80,96,112},{8,24,40,56,72,88,104,120},{1,17,33,49,65,81,..., dimensions={0} | all-to-all | bytes 1048576 | tf_op jit(solution)/shard_map/all_to_all | solution.py:53
  85.9 1.8 %collective-permute-start.4 = (bf16[8,2,32,512]{3,2,1,0:T(8,128)(2,1)S(1)}, bf16[8,2,32,512]{3,2,1,0:T(8,128)(2,1)S(1)}, u32[]{:S(2)}, u32[]{:S(2)}) collective-permute-start(bf16[8,2,32,512]{3,2,1,0:T(8,128)(2,1)S(1)} %all_to_all.41), channel_id=1, source_target_pairs={{0,8},{8,0},{16,24},{24,16},{32,40},{40,32},{48,56},{56,48},{64,72... | collective-permute-start | bytes 1572872 | tf_op jit(solution)/shard_map/ppermute | solution.py:57
  87.7 1.5 %collective-permute-done.4 = bf16[8,2,32,512]{3,2,1,0:T(8,128)(2,1)S(1)} collective-permute-done((bf16[8,2,32,512]{3,2,1,0:T(8,128)(2,1)S(1)}, bf16[8,2,32,512]{3,2,1,0:T(8,128)(2,1)S(1)}, u32[]{:S(2)}, u32[]{:S(2)}) %collective-permute-start.4) | collective-permute-done | bytes 524320 | tf_op jit(solution)/shard_map/ppermute | solution.py:57
  89.3 1.3 spread_row.3
  90.5 6.8 %all-to-all-start.5 = ((bf16[8,32,512]{2,1,0:T(8,128)(2,1)}), bf16[8,32,512]{2,1,0:T(8,128)(2,1)S(1)}, u32[]{:S(2)}, u32[]{:S(2)}) async-start(bf16[8,32,512]{2,1,0:T(8,128)(2,1)} %spread_row.3), calls=%async_computation.5 | async-start | bytes 524288 | tf_op jit(solution)/shard_map/all_to_all | solution.py:48
  97.4 9.9 %into_window.3 = bf16[16,32,512]{2,1,0:T(8,128)(2,1)} custom-call(s32[52]{0:T(128)S(1)} %concatenate.14.scal_ref, bf16[16,32,512]{2,1,0:T(8,128)(2,1)S(1)} %bitcast.22, bf16[16,32,512]{2,1,0:T(8,128)(2,1)S(1)} %bitcast.28, bf16[43,512,512]{2,1,0:T(8,128)(2,1)} %panel_ref.7), custom_call_target="tpu_custom_call" | custom-call | flops 700000000 | bytes 25000000 | tf_op jit(solution)/shard_map/into_window/pallas_call | solution.py:174
  108.0 6.9 %all-to-all-start.6 = ((bf16[8,2,32,512]{3,2,1,0:T(8,128)(2,1)}), bf16[8,2,32,512]{3,2,1,0:T(8,128)(2,1)S(1)}, u32[]{:S(2)}, u32[]{:S(2)}) async-start(bf16[8,2,32,512]{3,2,1,0:T(8,128)(2,1)} %bitcast.15), calls=%async_computation.6 | async-start | bytes 1048576 | tf_op jit(solution)/shard_map/all_to_all | solution.py:48
  114.9 11.5 %into_rows_next.1 = (f32[8,2,32,512]{3,2,1,0:T(8,128)S(1)}, bf16[8,2,32,512]{3,2,1,0:T(8,128)(2,1)}) custom-call(s32[52]{0:T(128)S(1)} %concatenate.14.scal_ref, bf16[16,32,512]{2,1,0:T(8,128)(2,1)S(1)} %bitcast.23, bf16[16,32,512]{2,1,0:T(8,128)(2,1)S(1)} %bitcast.29, bf16[8,32,512]{2,1,0:T(8,128)(2,1)S(1)} %all-to-all-done.5.win_ref, ...), custom_call_target="tpu_custom_call" | custom-call | flops 700000000 | bytes 30000000 | tf_op jit(solution)/shard_map/into_rows_next/pallas_call | solution.py:381
  127.6 1.0 collective-permute-done.7.got_share_ref
  129.3 12.6 %all_to_all.42.parts_ref = bf16[8,2,32,512]{3,2,1,0:T(8,128)(2,1)S(1)} all-to-all(bf16[8,2,32,512]{3,2,1,0:T(8,128)(2,1)S(1)} %pair_sum.3), channel_id=1, replica_groups={{0,16,32,48,64,80,96,112},{8,24,40,56,72,88,104,120},{1,17,33,49,65,81,..., dimensions={0} | all-to-all | bytes 1048576 | tf_op jit(solution)/shard_map/all_to_all | solution.py:53
  (37 shorter events, 8.5 us)
Async XLA Ops:
  0.6 0.9 copy-start
  1.5 45.7 %copy-start.3 = (f32[16]{0:T(128)S(1)}, f32[16]{0:T(128)}, u32[]{:S(2)}) copy-start(f32[16]{0:T(128)} %refs_0_.1) | copy-start | bytes 196
  2.4 16.6 %all-to-all-start = ((bf16[8,2,32,512]{3,2,1,0:T(8,128)(2,1)}), bf16[8,2,32,512]{3,2,1,0:T(8,128)(2,1)S(1)}, u32[]{:S(2)}, u32[]{:S(2)}) async-start(bf16[8,2,32,512]{3,2,1,0:T(8,128)(2,1)} %spread_start.1), calls=%async_computation | async-start | bytes 1048576 | tf_op jit(solution)/shard_map/all_to_all | solution.py:53
  19.0 2.4 %collective-permute-start = (bf16[8,2,32,512]{3,2,1,0:T(8,128)(2,1)S(1)}, bf16[8,2,32,512]{3,2,1,0:T(8,128)(2,1)S(1)}, u32[]{:S(2)}, u32[]{:S(2)}) collective-permute-start(bf16[8,2,32,512]{3,2,1,0:T(8,128)(2,1)S(1)} %all-to-all-done), channel_id=1, source_target_pairs={{0,8},{8,0},{16,24},{24,16},{32,40},{40,32},{48,56},{56,48},{64,72... | collective-permute-start | bytes 1572872 | tf_op jit(solution)/shard_map/ppermute | solution.py:57
  22.6 16.9 %all-to-all-start.1 = ((bf16[8,32,512]{2,1,0:T(8,128)(2,1)}), bf16[8,32,512]{2,1,0:T(8,128)(2,1)S(1)}, u32[]{:S(2)}, u32[]{:S(2)}) async-start(bf16[8,32,512]{2,1,0:T(8,128)(2,1)} %spread_row.2), calls=%async_computation.1 | async-start | bytes 524288 | tf_op jit(solution)/shard_map/all_to_all | solution.py:48
  29.7 44.5 %copy-start.1 = (f32[32,1024]{1,0:T(8,128)S(1)}, f32[32,1024]{1,0:T(8,128)}, u32[]{:S(2)}) copy-start(f32[32,1024]{1,0:T(8,128)} %trace_ref.3) | copy-start | bytes 393220
  29.7 44.5 %copy-start.2 = (f32[32,1024]{1,0:T(8,128)S(1)}, f32[32,1024]{1,0:T(8,128)}, u32[]{:S(2)}) copy-start(f32[32,1024]{1,0:T(8,128)} %load_ref.3) | copy-start | bytes 393220
  39.6 7.7 %collective-permute-start.1 = (bf16[8,32,512]{2,1,0:T(8,128)(2,1)S(1)}, bf16[8,32,512]{2,1,0:T(8,128)(2,1)S(1)}, u32[]{:S(2)}, u32[]{:S(2)}) collective-permute-start(bf16[8,32,512]{2,1,0:T(8,128)(2,1)S(1)} %all-to-all-done.1.win_ref), channel_id=1, source_target_pairs={{0,8},{8,0},{16,24},{24,16},{32,40},{40,32},{48,56},{56,48},{64,72... | collective-permute-start | bytes 786440 | tf_op jit(solution)/shard_map/ppermute | solution.py:57
  40.3 18.7 %all-to-all-start.2 = ((bf16[8,2,32,512]{3,2,1,0:T(8,128)(2,1)}), bf16[8,2,32,512]{3,2,1,0:T(8,128)(2,1)S(1)}, u32[]{:S(2)}, u32[]{:S(2)}) async-start(bf16[8,2,32,512]{3,2,1,0:T(8,128)(2,1)} %bitcast.12), calls=%async_computation.2 | async-start | bytes 1048576 | tf_op jit(solution)/shard_map/all_to_all | solution.py:48
  58.7 2.2 %collective-permute-start.2 = (bf16[8,2,32,512]{3,2,1,0:T(8,128)(2,1)}, bf16[8,2,32,512]{3,2,1,0:T(8,128)(2,1)S(1)}, u32[]{:S(2)}, u32[]{:S(2)}) collective-permute-start(bf16[8,2,32,512]{3,2,1,0:T(8,128)(2,1)} %get-tuple-element.14), channel_id=1, source_target_pairs={{0,8},{8,0},{16,24},{24,16},{32,40},{40,32},{48,56},{56,48},{64,72... | collective-permute-start | bytes 1572872 | tf_op jit(solution)/shard_map/ppermute | solution.py:57
  59.1 1.8 %collective-permute-start.3 = (f32[2,32,512]{2,1,0:T(8,128)S(1)}, f32[2,32,512]{2,1,0:T(8,128)S(1)}, u32[]{:S(2)}, u32[]{:S(2)}) collective-permute-start(f32[2,32,512]{2,1,0:T(8,128)S(1)} %window_share.2.share_ref), channel_id=1, source_target_pairs={{0,8},{8,0},{16,24},{24,16},{32,40},{40,32},{48,56},{56,48},{64,72... | collective-permute-start | bytes 393224 | tf_op jit(solution)/shard_map/ppermute | solution.py:57
  85.9 3.4 %collective-permute-start.4 = (bf16[8,2,32,512]{3,2,1,0:T(8,128)(2,1)S(1)}, bf16[8,2,32,512]{3,2,1,0:T(8,128)(2,1)S(1)}, u32[]{:S(2)}, u32[]{:S(2)}) collective-permute-start(bf16[8,2,32,512]{3,2,1,0:T(8,128)(2,1)S(1)} %all_to_all.41), channel_id=1, source_target_pairs={{0,8},{8,0},{16,24},{24,16},{32,40},{40,32},{48,56},{56,48},{64,72... | collective-permute-start | bytes 1572872 | tf_op jit(solution)/shard_map/ppermute | solution.py:57
  90.5 16.7 %all-to-all-start.5 = ((bf16[8,32,512]{2,1,0:T(8,128)(2,1)}), bf16[8,32,512]{2,1,0:T(8,128)(2,1)S(1)}, u32[]{:S(2)}, u32[]{:S(2)}) async-start(bf16[8,32,512]{2,1,0:T(8,128)(2,1)} %spread_row.3), calls=%async_computation.5 | async-start | bytes 524288 | tf_op jit(solution)/shard_map/all_to_all | solution.py:48
  107.3 7.7 %collective-permute-start.5 = (bf16[8,32,512]{2,1,0:T(8,128)(2,1)S(1)}, bf16[8,32,512]{2,1,0:T(8,128)(2,1)S(1)}, u32[]{:S(2)}, u32[]{:S(2)}) collective-permute-start(bf16[8,32,512]{2,1,0:T(8,128)(2,1)S(1)} %all-to-all-done.5.win_ref), channel_id=1, source_target_pairs={{0,8},{8,0},{16,24},{24,16},{32,40},{40,32},{48,56},{56,48},{64,72... | collective-permute-start | bytes 786440 | tf_op jit(solution)/shard_map/ppermute | solution.py:57
  108.0 18.8 %all-to-all-start.6 = ((bf16[8,2,32,512]{3,2,1,0:T(8,128)(2,1)}), bf16[8,2,32,512]{3,2,1,0:T(8,128)(2,1)S(1)}, u32[]{:S(2)}, u32[]{:S(2)}) async-start(bf16[8,2,32,512]{3,2,1,0:T(8,128)(2,1)} %bitcast.15), calls=%async_computation.6 | async-start | bytes 1048576 | tf_op jit(solution)/shard_map/all_to_all | solution.py:48
  126.4 2.2 %collective-permute-start.6 = (bf16[8,2,32,512]{3,2,1,0:T(8,128)(2,1)}, bf16[8,2,32,512]{3,2,1,0:T(8,128)(2,1)S(1)}, u32[]{:S(2)}, u32[]{:S(2)}) collective-permute-start(bf16[8,2,32,512]{3,2,1,0:T(8,128)(2,1)} %get-tuple-element.20), channel_id=1, source_target_pairs={{0,8},{8,0},{16,24},{24,16},{32,40},{40,32},{48,56},{56,48},{64,72... | collective-permute-start | bytes 1572872 | tf_op jit(solution)/shard_map/ppermute | solution.py:57
  126.9 1.7 %collective-permute-start.7 = (f32[2,32,512]{2,1,0:T(8,128)S(1)}, f32[2,32,512]{2,1,0:T(8,128)S(1)}, u32[]{:S(2)}, u32[]{:S(2)}) collective-permute-start(f32[2,32,512]{2,1,0:T(8,128)S(1)} %window_share.3.share_ref), channel_id=1, source_target_pairs={{0,8},{8,0},{16,24},{24,16},{32,40},{40,32},{48,56},{56,48},{64,72... | collective-permute-start | bytes 393224 | tf_op jit(solution)/shard_map/ppermute | solution.py:57

commit v7 on v6

--- a/solution.py
+++ b/solution.py
@@ -24,7 +24,7 @@
 DENSE_COLS = 12
 LAYERS = 4
 SLOTS = 43
-GROUP = 4
+GROUP = 6
 UNROLL = 17
 COEFS = 16
 BAND_TILES = 32
@@ -61,37 +61,48 @@
     return jnp.where(is_far == 0, near_ref[index], far_ref[index])
 
 
-def start_body(trace_ref, out_ref):
+def send_copies(block_ref, out_ref, sems):
+    copies = [
+        pltpu.make_async_copy(block_ref, out_ref.at[peer], sems.at[peer])
+        for peer in range(out_ref.shape[0])
+    ]
+    for copy in copies:
+        copy.start()
+    for copy in copies:
+        copy.wait()
+
+
+def start_body(trace_ref, out_ref, block_ref, sems):
     for half in range(2):
-        rounded = trace_ref[:, half * TILE : (half + 1) * TILE].astype(bf16)
-        for copy in range(CHIPS):
-            out_ref[copy, half] = rounded
+        block_ref[half] = trace_ref[:, half * TILE : (half + 1) * TILE].astype(bf16)
+    send_copies(block_ref, out_ref, sems)
 
 
 def spread_start(trace_start):
     return pl.pallas_call(
         start_body,
-        out_shape=jax.ShapeDtypeStruct((CHIPS, 2, RHS, TILE), bf16),
+        out_shape=pltpu.HBM((CHIPS, 2, RHS, TILE), bf16),
         in_specs=[VMEM],
-        out_specs=VMEM,
+        out_specs=ANY,
+        scratch_shapes=[pltpu.VMEM((2, RHS, TILE), bf16), pltpu.SemaphoreType.DMA((CHIPS,))],
         compiler_params=pltpu.CompilerParams(vmem_limit_bytes=6 * MIB),
         name="spread_start",
     )(trace_start)
 
 
 def row_body(first_iteration, scal_ref, near_ref, far_ref, *refs):
-    out_ref = refs[-1]
+    out_ref, block_ref, sems = refs[-3:]
     mine = pick(near_ref, far_ref, scal_ref[SLOTS + 5], scal_ref[SLOTS + 1])
     tail = pick(near_ref, far_ref, scal_ref[SLOTS + 7], scal_ref[SLOTS + 2])
-    for peer in range(N_ROW):
-        out_ref[peer, :, : 3 * LANES] = mine[:, : 3 * LANES]
-        out_ref[peer, :, 3 * LANES :] = tail[:, 3 * LANES :]
+    block_ref[:, : 3 * LANES] = mine[:, : 3 * LANES]
+    block_ref[:, 3 * LANES :] = tail[:, 3 * LANES :]
     if first_iteration:
 
         @pl.when(scal_ref[SLOTS] == 1)
         def _():
-            for peer in range(N_ROW):
-                out_ref[peer, :, LANES : 3 * LANES] = refs[0][...]
+            block_ref[:, LANES : 3 * LANES] = refs[0][...]
+
+    send_copies(block_ref, out_ref, sems)
 
 
 def spread_row(scal, near, far, edges):
@@ -99,9 +110,10 @@
     args = [scal, near, far] + ([edges] if first_iteration else [])
     return pl.pallas_call(
         functools.partial(row_body, first_iteration),
-        out_shape=jax.ShapeDtypeStruct((N_ROW, RHS, TILE), bf16),
+        out_shape=pltpu.HBM((N_ROW, RHS, TILE), bf16),
         in_specs=[SMEM] + [VMEM] * (len(args) - 1),
-        out_specs=VMEM,
+        out_specs=ANY,
+        scratch_shapes=[pltpu.VMEM((RHS, TILE), bf16), pltpu.SemaphoreType.DMA((N_ROW,))],
         compiler_params=pltpu.CompilerParams(vmem_limit_bytes=6 * MIB),
         name="spread_row",
     )(*args)
@@ -288,9 +300,10 @@
     else:
         state_in, coef_in, own_out, mate_out = refs[:4]
         refs = refs[4:]
-    band_acc, state_a, state_b, coef_ref, cell_ref, top_ref, sems, buffer_ref, panel_sems, traces_ref = refs[:10]
+    band_acc, state_a, state_b, coef_ref, cell_ref, top_ref, sems, buffer_ref, panel_sems = refs[:9]
+    traces_ref, mate_ref, mate_sems = refs[9:12]
     if first_iteration:
-        index_ref, source_ref = refs[10:]
+        index_ref, source_ref = refs[12:]
     is_volume = scal_ref[SLOTS] == 1
     core = scal_ref[SLOTS + 6]
 
@@ -352,18 +365,25 @@
             for save in saves:
                 save.wait()
 
+    def leave(chip):
+        return pltpu.make_async_copy(mate_ref.at[chip], mate_out.at[chip], mate_sems.at[chip])
+
+    for chip in range(CHIPS):
+        mate_ref[chip] = band_acc[pl.ds(4 * chip + 2 - 2 * core, 2)].astype(bf16)
+        leave(chip).start()
     for chip in range(CHIPS):
         own_out[chip] = band_acc[pl.ds(4 * chip + 2 * core, 2)]
-        mate_out[chip] = band_acc[pl.ds(4 * chip + 2 - 2 * core, 2)].astype(bf16)
+    for chip in range(CHIPS):
+        leave(chip).wait()
 
 
 def into_rows(scal, near, far, win, mate_win, panel, table, indices, sources, saved):
     first_iteration = saved is None
     outs = [
         jax.ShapeDtypeStruct((CHIPS, 2, RHS, TILE), f32),
-        jax.ShapeDtypeStruct((CHIPS, 2, RHS, TILE), bf16),
+        pltpu.HBM((CHIPS, 2, RHS, TILE), bf16),
     ]
-    out_specs = [VMEM, VMEM]
+    out_specs = [VMEM, ANY]
     in_specs = [SMEM, VMEM, VMEM, VMEM, VMEM, ANY]
     args = [scal, near, far, win, mate_win, panel]
     state = (EXT + 2, LAYERS, RHS, LANES)
@@ -394,6 +414,8 @@
             pltpu.VMEM((SLOTS, TILE, TILE), bf16),
             pltpu.SemaphoreType.DMA((SLOTS,)),
             pltpu.VMEM((WIN_TILES, RHS, TILE), bf16),
+            pltpu.VMEM((CHIPS, 2, RHS, TILE), bf16),
+            pltpu.SemaphoreType.DMA((CHIPS,)),
             *lines,
         ],
         compiler_params=pltpu.CompilerParams(vmem_limit_bytes=44 * MIB),

time: 144 us -> 144 us (level)
  transfers between devices with their start and end apart: 13 -> 13, of which waited for: 5 -> 7; matrix products, arithmetic and copies ran while one was open for 3% -> 3% of each run, Pallas kernels for 30% -> 30%
where the time goes in v7:
time: 144 us; the launch traced here: 143 us
  Pallas kernels  48.2 us (33%)
  starting transfers between devices  40.4 us (28%)
  blocking collectives  36.9 us (26%)
  waiting for transfers between devices  9.84 us (7%)
  between operations  2.77 us (2%)
  local copies, waits for them, and re-layouts  2.51 us (2%)
  other arithmetic  2.18 us (2%)
    all_to_all x3, blocking collectives, between_chips(): return lax.all_to_all(x, 'col', 0, 0, axis_index_groups=groups, tiled=True)  36.9 us
    all_to_all x4, starting transfers between devices, exchange(): return lax.all_to_all(x, axis, 0, 0, tiled=True)  27.5 us
    pallas_call x2, Pallas kernels, into_rows(): pl.pallas_call(functools.partial(rows_body, first_iteration), out_shape=o...  22.4 us
    pallas_call x2, Pallas kernels, into_window(): pl.pallas_call(window_body, out_shape=jax.ShapeDtypeStruct((WIN_TILES, RH...  19.9 us
    ppermute x8, starting transfers between devices, from_mate(): return lax.ppermute(x, 'col', [(i, i ^ 1) for i in range(N_COL)])  6.57 us
    all_to_all x1, starting transfers between devices, between_chips(): return lax.all_to_all(x, 'col', 0, 0, axis_index_groups=groups, tiled=True)  6.39 us
    all_to_all x1, waiting for transfers between devices, between_chips(): return lax.all_to_all(x, 'col', 0, 0, axis_index_groups=groups, tiled=True)  5.21 us
    ppermute x8, waiting for transfers between devices, from_mate(): return lax.ppermute(x, 'col', [(i, i ^ 1) for i in range(N_COL)])  4.26 us
  transfers between devices with their start and end apart: 13, of which 7 were waited for; matrix products, arithmetic and copies ran while one was open for 3% of the time, Pallas kernels for 30%

profile of v7, /device:TPU:1, one launch (start us, length us, event | category | flops | bytes accessed | tf_op | source)
XLA Modules:
  0.0 142.8 jit_solution(11015771876646603501)
XLA Ops:
  0.6 0.9 copy-done
  1.5 0.9 spread_start.1
  2.4 6.4 %all-to-all-start = ((bf16[8,2,32,512]{3,2,1,0:T(8,128)(2,1)}), bf16[8,2,32,512]{3,2,1,0:T(8,128)(2,1)S(1)}, u32[]{:S(2)}, u32[]{:S(2)}) async-start(bf16[8,2,32,512]{3,2,1,0:T(8,128)(2,1)} %spread_start.1), calls=%async_computation | async-start | bytes 1048576 | tf_op jit(solution)/shard_map/all_to_all | solution.py:53
  9.7 1.3 fusion.10
  12.9 0.9 fusion
  13.8 5.2 %all-to-all-done = bf16[8,2,32,512]{3,2,1,0:T(8,128)(2,1)S(1)} async-done(((bf16[8,2,32,512]{3,2,1,0:T(8,128)(2,1)}), bf16[8,2,32,512]{3,2,1,0:T(8,128)(2,1)S(1)}, u32[]{:S(2)}, u32[]{:S(2)}) %all-to-all-start) | async-done | bytes 524320 | tf_op jit(solution)/shard_map/all_to_all | solution.py:53
  19.0 0.8 collective-permute-start
  21.4 1.3 spread_row.2
  22.7 7.1 %all-to-all-start.1 = ((bf16[8,32,512]{2,1,0:T(8,128)(2,1)}), bf16[8,32,512]{2,1,0:T(8,128)(2,1)S(1)}, u32[]{:S(2)}, u32[]{:S(2)}) async-start(bf16[8,32,512]{2,1,0:T(8,128)(2,1)} %spread_row.2), calls=%async_computation.1 | async-start | bytes 524288 | tf_op jit(solution)/shard_map/all_to_all | solution.py:48
  29.8 9.9 %into_window.2 = bf16[16,32,512]{2,1,0:T(8,128)(2,1)} custom-call(s32[52]{0:T(128)S(1)} %concatenate.14.scal_ref, bf16[16,32,512]{2,1,0:T(8,128)(2,1)S(1)} %bitcast.19, bf16[16,32,512]{2,1,0:T(8,128)(2,1)S(1)} %bitcast.25, bf16[43,512,512]{2,1,0:T(8,128)(2,1)} %panel_ref.7), custom_call_target="tpu_custom_call" | custom-call | flops 700000000 | bytes 25000000 | tf_op jit(solution)/shard_map/into_window/pallas_call | solution.py:186
  40.5 6.9 %all-to-all-start.2 = ((bf16[8,2,32,512]{3,2,1,0:T(8,128)(2,1)}), bf16[8,2,32,512]{3,2,1,0:T(8,128)(2,1)S(1)}, u32[]{:S(2)}, u32[]{:S(2)}) async-start(bf16[8,2,32,512]{3,2,1,0:T(8,128)(2,1)} %bitcast.12), calls=%async_computation.2 | async-start | bytes 1048576 | tf_op jit(solution)/shard_map/all_to_all | solution.py:48
  47.4 11.2 %into_rows_first.1 = (f32[8,2,32,512]{3,2,1,0:T(8,128)S(1)}, bf16[8,2,32,512]{3,2,1,0:T(8,128)(2,1)}, f32[36,4,32,128]{3,2,1,0:T(8,128)}, f32[34,48,128]{2,1,0:T(8,128)}) custom-call(s32[52]{0:T(128)S(1)} %concatenate.14.scal_ref, bf16[16,32,512]{2,1,0:T(8,128)(2,1)S(1)} %bitcast.20, bf16[16,32,512]{2,1,0:T(8,128)(2,1)S(1)} %bitcast.26, ...), custom_call_target="tpu_custom_call" | custom-call | flops 700000000 | bytes 30000000 | tf_op jit(solution)/shard_map/into_rows_first/pallas_call | solution.py:401
  60.1 1.0 collective-permute-done.3.got_share_ref
  61.8 12.6 %all_to_all.40.parts_ref = bf16[8,2,32,512]{3,2,1,0:T(8,128)(2,1)S(1)} all-to-all(bf16[8,2,32,512]{3,2,1,0:T(8,128)(2,1)S(1)} %pair_sum.2), channel_id=1, replica_groups={{0,16,32,48,64,80,96,112},{8,24,40,56,72,88,104,120},{1,17,33,49,65,81,..., dimensions={0} | all-to-all | bytes 1048576 | tf_op jit(solution)/shard_map/all_to_all | solution.py:53
  74.5 11.6 %all_to_all.41 = bf16[8,2,32,512]{3,2,1,0:T(8,128)(2,1)S(1)} all-to-all(bf16[8,2,32,512]{3,2,1,0:T(8,128)(2,1)S(1)} %get-tuple-element.15), channel_id=1, replica_groups={{0,16,32,48,64,80,96,112},{8,24,40,56,72,88,104,120},{1,17,33,49,65,81,..., dimensions={0} | all-to-all | bytes 1048576 | tf_op jit(solution)/shard_map/all_to_all | solution.py:53
  86.1 1.8 %collective-permute-start.4 = (bf16[8,2,32,512]{3,2,1,0:T(8,128)(2,1)S(1)}, bf16[8,2,32,512]{3,2,1,0:T(8,128)(2,1)S(1)}, u32[]{:S(2)}, u32[]{:S(2)}) collective-permute-start(bf16[8,2,32,512]{3,2,1,0:T(8,128)(2,1)S(1)} %all_to_all.41), channel_id=1, source_target_pairs={{0,8},{8,0},{16,24},{24,16},{32,40},{40,32},{48,56},{56,48},{64,72... | collective-permute-start | bytes 1572872 | tf_op jit(solution)/shard_map/ppermute | solution.py:57
  88.0 1.5 %collective-permute-done.4 = bf16[8,2,32,512]{3,2,1,0:T(8,128)(2,1)S(1)} collective-permute-done((bf16[8,2,32,512]{3,2,1,0:T(8,128)(2,1)S(1)}, bf16[8,2,32,512]{3,2,1,0:T(8,128)(2,1)S(1)}, u32[]{:S(2)}, u32[]{:S(2)}) %collective-permute-start.4) | collective-permute-done | bytes 524320 | tf_op jit(solution)/shard_map/ppermute | solution.py:57
  89.5 1.3 spread_row.3
  90.8 6.6 %all-to-all-start.5 = ((bf16[8,32,512]{2,1,0:T(8,128)(2,1)}), bf16[8,32,512]{2,1,0:T(8,128)(2,1)S(1)}, u32[]{:S(2)}, u32[]{:S(2)}) async-start(bf16[8,32,512]{2,1,0:T(8,128)(2,1)} %spread_row.3), calls=%async_computation.5 | async-start | bytes 524288 | tf_op jit(solution)/shard_map/all_to_all | solution.py:48
  97.4 9.9 %into_window.3 = bf16[16,32,512]{2,1,0:T(8,128)(2,1)} custom-call(s32[52]{0:T(128)S(1)} %concatenate.14.scal_ref, bf16[16,32,512]{2,1,0:T(8,128)(2,1)S(1)} %bitcast.22, bf16[16,32,512]{2,1,0:T(8,128)(2,1)S(1)} %bitcast.28, bf16[43,512,512]{2,1,0:T(8,128)(2,1)} %panel_ref.7), custom_call_target="tpu_custom_call" | custom-call | flops 700000000 | bytes 25000000 | tf_op jit(solution)/shard_map/into_window/pallas_call | solution.py:186
  108.1 6.9 %all-to-all-start.6 = ((bf16[8,2,32,512]{3,2,1,0:T(8,128)(2,1)}), bf16[8,2,32,512]{3,2,1,0:T(8,128)(2,1)S(1)}, u32[]{:S(2)}, u32[]{:S(2)}) async-start(bf16[8,2,32,512]{3,2,1,0:T(8,128)(2,1)} %bitcast.15), calls=%async_computation.6 | async-start | bytes 1048576 | tf_op jit(solution)/shard_map/all_to_all | solution.py:48
  115.0 11.2 %into_rows_next.1 = (f32[8,2,32,512]{3,2,1,0:T(8,128)S(1)}, bf16[8,2,32,512]{3,2,1,0:T(8,128)(2,1)}) custom-call(s32[52]{0:T(128)S(1)} %concatenate.14.scal_ref, bf16[16,32,512]{2,1,0:T(8,128)(2,1)S(1)} %bitcast.23, bf16[16,32,512]{2,1,0:T(8,128)(2,1)S(1)} %bitcast.29, bf16[8,32,512]{2,1,0:T(8,128)(2,1)S(1)} %all-to-all-done.5.win_ref, ...), custom_call_target="tpu_custom_call" | custom-call | flops 700000000 | bytes 30000000 | tf_op jit(solution)/shard_map/into_rows_next/pallas_call | solution.py:401
  127.7 1.0 collective-permute-done.7.got_share_ref
  129.4 12.6 %all_to_all.42.parts_ref = bf16[8,2,32,512]{3,2,1,0:T(8,128)(2,1)S(1)} all-to-all(bf16[8,2,32,512]{3,2,1,0:T(8,128)(2,1)S(1)} %pair_sum.3), channel_id=1, replica_groups={{0,16,32,48,64,80,96,112},{8,24,40,56,72,88,104,120},{1,17,33,49,65,81,..., dimensions={0} | all-to-all | bytes 1048576 | tf_op jit(solution)/shard_map/all_to_all | solution.py:53
  (37 shorter events, 9.0 us)
Async XLA Ops:
  0.6 0.9 copy-start
  1.5 45.9 %copy-start.3 = (f32[16]{0:T(128)S(1)}, f32[16]{0:T(128)}, u32[]{:S(2)}) copy-start(f32[16]{0:T(128)} %refs_0_.1) | copy-start | bytes 196
  2.4 16.6 %all-to-all-start = ((bf16[8,2,32,512]{3,2,1,0:T(8,128)(2,1)}), bf16[8,2,32,512]{3,2,1,0:T(8,128)(2,1)S(1)}, u32[]{:S(2)}, u32[]{:S(2)}) async-start(bf16[8,2,32,512]{3,2,1,0:T(8,128)(2,1)} %spread_start.1), calls=%async_computation | async-start | bytes 1048576 | tf_op jit(solution)/shard_map/all_to_all | solution.py:53
  19.0 2.4 %collective-permute-start = (bf16[8,2,32,512]{3,2,1,0:T(8,128)(2,1)S(1)}, bf16[8,2,32,512]{3,2,1,0:T(8,128)(2,1)S(1)}, u32[]{:S(2)}, u32[]{:S(2)}) collective-permute-start(bf16[8,2,32,512]{3,2,1,0:T(8,128)(2,1)S(1)} %all-to-all-done), channel_id=1, source_target_pairs={{0,8},{8,0},{16,24},{24,16},{32,40},{40,32},{48,56},{56,48},{64,72... | collective-permute-start | bytes 1572872 | tf_op jit(solution)/shard_map/ppermute | solution.py:57
  22.7 17.0 %all-to-all-start.1 = ((bf16[8,32,512]{2,1,0:T(8,128)(2,1)}), bf16[8,32,512]{2,1,0:T(8,128)(2,1)S(1)}, u32[]{:S(2)}, u32[]{:S(2)}) async-start(bf16[8,32,512]{2,1,0:T(8,128)(2,1)} %spread_row.2), calls=%async_computation.1 | async-start | bytes 524288 | tf_op jit(solution)/shard_map/all_to_all | solution.py:48
  29.8 44.6 %copy-start.1 = (f32[32,1024]{1,0:T(8,128)S(1)}, f32[32,1024]{1,0:T(8,128)}, u32[]{:S(2)}) copy-start(f32[32,1024]{1,0:T(8,128)} %trace_ref.3) | copy-start | bytes 393220
  29.8 44.6 %copy-start.2 = (f32[32,1024]{1,0:T(8,128)S(1)}, f32[32,1024]{1,0:T(8,128)}, u32[]{:S(2)}) copy-start(f32[32,1024]{1,0:T(8,128)} %load_ref.3) | copy-start | bytes 393220
  39.8 7.7 %collective-permute-start.1 = (bf16[8,32,512]{2,1,0:T(8,128)(2,1)S(1)}, bf16[8,32,512]{2,1,0:T(8,128)(2,1)S(1)}, u32[]{:S(2)}, u32[]{:S(2)}) collective-permute-start(bf16[8,32,512]{2,1,0:T(8,128)(2,1)S(1)} %all-to-all-done.1.win_ref), channel_id=1, source_target_pairs={{0,8},{8,0},{16,24},{24,16},{32,40},{40,32},{48,56},{56,48},{64,72... | collective-permute-start | bytes 786440 | tf_op jit(solution)/shard_map/ppermute | solution.py:57
  40.5 18.7 %all-to-all-start.2 = ((bf16[8,2,32,512]{3,2,1,0:T(8,128)(2,1)}), bf16[8,2,32,512]{3,2,1,0:T(8,128)(2,1)S(1)}, u32[]{:S(2)}, u32[]{:S(2)}) async-start(bf16[8,2,32,512]{3,2,1,0:T(8,128)(2,1)} %bitcast.12), calls=%async_computation.2 | async-start | bytes 1048576 | tf_op jit(solution)/shard_map/all_to_all | solution.py:48
  58.6 2.5 %collective-permute-start.2 = (bf16[8,2,32,512]{3,2,1,0:T(8,128)(2,1)}, bf16[8,2,32,512]{3,2,1,0:T(8,128)(2,1)S(1)}, u32[]{:S(2)}, u32[]{:S(2)}) collective-permute-start(bf16[8,2,32,512]{3,2,1,0:T(8,128)(2,1)} %get-tuple-element.14), channel_id=1, source_target_pairs={{0,8},{8,0},{16,24},{24,16},{32,40},{40,32},{48,56},{56,48},{64,72... | collective-permute-start | bytes 1572872 | tf_op jit(solution)/shard_map/ppermute | solution.py:57
  59.3 1.8 %collective-permute-start.3 = (f32[2,32,512]{2,1,0:T(8,128)S(1)}, f32[2,32,512]{2,1,0:T(8,128)S(1)}, u32[]{:S(2)}, u32[]{:S(2)}) collective-permute-start(f32[2,32,512]{2,1,0:T(8,128)S(1)} %window_share.2.share_ref), channel_id=1, source_target_pairs={{0,8},{8,0},{16,24},{24,16},{32,40},{40,32},{48,56},{56,48},{64,72... | collective-permute-start | bytes 393224 | tf_op jit(solution)/shard_map/ppermute | solution.py:57
  86.1 3.4 %collective-permute-start.4 = (bf16[8,2,32,512]{3,2,1,0:T(8,128)(2,1)S(1)}, bf16[8,2,32,512]{3,2,1,0:T(8,128)(2,1)S(1)}, u32[]{:S(2)}, u32[]{:S(2)}) collective-permute-start(bf16[8,2,32,512]{3,2,1,0:T(8,128)(2,1)S(1)} %all_to_all.41), channel_id=1, source_target_pairs={{0,8},{8,0},{16,24},{24,16},{32,40},{40,32},{48,56},{56,48},{64,72... | collective-permute-start | bytes 1572872 | tf_op jit(solution)/shard_map/ppermute | solution.py:57
  90.8 16.5 %all-to-all-start.5 = ((bf16[8,32,512]{2,1,0:T(8,128)(2,1)}), bf16[8,32,512]{2,1,0:T(8,128)(2,1)S(1)}, u32[]{:S(2)}, u32[]{:S(2)}) async-start(bf16[8,32,512]{2,1,0:T(8,128)(2,1)} %spread_row.3), calls=%async_computation.5 | async-start | bytes 524288 | tf_op jit(solution)/shard_map/all_to_all | solution.py:48
  107.4 7.7 %collective-permute-start.5 = (bf16[8,32,512]{2,1,0:T(8,128)(2,1)S(1)}, bf16[8,32,512]{2,1,0:T(8,128)(2,1)S(1)}, u32[]{:S(2)}, u32[]{:S(2)}) collective-permute-start(bf16[8,32,512]{2,1,0:T(8,128)(2,1)S(1)} %all-to-all-done.5.win_ref), channel_id=1, source_target_pairs={{0,8},{8,0},{16,24},{24,16},{32,40},{40,32},{48,56},{56,48},{64,72... | collective-permute-start | bytes 786440 | tf_op jit(solution)/shard_map/ppermute | solution.py:57
  108.1 18.7 %all-to-all-start.6 = ((bf16[8,2,32,512]{3,2,1,0:T(8,128)(2,1)}), bf16[8,2,32,512]{3,2,1,0:T(8,128)(2,1)S(1)}, u32[]{:S(2)}, u32[]{:S(2)}) async-start(bf16[8,2,32,512]{3,2,1,0:T(8,128)(2,1)} %bitcast.15), calls=%async_computation.6 | async-start | bytes 1048576 | tf_op jit(solution)/shard_map/all_to_all | solution.py:48
  126.3 2.4 %collective-permute-start.6 = (bf16[8,2,32,512]{3,2,1,0:T(8,128)(2,1)}, bf16[8,2,32,512]{3,2,1,0:T(8,128)(2,1)S(1)}, u32[]{:S(2)}, u32[]{:S(2)}) collective-permute-start(bf16[8,2,32,512]{3,2,1,0:T(8,128)(2,1)} %get-tuple-element.20), channel_id=1, source_target_pairs={{0,8},{8,0},{16,24},{24,16},{32,40},{40,32},{48,56},{56,48},{64,72... | collective-permute-start | bytes 1572872 | tf_op jit(solution)/shard_map/ppermute | solution.py:57
  126.9 1.8 %collective-permute-start.7 = (f32[2,32,512]{2,1,0:T(8,128)S(1)}, f32[2,32,512]{2,1,0:T(8,128)S(1)}, u32[]{:S(2)}, u32[]{:S(2)}) collective-permute-start(f32[2,32,512]{2,1,0:T(8,128)S(1)} %window_share.3.share_ref), channel_id=1, source_target_pairs={{0,8},{8,0},{16,24},{24,16},{32,40},{40,32},{48,56},{56,48},{64,72... | collective-permute-start | bytes 393224 | tf_op jit(solution)/shard_map/ppermute | solution.py:57

commit v8 on v7

--- a/solution.py
+++ b/solution.py
@@ -24,7 +24,8 @@
 DENSE_COLS = 12
 LAYERS = 4
 SLOTS = 43
-GROUP = 6
+WINDOW_GROUPS = (6, 6, 6, 6, 6, 5, 4, 2, 2)
+ROW_GROUPS = (2, 3, 4, 6, 7, 7, 7, 7)
 UNROLL = 17
 COEFS = 16
 BAND_TILES = 32
@@ -72,9 +73,12 @@
         copy.wait()
 
 
-def start_body(trace_ref, out_ref, block_ref, sems):
+def start_body(trace_ref, out_ref, trace_vmem, block_ref, load_sem, sems):
+    load = pltpu.make_async_copy(trace_ref, trace_vmem, load_sem)
+    load.start()
+    load.wait()
     for half in range(2):
-        block_ref[half] = trace_ref[:, half * TILE : (half + 1) * TILE].astype(bf16)
+        block_ref[half] = trace_vmem[:, half * TILE : (half + 1) * TILE].astype(bf16)
     send_copies(block_ref, out_ref, sems)
 
 
@@ -82,12 +86,17 @@
     return pl.pallas_call(
         start_body,
         out_shape=pltpu.HBM((CHIPS, 2, RHS, TILE), bf16),
-        in_specs=[VMEM],
+        in_specs=[ANY],
         out_specs=ANY,
-        scratch_shapes=[pltpu.VMEM((2, RHS, TILE), bf16), pltpu.SemaphoreType.DMA((CHIPS,))],
+        scratch_shapes=[
+            pltpu.VMEM(trace_start.shape, f32),
+            pltpu.VMEM((2, RHS, TILE), bf16),
+            pltpu.SemaphoreType.DMA(()),
+            pltpu.SemaphoreType.DMA((CHIPS,)),
+        ],
         compiler_params=pltpu.CompilerParams(vmem_limit_bytes=6 * MIB),
         name="spread_start",
-    )(trace_start)
+    )(in_hbm(trace_start))
 
 
 def row_body(first_iteration, scal_ref, near_ref, far_ref, *refs):
@@ -126,7 +135,7 @@
         out_ref[(2 * block + 1 - core) * run + part] = far_ref[index]
 
 
-def for_slots(scal_ref, panel_ref, buffer_ref, sems, acc_ref, prepare, do_slot):
+def for_slots(groups, scal_ref, panel_ref, buffer_ref, sems, acc_ref, prepare, do_slot):
     def fetch(slot):
         return pltpu.make_async_copy(panel_ref.at[slot], buffer_ref.at[slot], sems.at[slot])
 
@@ -147,17 +156,13 @@
         shard = lax.shift_right_logical(row_tile, 4)
         do_slot(slot, named, shard, jnp.bitwise_and(row_tile, 1), col_tile)
 
-    def group(index, carry):
-        for extra in range(GROUP):
-            fetch(index * GROUP + extra).wait()
-        for extra in range(GROUP):
-            place(index * GROUP + extra)
-        return carry
-
-    lax.fori_loop(0, SLOTS // GROUP, group, 0)
-    for slot in range(SLOTS // GROUP * GROUP, SLOTS):
-        fetch(slot).wait()
-        place(slot)
+    begin = 0
+    for size in groups:
+        for slot in range(begin, begin + size):
+            fetch(slot).wait()
+        for slot in range(begin, begin + size):
+            place(slot)
+        begin += size
 
 
 def window_body(scal_ref, near_ref, far_ref, panel_ref, win_out, win_acc, buffer_ref, sems, traces_ref):
@@ -173,7 +178,7 @@
             )
 
         prepare = functools.partial(interleave, near_ref, far_ref, core, 2, traces_ref)
-        for_slots(scal_ref, panel_ref, buffer_ref, sems, win_acc, prepare, one_slot)
+        for_slots(WINDOW_GROUPS, scal_ref, panel_ref, buffer_ref, sems, win_acc, prepare, one_slot)
 
         win_out[...] = win_acc[:WIN_TILES].astype(bf16)
 
@@ -318,7 +323,7 @@
             )
 
         prepare = functools.partial(interleave, win_ref, mate_win_ref, core, 1, traces_ref)
-        for_slots(scal_ref, panel_ref, buffer_ref, panel_sems, band_acc, prepare, one_slot)
+        for_slots(ROW_GROUPS, scal_ref, panel_ref, buffer_ref, panel_sems, band_acc, prepare, one_slot)
 
     @pl.when(is_volume)
     def _():

time: 144 us -> 143 us (level)
  transfers between devices with their start and end apart: 13 -> 13, of which waited for: 7 -> 7; matrix products, arithmetic and copies ran while one was open for 3% -> 3% of each run, Pallas kernels for 30% -> 29%
where the time goes in v8:
time: 143 us; the launch traced here: 142 us
  Pallas kernels  47.9 us (33%)
  starting transfers between devices  40.1 us (28%)
  blocking collectives  36.9 us (26%)
  waiting for transfers between devices  10.5 us (7%)
  between operations  2.76 us (2%)
  other arithmetic  2.18 us (2%)
  local copies, waits for them, and re-layouts  1.61 us (1%)
    all_to_all x3, blocking collectives, between_chips(): return lax.all_to_all(x, 'col', 0, 0, axis_index_groups=groups, tiled=True)  36.9 us
    all_to_all x4, starting transfers between devices, exchange(): return lax.all_to_all(x, axis, 0, 0, tiled=True)  27 us
    pallas_call x2, Pallas kernels, into_rows(): pl.pallas_call(functools.partial(rows_body, first_iteration), out_shape=o...  21.7 us
    pallas_call x2, Pallas kernels, into_window(): pl.pallas_call(window_body, out_shape=jax.ShapeDtypeStruct((WIN_TILES, RH...  19.4 us
    ppermute x8, starting transfers between devices, from_mate(): return lax.ppermute(x, 'col', [(i, i ^ 1) for i in range(N_COL)])  6.77 us
    all_to_all x1, starting transfers between devices, between_chips(): return lax.all_to_all(x, 'col', 0, 0, axis_index_groups=groups, tiled=True)  6.39 us
    all_to_all x1, waiting for transfers between devices, between_chips(): return lax.all_to_all(x, 'col', 0, 0, axis_index_groups=groups, tiled=True)  5.21 us
    ppermute x8, waiting for transfers between devices, from_mate(): return lax.ppermute(x, 'col', [(i, i ^ 1) for i in range(N_COL)])  4.26 us
  transfers between devices with their start and end apart: 13, of which 7 were waited for; matrix products, arithmetic and copies ran while one was open for 3% of the time, Pallas kernels for 29%

profile of v8, /device:TPU:1, one launch (start us, length us, event | category | flops | bytes accessed | tf_op | source)
XLA Modules:
  0.0 142.0 jit_solution(17651560326228412090)
XLA Ops:
  0.6 1.8 %spread_start.1 = bf16[8,2,32,512]{3,2,1,0:T(8,128)(2,1)} custom-call(f32[32,1024]{1,0:T(8,128)} %trace_ref.3), custom_call_target="tpu_custom_call" | custom-call | tf_op jit(solution)/shard_map/spread_start/pallas_call | solution.py:86
  2.4 6.4 %all-to-all-start = ((bf16[8,2,32,512]{3,2,1,0:T(8,128)(2,1)}), bf16[8,2,32,512]{3,2,1,0:T(8,128)(2,1)S(1)}, u32[]{:S(2)}, u32[]{:S(2)}) async-start(bf16[8,2,32,512]{3,2,1,0:T(8,128)(2,1)} %spread_start.1), calls=%async_computation | async-start | bytes 1048576 | tf_op jit(solution)/shard_map/all_to_all | solution.py:54
  9.7 1.3 fusion.10
  13.0 0.9 fusion
  13.8 5.2 %all-to-all-done = bf16[8,2,32,512]{3,2,1,0:T(8,128)(2,1)S(1)} async-done(((bf16[8,2,32,512]{3,2,1,0:T(8,128)(2,1)}), bf16[8,2,32,512]{3,2,1,0:T(8,128)(2,1)S(1)}, u32[]{:S(2)}, u32[]{:S(2)}) %all-to-all-start) | async-done | bytes 524320 | tf_op jit(solution)/shard_map/all_to_all | solution.py:54
  19.0 0.8 collective-permute-start
  21.4 1.3 spread_row.2
  22.7 7.1 %all-to-all-start.1 = ((bf16[8,32,512]{2,1,0:T(8,128)(2,1)}), bf16[8,32,512]{2,1,0:T(8,128)(2,1)S(1)}, u32[]{:S(2)}, u32[]{:S(2)}) async-start(bf16[8,32,512]{2,1,0:T(8,128)(2,1)} %spread_row.2), calls=%async_computation.1 | async-start | bytes 524288 | tf_op jit(solution)/shard_map/all_to_all | solution.py:49
  29.8 9.7 %into_window.2 = bf16[16,32,512]{2,1,0:T(8,128)(2,1)} custom-call(s32[52]{0:T(128)S(1)} %concatenate.14.scal_ref, bf16[16,32,512]{2,1,0:T(8,128)(2,1)S(1)} %bitcast.19, bf16[16,32,512]{2,1,0:T(8,128)(2,1)S(1)} %bitcast.25, bf16[43,512,512]{2,1,0:T(8,128)(2,1)} %panel_ref.7), custom_call_target="tpu_custom_call" | custom-call | flops 700000000 | bytes 25000000 | tf_op jit(solution)/shard_map/into_window/pallas_call | solution.py:191
  40.3 6.9 %all-to-all-start.2 = ((bf16[8,2,32,512]{3,2,1,0:T(8,128)(2,1)}), bf16[8,2,32,512]{3,2,1,0:T(8,128)(2,1)S(1)}, u32[]{:S(2)}, u32[]{:S(2)}) async-start(bf16[8,2,32,512]{3,2,1,0:T(8,128)(2,1)} %bitcast.12), calls=%async_computation.2 | async-start | bytes 1048576 | tf_op jit(solution)/shard_map/all_to_all | solution.py:49
  47.2 10.9 %into_rows_first.1 = (f32[8,2,32,512]{3,2,1,0:T(8,128)S(1)}, bf16[8,2,32,512]{3,2,1,0:T(8,128)(2,1)}, f32[36,4,32,128]{3,2,1,0:T(8,128)}, f32[34,48,128]{2,1,0:T(8,128)}) custom-call(s32[52]{0:T(128)S(1)} %concatenate.14.scal_ref, bf16[16,32,512]{2,1,0:T(8,128)(2,1)S(1)} %bitcast.20, bf16[16,32,512]{2,1,0:T(8,128)(2,1)S(1)} %bitcast.26, ...), custom_call_target="tpu_custom_call" | custom-call | flops 700000000 | bytes 30000000 | tf_op jit(solution)/shard_map/into_rows_first/pallas_call | solution.py:406
  59.0 1.0 collective-permute-start.3
  60.0 1.0 collective-permute-done.3.got_share_ref
  61.7 12.6 %all_to_all.40.parts_ref = bf16[8,2,32,512]{3,2,1,0:T(8,128)(2,1)S(1)} all-to-all(bf16[8,2,32,512]{3,2,1,0:T(8,128)(2,1)S(1)} %pair_sum.2), channel_id=1, replica_groups={{0,16,32,48,64,80,96,112},{8,24,40,56,72,88,104,120},{1,17,33,49,65,81,..., dimensions={0} | all-to-all | bytes 1048576 | tf_op jit(solution)/shard_map/all_to_all | solution.py:54
  74.4 11.6 %all_to_all.41 = bf16[8,2,32,512]{3,2,1,0:T(8,128)(2,1)S(1)} all-to-all(bf16[8,2,32,512]{3,2,1,0:T(8,128)(2,1)S(1)} %get-tuple-element.15), channel_id=1, replica_groups={{0,16,32,48,64,80,96,112},{8,24,40,56,72,88,104,120},{1,17,33,49,65,81,..., dimensions={0} | all-to-all | bytes 1048576 | tf_op jit(solution)/shard_map/all_to_all | solution.py:54
  86.1 1.8 %collective-permute-start.4 = (bf16[8,2,32,512]{3,2,1,0:T(8,128)(2,1)S(1)}, bf16[8,2,32,512]{3,2,1,0:T(8,128)(2,1)S(1)}, u32[]{:S(2)}, u32[]{:S(2)}) collective-permute-start(bf16[8,2,32,512]{3,2,1,0:T(8,128)(2,1)S(1)} %all_to_all.41), channel_id=1, source_target_pairs={{0,8},{8,0},{16,24},{24,16},{32,40},{40,32},{48,56},{56,48},{64,72... | collective-permute-start | bytes 1572872 | tf_op jit(solution)/shard_map/ppermute | solution.py:58
  87.9 1.5 %collective-permute-done.4 = bf16[8,2,32,512]{3,2,1,0:T(8,128)(2,1)S(1)} collective-permute-done((bf16[8,2,32,512]{3,2,1,0:T(8,128)(2,1)S(1)}, bf16[8,2,32,512]{3,2,1,0:T(8,128)(2,1)S(1)}, u32[]{:S(2)}, u32[]{:S(2)}) %collective-permute-start.4) | collective-permute-done | bytes 524320 | tf_op jit(solution)/shard_map/ppermute | solution.py:58
  89.4 1.3 spread_row.3
  90.7 6.1 %all-to-all-start.5 = ((bf16[8,32,512]{2,1,0:T(8,128)(2,1)}), bf16[8,32,512]{2,1,0:T(8,128)(2,1)S(1)}, u32[]{:S(2)}, u32[]{:S(2)}) async-start(bf16[8,32,512]{2,1,0:T(8,128)(2,1)} %spread_row.3), calls=%async_computation.5 | async-start | bytes 524288 | tf_op jit(solution)/shard_map/all_to_all | solution.py:49
  96.8 9.7 %into_window.3 = bf16[16,32,512]{2,1,0:T(8,128)(2,1)} custom-call(s32[52]{0:T(128)S(1)} %concatenate.14.scal_ref, bf16[16,32,512]{2,1,0:T(8,128)(2,1)S(1)} %bitcast.22, bf16[16,32,512]{2,1,0:T(8,128)(2,1)S(1)} %bitcast.28, bf16[43,512,512]{2,1,0:T(8,128)(2,1)} %panel_ref.7), custom_call_target="tpu_custom_call" | custom-call | flops 700000000 | bytes 25000000 | tf_op jit(solution)/shard_map/into_window/pallas_call | solution.py:191
  107.3 6.9 %all-to-all-start.6 = ((bf16[8,2,32,512]{3,2,1,0:T(8,128)(2,1)}), bf16[8,2,32,512]{3,2,1,0:T(8,128)(2,1)S(1)}, u32[]{:S(2)}, u32[]{:S(2)}) async-start(bf16[8,2,32,512]{3,2,1,0:T(8,128)(2,1)} %bitcast.15), calls=%async_computation.6 | async-start | bytes 1048576 | tf_op jit(solution)/shard_map/all_to_all | solution.py:49
  114.2 10.9 %into_rows_next.1 = (f32[8,2,32,512]{3,2,1,0:T(8,128)S(1)}, bf16[8,2,32,512]{3,2,1,0:T(8,128)(2,1)}) custom-call(s32[52]{0:T(128)S(1)} %concatenate.14.scal_ref, bf16[16,32,512]{2,1,0:T(8,128)(2,1)S(1)} %bitcast.23, bf16[16,32,512]{2,1,0:T(8,128)(2,1)S(1)} %bitcast.29, bf16[8,32,512]{2,1,0:T(8,128)(2,1)S(1)} %all-to-all-done.5.win_ref, ...), custom_call_target="tpu_custom_call" | custom-call | flops 700000000 | bytes 30000000 | tf_op jit(solution)/shard_map/into_rows_next/pallas_call | solution.py:406
  126.9 1.0 collective-permute-done.7.got_share_ref
  128.5 12.6 %all_to_all.42.parts_ref = bf16[8,2,32,512]{3,2,1,0:T(8,128)(2,1)S(1)} all-to-all(bf16[8,2,32,512]{3,2,1,0:T(8,128)(2,1)S(1)} %pair_sum.3), channel_id=1, replica_groups={{0,16,32,48,64,80,96,112},{8,24,40,56,72,88,104,120},{1,17,33,49,65,81,..., dimensions={0} | all-to-all | bytes 1048576 | tf_op jit(solution)/shard_map/all_to_all | solution.py:54
  (35 shorter events, 8.8 us)
Async XLA Ops:
  0.6 46.6 %copy-start.2 = (f32[16]{0:T(128)S(1)}, f32[16]{0:T(128)}, u32[]{:S(2)}) copy-start(f32[16]{0:T(128)} %refs_0_.1) | copy-start | bytes 196
  2.4 16.6 %all-to-all-start = ((bf16[8,2,32,512]{3,2,1,0:T(8,128)(2,1)}), bf16[8,2,32,512]{3,2,1,0:T(8,128)(2,1)S(1)}, u32[]{:S(2)}, u32[]{:S(2)}) async-start(bf16[8,2,32,512]{3,2,1,0:T(8,128)(2,1)} %spread_start.1), calls=%async_computation | async-start | bytes 1048576 | tf_op jit(solution)/shard_map/all_to_all | solution.py:54
  19.0 2.4 %collective-permute-start = (bf16[8,2,32,512]{3,2,1,0:T(8,128)(2,1)S(1)}, bf16[8,2,32,512]{3,2,1,0:T(8,128)(2,1)S(1)}, u32[]{:S(2)}, u32[]{:S(2)}) collective-permute-start(bf16[8,2,32,512]{3,2,1,0:T(8,128)(2,1)S(1)} %all-to-all-done), channel_id=1, source_target_pairs={{0,8},{8,0},{16,24},{24,16},{32,40},{40,32},{48,56},{56,48},{64,72... | collective-permute-start | bytes 1572872 | tf_op jit(solution)/shard_map/ppermute | solution.py:58
  22.7 16.8 %all-to-all-start.1 = ((bf16[8,32,512]{2,1,0:T(8,128)(2,1)}), bf16[8,32,512]{2,1,0:T(8,128)(2,1)S(1)}, u32[]{:S(2)}, u32[]{:S(2)}) async-start(bf16[8,32,512]{2,1,0:T(8,128)(2,1)} %spread_row.2), calls=%async_computation.1 | async-start | bytes 524288 | tf_op jit(solution)/shard_map/all_to_all | solution.py:49
  29.8 44.5 %copy-start = (f32[32,1024]{1,0:T(8,128)S(1)}, f32[32,1024]{1,0:T(8,128)}, u32[]{:S(2)}) copy-start(f32[32,1024]{1,0:T(8,128)} %trace_ref.3) | copy-start | bytes 393220
  29.8 44.5 %copy-start.1 = (f32[32,1024]{1,0:T(8,128)S(1)}, f32[32,1024]{1,0:T(8,128)}, u32[]{:S(2)}) copy-start(f32[32,1024]{1,0:T(8,128)} %load_ref.3) | copy-start | bytes 393220
  39.5 7.7 %collective-permute-start.1 = (bf16[8,32,512]{2,1,0:T(8,128)(2,1)S(1)}, bf16[8,32,512]{2,1,0:T(8,128)(2,1)S(1)}, u32[]{:S(2)}, u32[]{:S(2)}) collective-permute-start(bf16[8,32,512]{2,1,0:T(8,128)(2,1)S(1)} %all-to-all-done.1.win_ref), channel_id=1, source_target_pairs={{0,8},{8,0},{16,24},{24,16},{32,40},{40,32},{48,56},{56,48},{64,72... | collective-permute-start | bytes 786440 | tf_op jit(solution)/shard_map/ppermute | solution.py:58
  40.3 18.7 %all-to-all-start.2 = ((bf16[8,2,32,512]{3,2,1,0:T(8,128)(2,1)}), bf16[8,2,32,512]{3,2,1,0:T(8,128)(2,1)S(1)}, u32[]{:S(2)}, u32[]{:S(2)}) async-start(bf16[8,2,32,512]{3,2,1,0:T(8,128)(2,1)} %bitcast.12), calls=%async_computation.2 | async-start | bytes 1048576 | tf_op jit(solution)/shard_map/all_to_all | solution.py:49
  58.1 3.0 %collective-permute-start.2 = (bf16[8,2,32,512]{3,2,1,0:T(8,128)(2,1)}, bf16[8,2,32,512]{3,2,1,0:T(8,128)(2,1)S(1)}, u32[]{:S(2)}, u32[]{:S(2)}) collective-permute-start(bf16[8,2,32,512]{3,2,1,0:T(8,128)(2,1)} %get-tuple-element.14), channel_id=1, source_target_pairs={{0,8},{8,0},{16,24},{24,16},{32,40},{40,32},{48,56},{56,48},{64,72... | collective-permute-start | bytes 1572872 | tf_op jit(solution)/shard_map/ppermute | solution.py:58
  59.0 2.0 %collective-permute-start.3 = (f32[2,32,512]{2,1,0:T(8,128)S(1)}, f32[2,32,512]{2,1,0:T(8,128)S(1)}, u32[]{:S(2)}, u32[]{:S(2)}) collective-permute-start(f32[2,32,512]{2,1,0:T(8,128)S(1)} %window_share.2.share_ref), channel_id=1, source_target_pairs={{0,8},{8,0},{16,24},{24,16},{32,40},{40,32},{48,56},{56,48},{64,72... | collective-permute-start | bytes 393224 | tf_op jit(solution)/shard_map/ppermute | solution.py:58
  86.1 3.4 %collective-permute-start.4 = (bf16[8,2,32,512]{3,2,1,0:T(8,128)(2,1)S(1)}, bf16[8,2,32,512]{3,2,1,0:T(8,128)(2,1)S(1)}, u32[]{:S(2)}, u32[]{:S(2)}) collective-permute-start(bf16[8,2,32,512]{3,2,1,0:T(8,128)(2,1)S(1)} %all_to_all.41), channel_id=1, source_target_pairs={{0,8},{8,0},{16,24},{24,16},{32,40},{40,32},{48,56},{56,48},{64,72... | collective-permute-start | bytes 1572872 | tf_op jit(solution)/shard_map/ppermute | solution.py:58
  90.7 15.8 %all-to-all-start.5 = ((bf16[8,32,512]{2,1,0:T(8,128)(2,1)}), bf16[8,32,512]{2,1,0:T(8,128)(2,1)S(1)}, u32[]{:S(2)}, u32[]{:S(2)}) async-start(bf16[8,32,512]{2,1,0:T(8,128)(2,1)} %spread_row.3), calls=%async_computation.5 | async-start | bytes 524288 | tf_op jit(solution)/shard_map/all_to_all | solution.py:49
  106.6 7.7 %collective-permute-start.5 = (bf16[8,32,512]{2,1,0:T(8,128)(2,1)S(1)}, bf16[8,32,512]{2,1,0:T(8,128)(2,1)S(1)}, u32[]{:S(2)}, u32[]{:S(2)}) collective-permute-start(bf16[8,32,512]{2,1,0:T(8,128)(2,1)S(1)} %all-to-all-done.5.win_ref), channel_id=1, source_target_pairs={{0,8},{8,0},{16,24},{24,16},{32,40},{40,32},{48,56},{56,48},{64,72... | collective-permute-start | bytes 786440 | tf_op jit(solution)/shard_map/ppermute | solution.py:58
  107.3 18.7 %all-to-all-start.6 = ((bf16[8,2,32,512]{3,2,1,0:T(8,128)(2,1)}), bf16[8,2,32,512]{3,2,1,0:T(8,128)(2,1)S(1)}, u32[]{:S(2)}, u32[]{:S(2)}) async-start(bf16[8,2,32,512]{3,2,1,0:T(8,128)(2,1)} %bitcast.15), calls=%async_computation.6 | async-start | bytes 1048576 | tf_op jit(solution)/shard_map/all_to_all | solution.py:49
  125.1 2.8 %collective-permute-start.6 = (bf16[8,2,32,512]{3,2,1,0:T(8,128)(2,1)}, bf16[8,2,32,512]{3,2,1,0:T(8,128)(2,1)S(1)}, u32[]{:S(2)}, u32[]{:S(2)}) collective-permute-start(bf16[8,2,32,512]{3,2,1,0:T(8,128)(2,1)} %get-tuple-element.20), channel_id=1, source_target_pairs={{0,8},{8,0},{16,24},{24,16},{32,40},{40,32},{48,56},{56,48},{64,72... | collective-permute-start | bytes 1572872 | tf_op jit(solution)/shard_map/ppermute | solution.py:58
  126.1 1.8 %collective-permute-start.7 = (f32[2,32,512]{2,1,0:T(8,128)S(1)}, f32[2,32,512]{2,1,0:T(8,128)S(1)}, u32[]{:S(2)}, u32[]{:S(2)}) collective-permute-start(f32[2,32,512]{2,1,0:T(8,128)S(1)} %window_share.3.share_ref), channel_id=1, source_target_pairs={{0,8},{8,0},{16,24},{24,16},{32,40},{40,32},{48,56},{56,48},{64,72... | collective-permute-start | bytes 393224 | tf_op jit(solution)/shard_map/ppermute | solution.py:58

commit v9 on v8

--- a/solution.py
+++ b/solution.py
@@ -165,7 +165,7 @@
         begin += size
 
 
-def window_body(scal_ref, near_ref, far_ref, panel_ref, win_out, win_acc, buffer_ref, sems, traces_ref):
+def window_body(scal_ref, near_ref, far_ref, panel_ref, win_out, win_acc, buffer_ref, sems, traces_ref, sum_ref, out_sems):
     is_volume = scal_ref[SLOTS] == 1
 
     @pl.when(jnp.logical_not(is_volume))
@@ -180,24 +180,34 @@
         prepare = functools.partial(interleave, near_ref, far_ref, core, 2, traces_ref)
         for_slots(WINDOW_GROUPS, scal_ref, panel_ref, buffer_ref, sems, win_acc, prepare, one_slot)
 
-        win_out[...] = win_acc[:WIN_TILES].astype(bf16)
 
     @pl.when(is_volume)
     def _():
-        win_out[...] = jnp.zeros_like(win_out)
+        win_acc[...] = jnp.zeros_like(win_acc)
+
+    def leave(peer):
+        return pltpu.make_async_copy(sum_ref.at[peer], win_out.at[peer], out_sems.at[peer])
+
+    for peer in range(N_ROW):
+        sum_ref[peer] = win_acc[2 * peer : 2 * peer + 2].astype(bf16)
+        leave(peer).start()
+    for peer in range(N_ROW):
+        leave(peer).wait()
 
 
 def into_window(scal, near, far, panel):
     return pl.pallas_call(
         window_body,
-        out_shape=jax.ShapeDtypeStruct((WIN_TILES, RHS, TILE), bf16),
+        out_shape=pltpu.HBM((N_ROW, 2, RHS, TILE), bf16),
         in_specs=[SMEM, VMEM, VMEM, ANY],
-        out_specs=VMEM,
+        out_specs=ANY,
         scratch_shapes=[
             pltpu.VMEM((WIN_TILES + 1, RHS, TILE), f32),
             pltpu.VMEM((SLOTS, TILE, TILE), bf16),
             pltpu.SemaphoreType.DMA((SLOTS,)),
             pltpu.VMEM((BAND_TILES, RHS, TILE), bf16),
+            pltpu.VMEM((N_ROW, 2, RHS, TILE), bf16),
+            pltpu.SemaphoreType.DMA((N_ROW,)),
         ],
         compiler_params=pltpu.CompilerParams(vmem_limit_bytes=44 * MIB),
         cost_estimate=pl.CostEstimate(flops=7 * 10**8, transcendentals=0, bytes_accessed=25 * 10**6),
@@ -546,7 +556,7 @@
         win_part = into_window(scal, near, far, panel)
         win, _ = lax.optimization_barrier((win, win_part))
         mate_win = from_mate(win)
-        parts = exchange(win_part.reshape(N_ROW, 2, RHS, TILE), "row")
+        parts = exchange(win_part, "row")
         own, mate, *saved = into_rows(
             scal, near, far, win, mate_win, panel, coef_table, coef_index, vol_source, saved
         )

time: 143 us -> 143 us (level)
  no operation moved by 1% of the time
where the time goes in v9:
time: 143 us; the launch traced here: 142 us
  Pallas kernels  47.9 us (33%)
  starting transfers between devices  40.1 us (28%)
  blocking collectives  36.9 us (26%)
  waiting for transfers between devices  10.5 us (7%)
  between operations  2.76 us (2%)
  other arithmetic  2.18 us (2%)
  local copies, waits for them, and re-layouts  1.61 us (1%)
    all_to_all x3, blocking collectives, between_chips(): return lax.all_to_all(x, 'col', 0, 0, axis_index_groups=groups, tiled=True)  36.9 us
    all_to_all x4, starting transfers between devices, exchange(): return lax.all_to_all(x, axis, 0, 0, tiled=True)  27 us
    pallas_call x2, Pallas kernels, into_rows(): pl.pallas_call(functools.partial(rows_body, first_iteration), out_shape=o...  21.7 us
    pallas_call x2, Pallas kernels, into_window(): pl.pallas_call(window_body, out_shape=pltpu.HBM((N_ROW, 2, RHS, TILE), bf...  19.5 us
    ppermute x8, starting transfers between devices, from_mate(): return lax.ppermute(x, 'col', [(i, i ^ 1) for i in range(N_COL)])  6.76 us
    all_to_all x1, starting transfers between devices, between_chips(): return lax.all_to_all(x, 'col', 0, 0, axis_index_groups=groups, tiled=True)  6.39 us
    all_to_all x1, waiting for transfers between devices, between_chips(): return lax.all_to_all(x, 'col', 0, 0, axis_index_groups=groups, tiled=True)  5.21 us
    ppermute x8, waiting for transfers between devices, from_mate(): return lax.ppermute(x, 'col', [(i, i ^ 1) for i in range(N_COL)])  4.26 us
  transfers between devices with their start and end apart: 13, of which 7 were waited for; matrix products, arithmetic and copies ran while one was open for 3% of the time, Pallas kernels for 29%

profile of v9, /device:TPU:1, one launch (start us, length us, event | category | flops | bytes accessed | tf_op | source)
XLA Modules:
  0.0 142.0 jit_solution(13612090609043730335)
XLA Ops:
  0.6 1.8 %spread_start.1 = bf16[8,2,32,512]{3,2,1,0:T(8,128)(2,1)} custom-call(f32[32,1024]{1,0:T(8,128)} %trace_ref.3), custom_call_target="tpu_custom_call" | custom-call | tf_op jit(solution)/shard_map/spread_start/pallas_call | solution.py:86
  2.4 6.4 %all-to-all-start = ((bf16[8,2,32,512]{3,2,1,0:T(8,128)(2,1)}), bf16[8,2,32,512]{3,2,1,0:T(8,128)(2,1)S(1)}, u32[]{:S(2)}, u32[]{:S(2)}) async-start(bf16[8,2,32,512]{3,2,1,0:T(8,128)(2,1)} %spread_start.1), calls=%async_computation | async-start | bytes 1048576 | tf_op jit(solution)/shard_map/all_to_all | solution.py:54
  9.7 1.3 fusion.10
  13.0 0.9 fusion
  13.8 5.2 %all-to-all-done = bf16[8,2,32,512]{3,2,1,0:T(8,128)(2,1)S(1)} async-done(((bf16[8,2,32,512]{3,2,1,0:T(8,128)(2,1)}), bf16[8,2,32,512]{3,2,1,0:T(8,128)(2,1)S(1)}, u32[]{:S(2)}, u32[]{:S(2)}) %all-to-all-start) | async-done | bytes 524320 | tf_op jit(solution)/shard_map/all_to_all | solution.py:54
  19.0 0.8 collective-permute-start
  21.4 1.3 spread_row.2
  22.7 7.1 %all-to-all-start.1 = ((bf16[8,32,512]{2,1,0:T(8,128)(2,1)}), bf16[8,32,512]{2,1,0:T(8,128)(2,1)S(1)}, u32[]{:S(2)}, u32[]{:S(2)}) async-start(bf16[8,32,512]{2,1,0:T(8,128)(2,1)} %spread_row.2), calls=%async_computation.1 | async-start | bytes 524288 | tf_op jit(solution)/shard_map/all_to_all | solution.py:49
  29.8 9.7 %into_window.2 = bf16[8,2,32,512]{3,2,1,0:T(8,128)(2,1)} custom-call(s32[52]{0:T(128)S(1)} %concatenate.14.scal_ref, bf16[16,32,512]{2,1,0:T(8,128)(2,1)S(1)} %bitcast.17, bf16[16,32,512]{2,1,0:T(8,128)(2,1)S(1)} %bitcast.23, bf16[43,512,512]{2,1,0:T(8,128)(2,1)} %panel_ref.7), custom_call_target="tpu_custom_call" | custom-call | flops 700000000 | bytes 25000000 | tf_op jit(solution)/shard_map/into_window/pallas_call | solution.py:199
  40.3 6.9 %all-to-all-start.2 = ((bf16[8,2,32,512]{3,2,1,0:T(8,128)(2,1)}), bf16[8,2,32,512]{3,2,1,0:T(8,128)(2,1)S(1)}, u32[]{:S(2)}, u32[]{:S(2)}) async-start(bf16[8,2,32,512]{3,2,1,0:T(8,128)(2,1)} %into_window.2), calls=%async_computation.2 | async-start | bytes 1048576 | tf_op jit(solution)/shard_map/all_to_all | solution.py:49
  47.2 10.9 %into_rows_first.1 = (f32[8,2,32,512]{3,2,1,0:T(8,128)S(1)}, bf16[8,2,32,512]{3,2,1,0:T(8,128)(2,1)}, f32[36,4,32,128]{3,2,1,0:T(8,128)}, f32[34,48,128]{2,1,0:T(8,128)}) custom-call(s32[52]{0:T(128)S(1)} %concatenate.14.scal_ref, bf16[16,32,512]{2,1,0:T(8,128)(2,1)S(1)} %bitcast.18, bf16[16,32,512]{2,1,0:T(8,128)(2,1)S(1)} %bitcast.24, ...), custom_call_target="tpu_custom_call" | custom-call | flops 700000000 | bytes 30000000 | tf_op jit(solution)/shard_map/into_rows_first/pallas_call | solution.py:416
  59.1 1.0 collective-permute-start.3
  60.1 1.0 collective-permute-done.3.got_share_ref
  61.7 12.6 %all_to_all.40.parts_ref = bf16[8,2,32,512]{3,2,1,0:T(8,128)(2,1)S(1)} all-to-all(bf16[8,2,32,512]{3,2,1,0:T(8,128)(2,1)S(1)} %pair_sum.2), channel_id=1, replica_groups={{0,16,32,48,64,80,96,112},{8,24,40,56,72,88,104,120},{1,17,33,49,65,81,..., dimensions={0} | all-to-all | bytes 1048576 | tf_op jit(solution)/shard_map/all_to_all | solution.py:54
  74.5 11.6 %all_to_all.41 = bf16[8,2,32,512]{3,2,1,0:T(8,128)(2,1)S(1)} all-to-all(bf16[8,2,32,512]{3,2,1,0:T(8,128)(2,1)S(1)} %get-tuple-element.15), channel_id=1, replica_groups={{0,16,32,48,64,80,96,112},{8,24,40,56,72,88,104,120},{1,17,33,49,65,81,..., dimensions={0} | all-to-all | bytes 1048576 | tf_op jit(solution)/shard_map/all_to_all | solution.py:54
  86.1 1.8 %collective-permute-start.4 = (bf16[8,2,32,512]{3,2,1,0:T(8,128)(2,1)S(1)}, bf16[8,2,32,512]{3,2,1,0:T(8,128)(2,1)S(1)}, u32[]{:S(2)}, u32[]{:S(2)}) collective-permute-start(bf16[8,2,32,512]{3,2,1,0:T(8,128)(2,1)S(1)} %all_to_all.41), channel_id=1, source_target_pairs={{0,8},{8,0},{16,24},{24,16},{32,40},{40,32},{48,56},{56,48},{64,72... | collective-permute-start | bytes 1572872 | tf_op jit(solution)/shard_map/ppermute | solution.py:58
  87.9 1.5 %collective-permute-done.4 = bf16[8,2,32,512]{3,2,1,0:T(8,128)(2,1)S(1)} collective-permute-done((bf16[8,2,32,512]{3,2,1,0:T(8,128)(2,1)S(1)}, bf16[8,2,32,512]{3,2,1,0:T(8,128)(2,1)S(1)}, u32[]{:S(2)}, u32[]{:S(2)}) %collective-permute-start.4) | collective-permute-done | bytes 524320 | tf_op jit(solution)/shard_map/ppermute | solution.py:58
  89.5 1.3 spread_row.3
  90.8 6.1 %all-to-all-start.5 = ((bf16[8,32,512]{2,1,0:T(8,128)(2,1)}), bf16[8,32,512]{2,1,0:T(8,128)(2,1)S(1)}, u32[]{:S(2)}, u32[]{:S(2)}) async-start(bf16[8,32,512]{2,1,0:T(8,128)(2,1)} %spread_row.3), calls=%async_computation.5 | async-start | bytes 524288 | tf_op jit(solution)/shard_map/all_to_all | solution.py:49
  96.9 9.7 %into_window.3 = bf16[8,2,32,512]{3,2,1,0:T(8,128)(2,1)} custom-call(s32[52]{0:T(128)S(1)} %concatenate.14.scal_ref, bf16[16,32,512]{2,1,0:T(8,128)(2,1)S(1)} %bitcast.20, bf16[16,32,512]{2,1,0:T(8,128)(2,1)S(1)} %bitcast.26, bf16[43,512,512]{2,1,0:T(8,128)(2,1)} %panel_ref.7), custom_call_target="tpu_custom_call" | custom-call | flops 700000000 | bytes 25000000 | tf_op jit(solution)/shard_map/into_window/pallas_call | solution.py:199
  107.3 6.9 %all-to-all-start.6 = ((bf16[8,2,32,512]{3,2,1,0:T(8,128)(2,1)}), bf16[8,2,32,512]{3,2,1,0:T(8,128)(2,1)S(1)}, u32[]{:S(2)}, u32[]{:S(2)}) async-start(bf16[8,2,32,512]{3,2,1,0:T(8,128)(2,1)} %into_window.3), calls=%async_computation.6 | async-start | bytes 1048576 | tf_op jit(solution)/shard_map/all_to_all | solution.py:49
  114.3 10.9 %into_rows_next.1 = (f32[8,2,32,512]{3,2,1,0:T(8,128)S(1)}, bf16[8,2,32,512]{3,2,1,0:T(8,128)(2,1)}) custom-call(s32[52]{0:T(128)S(1)} %concatenate.14.scal_ref, bf16[16,32,512]{2,1,0:T(8,128)(2,1)S(1)} %bitcast.21, bf16[16,32,512]{2,1,0:T(8,128)(2,1)S(1)} %bitcast.27, bf16[8,32,512]{2,1,0:T(8,128)(2,1)S(1)} %all-to-all-done.5.win_ref, ...), custom_call_target="tpu_custom_call" | custom-call | flops 700000000 | bytes 30000000 | tf_op jit(solution)/shard_map/into_rows_next/pallas_call | solution.py:416
  127.0 1.0 collective-permute-done.7.got_share_ref
  128.6 12.6 %all_to_all.42.parts_ref = bf16[8,2,32,512]{3,2,1,0:T(8,128)(2,1)S(1)} all-to-all(bf16[8,2,32,512]{3,2,1,0:T(8,128)(2,1)S(1)} %pair_sum.3), channel_id=1, replica_groups={{0,16,32,48,64,80,96,112},{8,24,40,56,72,88,104,120},{1,17,33,49,65,81,..., dimensions={0} | all-to-all | bytes 1048576 | tf_op jit(solution)/shard_map/all_to_all | solution.py:54
  (35 shorter events, 8.8 us)
Async XLA Ops:
  0.6 46.6 %copy-start.2 = (f32[16]{0:T(128)S(1)}, f32[16]{0:T(128)}, u32[]{:S(2)}) copy-start(f32[16]{0:T(128)} %refs_0_.1) | copy-start | bytes 196
  2.4 16.6 %all-to-all-start = ((bf16[8,2,32,512]{3,2,1,0:T(8,128)(2,1)}), bf16[8,2,32,512]{3,2,1,0:T(8,128)(2,1)S(1)}, u32[]{:S(2)}, u32[]{:S(2)}) async-start(bf16[8,2,32,512]{3,2,1,0:T(8,128)(2,1)} %spread_start.1), calls=%async_computation | async-start | bytes 1048576 | tf_op jit(solution)/shard_map/all_to_all | solution.py:54
  19.0 2.4 %collective-permute-start = (bf16[8,2,32,512]{3,2,1,0:T(8,128)(2,1)S(1)}, bf16[8,2,32,512]{3,2,1,0:T(8,128)(2,1)S(1)}, u32[]{:S(2)}, u32[]{:S(2)}) collective-permute-start(bf16[8,2,32,512]{3,2,1,0:T(8,128)(2,1)S(1)} %all-to-all-done), channel_id=1, source_target_pairs={{0,8},{8,0},{16,24},{24,16},{32,40},{40,32},{48,56},{56,48},{64,72... | collective-permute-start | bytes 1572872 | tf_op jit(solution)/shard_map/ppermute | solution.py:58
  22.7 16.8 %all-to-all-start.1 = ((bf16[8,32,512]{2,1,0:T(8,128)(2,1)}), bf16[8,32,512]{2,1,0:T(8,128)(2,1)S(1)}, u32[]{:S(2)}, u32[]{:S(2)}) async-start(bf16[8,32,512]{2,1,0:T(8,128)(2,1)} %spread_row.2), calls=%async_computation.1 | async-start | bytes 524288 | tf_op jit(solution)/shard_map/all_to_all | solution.py:49
  29.8 44.6 %copy-start = (f32[32,1024]{1,0:T(8,128)S(1)}, f32[32,1024]{1,0:T(8,128)}, u32[]{:S(2)}) copy-start(f32[32,1024]{1,0:T(8,128)} %trace_ref.3) | copy-start | bytes 393220
  29.8 44.6 %copy-start.1 = (f32[32,1024]{1,0:T(8,128)S(1)}, f32[32,1024]{1,0:T(8,128)}, u32[]{:S(2)}) copy-start(f32[32,1024]{1,0:T(8,128)} %load_ref.3) | copy-start | bytes 393220
  39.6 7.6 %collective-permute-start.1 = (bf16[8,32,512]{2,1,0:T(8,128)(2,1)S(1)}, bf16[8,32,512]{2,1,0:T(8,128)(2,1)S(1)}, u32[]{:S(2)}, u32[]{:S(2)}) collective-permute-start(bf16[8,32,512]{2,1,0:T(8,128)(2,1)S(1)} %all-to-all-done.1.win_ref), channel_id=1, source_target_pairs={{0,8},{8,0},{16,24},{24,16},{32,40},{40,32},{48,56},{56,48},{64,72... | collective-permute-start | bytes 786440 | tf_op jit(solution)/shard_map/ppermute | solution.py:58
  40.3 18.7 %all-to-all-start.2 = ((bf16[8,2,32,512]{3,2,1,0:T(8,128)(2,1)}), bf16[8,2,32,512]{3,2,1,0:T(8,128)(2,1)S(1)}, u32[]{:S(2)}, u32[]{:S(2)}) async-start(bf16[8,2,32,512]{3,2,1,0:T(8,128)(2,1)} %into_window.2), calls=%async_computation.2 | async-start | bytes 1048576 | tf_op jit(solution)/shard_map/all_to_all | solution.py:49
  58.1 3.0 %collective-permute-start.2 = (bf16[8,2,32,512]{3,2,1,0:T(8,128)(2,1)}, bf16[8,2,32,512]{3,2,1,0:T(8,128)(2,1)S(1)}, u32[]{:S(2)}, u32[]{:S(2)}) collective-permute-start(bf16[8,2,32,512]{3,2,1,0:T(8,128)(2,1)} %get-tuple-element.14), channel_id=1, source_target_pairs={{0,8},{8,0},{16,24},{24,16},{32,40},{40,32},{48,56},{56,48},{64,72... | collective-permute-start | bytes 1572872 | tf_op jit(solution)/shard_map/ppermute | solution.py:58
  59.1 2.0 %collective-permute-start.3 = (f32[2,32,512]{2,1,0:T(8,128)S(1)}, f32[2,32,512]{2,1,0:T(8,128)S(1)}, u32[]{:S(2)}, u32[]{:S(2)}) collective-permute-start(f32[2,32,512]{2,1,0:T(8,128)S(1)} %window_share.2.share_ref), channel_id=1, source_target_pairs={{0,8},{8,0},{16,24},{24,16},{32,40},{40,32},{48,56},{56,48},{64,72... | collective-permute-start | bytes 393224 | tf_op jit(solution)/shard_map/ppermute | solution.py:58
  86.1 3.4 %collective-permute-start.4 = (bf16[8,2,32,512]{3,2,1,0:T(8,128)(2,1)S(1)}, bf16[8,2,32,512]{3,2,1,0:T(8,128)(2,1)S(1)}, u32[]{:S(2)}, u32[]{:S(2)}) collective-permute-start(bf16[8,2,32,512]{3,2,1,0:T(8,128)(2,1)S(1)} %all_to_all.41), channel_id=1, source_target_pairs={{0,8},{8,0},{16,24},{24,16},{32,40},{40,32},{48,56},{56,48},{64,72... | collective-permute-start | bytes 1572872 | tf_op jit(solution)/shard_map/ppermute | solution.py:58
  90.8 15.8 %all-to-all-start.5 = ((bf16[8,32,512]{2,1,0:T(8,128)(2,1)}), bf16[8,32,512]{2,1,0:T(8,128)(2,1)S(1)}, u32[]{:S(2)}, u32[]{:S(2)}) async-start(bf16[8,32,512]{2,1,0:T(8,128)(2,1)} %spread_row.3), calls=%async_computation.5 | async-start | bytes 524288 | tf_op jit(solution)/shard_map/all_to_all | solution.py:49
  106.6 7.7 %collective-permute-start.5 = (bf16[8,32,512]{2,1,0:T(8,128)(2,1)S(1)}, bf16[8,32,512]{2,1,0:T(8,128)(2,1)S(1)}, u32[]{:S(2)}, u32[]{:S(2)}) collective-permute-start(bf16[8,32,512]{2,1,0:T(8,128)(2,1)S(1)} %all-to-all-done.5.win_ref), channel_id=1, source_target_pairs={{0,8},{8,0},{16,24},{24,16},{32,40},{40,32},{48,56},{56,48},{64,72... | collective-permute-start | bytes 786440 | tf_op jit(solution)/shard_map/ppermute | solution.py:58
  107.3 18.7 %all-to-all-start.6 = ((bf16[8,2,32,512]{3,2,1,0:T(8,128)(2,1)}), bf16[8,2,32,512]{3,2,1,0:T(8,128)(2,1)S(1)}, u32[]{:S(2)}, u32[]{:S(2)}) async-start(bf16[8,2,32,512]{3,2,1,0:T(8,128)(2,1)} %into_window.3), calls=%async_computation.6 | async-start | bytes 1048576 | tf_op jit(solution)/shard_map/all_to_all | solution.py:49
  125.1 2.8 %collective-permute-start.6 = (bf16[8,2,32,512]{3,2,1,0:T(8,128)(2,1)}, bf16[8,2,32,512]{3,2,1,0:T(8,128)(2,1)S(1)}, u32[]{:S(2)}, u32[]{:S(2)}) collective-permute-start(bf16[8,2,32,512]{3,2,1,0:T(8,128)(2,1)} %get-tuple-element.20), channel_id=1, source_target_pairs={{0,8},{8,0},{16,24},{24,16},{32,40},{40,32},{48,56},{56,48},{64,72... | collective-permute-start | bytes 1572872 | tf_op jit(solution)/shard_map/ppermute | solution.py:58
  126.1 1.8 %collective-permute-start.7 = (f32[2,32,512]{2,1,0:T(8,128)S(1)}, f32[2,32,512]{2,1,0:T(8,128)S(1)}, u32[]{:S(2)}, u32[]{:S(2)}) collective-permute-start(f32[2,32,512]{2,1,0:T(8,128)S(1)} %window_share.3.share_ref), channel_id=1, source_target_pairs={{0,8},{8,0},{16,24},{24,16},{32,40},{40,32},{48,56},{56,48},{64,72... | collective-permute-start | bytes 393224 | tf_op jit(solution)/shard_map/ppermute | solution.py:58
